TPU v7x, 32 devices: a whole 2x2x4 slice. The times are simulated.
32 devices in a mesh: dp: 4 (over y, x), ctx: 8 (over z, core).
Axes of the slice: x: 2, y: 2, z: 4, core: 2. Of those that a mesh axis runs over, the one named last changes fastest.
Arguments:
- stream: bfloat16 [16, 4096, 1600], P('dp', 'ctx'), may hold values from -16 to 16
- segments: int32 [16, 4096], P('dp'), may hold values from 0 to 3, never falling along the last dimension, each value on 1 to 2000 neighbouring positions
- cotangent: bfloat16 [16, 4096, 1600], P('dp', 'ctx'), may hold values from -6 to 6
- gain_zero: bfloat16 [1600], P('dp'), may hold values from 0.099609375 to 1.8984375
- shift_zero: bfloat16 [1600], P('dp'), may hold values from -2.390625 to 2.390625
- weight_in: bfloat16 [1600, 800], P('dp'), may hold values from -0.21875 to 0.21875
- bias_in: bfloat16 [800], P('dp'), may hold values from -3 to 3
- gain_one: bfloat16 [800], P('dp'), may hold values from 0.099609375 to 1.8984375
- shift_one: bfloat16 [800], P('dp'), may hold values from -2.390625 to 2.390625
- weight_conv: bfloat16 [3, 800, 800], P(None, 'dp'), may hold values from -0.15625 to 0.15625
- bias_conv: bfloat16 [800], P('dp'), may hold values from -3 to 3
- gain_two: bfloat16 [800], P('dp'), may hold values from 0.099609375 to 1.8984375
- shift_two: bfloat16 [800], P('dp'), may hold values from -2.390625 to 2.390625
- weight_out: bfloat16 [800, 1600], P('dp'), may hold values from -0.3125 to 0.3125
- bias_out: bfloat16 [1600], P('dp'), may hold values from -3 to 3
Outputs:
- output: bfloat16 [16, 4096, 1600], P('dp', 'ctx')
- grad_stream: bfloat16 [16, 4096, 1600], P('dp', 'ctx')
- grad_gain_zero: float32 [1600], P('dp')
- grad_shift_zero: float32 [1600], P('dp')
- grad_weight_in: float32 [1600, 800], P('dp')
- grad_bias_in: float32 [800], P('dp')
- grad_gain_one: float32 [800], P('dp')
- grad_shift_one: float32 [800], P('dp')
- grad_weight_conv: float32 [3, 800, 800], P(None, 'dp')
- grad_bias_conv: float32 [800], P('dp')
- grad_gain_two: float32 [800], P('dp')
- grad_shift_two: float32 [800], P('dp')
- grad_weight_out: float32 [800, 1600], P('dp')
- grad_bias_out: float32 [1600], P('dp')
- rms_in: float32 [], replicated
- rms_out: float32 [], replicated
- rms_hidden_one: float32 [], replicated
- rms_hidden_two: float32 [], replicated
- rms_branch: float32 [], replicated
All inputs are finite; a program needn't handle non-finite values.
Results may differ from a plain program's by a relative error of at most 0.0066.
Values may be sent and summed in bfloat16 or wider, within the bound.
No kernel may reach another device: no remote copies, remote signals or barrier semaphores. Data moves between devices by JAX's collectives and lax.ppermute only.
A program may use at most 256 MiB of HBM per device.

v0:
```python
import functools

import jax
import jax.numpy as jnp
from jax import lax
from jax.experimental import pallas as pl
from jax.experimental.pallas import tpu as pltpu
from jax.sharding import PartitionSpec as P

F32 = jnp.float32
BF = jnp.bfloat16
EPS = 1e-05
ROWS = 16
NN = (((1,), (0,)), ((), ()))
NT = (((1,), (1,)), ((), ()))
MIB = 1024 * 1024


def by_core(value, even_mask, odd_mask):
    n_dp, n_ctx = lax.axis_size("dp"), lax.axis_size("ctx")
    masks = (even_mask, odd_mask)
    pairs = [
        (d * n_ctx + t, (d ^ masks[t % 2]) * n_ctx + t) for d in range(n_dp) for t in range(n_ctx)
    ]
    return lax.ppermute(value, ("dp", "ctx"), pairs)


def swap(value, axis, mask):
    return lax.ppermute(value, axis, [(i, i ^ mask) for i in range(lax.axis_size(axis))])


def shifted(value, by):
    size = lax.axis_size("ctx")
    return lax.ppermute(value, "ctx", [(i, i + by) for i in range(size) if 0 <= i + by < size])


def half_of(rows):
    off = rows // 2 // 16 * 16
    return off, rows - off


def gated(value, gate):
    return value if gate is None else lax.optimization_barrier((value, gate))[0]


def after(value, *others):
    return lax.optimization_barrier((value, *others))[0]


def gather_halves(half):
    first = by_core(half, 1, 2)
    gate = yield half
    sent = jnp.stack([half, gated(first, gate)])
    second = by_core(sent, 2, 1)
    gate = yield sent
    second = gated(second, gate)
    other_first = swap(first, "ctx", 1)
    other_second = swap(second, "ctx", 1)
    yield second
    yield first, second, other_first, other_second


def halved(value, bit):
    rows = value.shape[1]
    off, size = parts_of(rows)
    keep = lax.dynamic_slice_in_dim(value, bit * off, size, 1)
    return keep, lax.dynamic_slice_in_dim(value, (1 - bit) * off, size, 1)


def parts_of(rows):
    off = rows // 2 // 8 * 8
    return off, rows - off


def joined(mine, other, bit, rows):
    off, size = parts_of(rows)
    low = jnp.where(bit == 0, mine, other)
    high = jnp.where(bit == 0, other, mine)
    return jnp.concatenate([low, high[:, size - off :]], axis=1)


def sum_shards(keep, send, halving):
    got = swap(send, "ctx", 1)
    gate = yield send
    got = gated(got, gate)
    sent = (keep[2:4].astype(F32) + got[2:4].astype(F32)).astype(BF)
    one = by_core(sent, 1, 2)
    gate = yield sent
    one = gated(one, gate)
    sent = (keep[1].astype(F32) + got[1].astype(F32) + one[1].astype(F32)).astype(BF)
    two = by_core(sent, 2, 1)
    gate = yield sent
    two = gated(two, gate)
    part = keep[0].astype(F32) + got[0].astype(F32) + one[0].astype(F32) + two.astype(F32)
    place = lax.axis_index("ctx")
    masks = [1 << b for b in range(1, (lax.axis_size("ctx") - 1).bit_length())]
    split = [(mask, (place // mask) % 2) for mask in masks[: 2 if halving else 0]]
    sizes = []
    for mask, bit in split:
        sizes.append(part.shape[1])
        part, sent = halved(part, bit)
        sent = sent.astype(BF)
        came = swap(sent, "ctx", mask)
        gate = yield sent
        part = part + gated(came, gate).astype(F32)
    for mask in masks[len(split) :]:
        sent = part.astype(BF)
        came = swap(sent, "ctx", mask)
        gate = yield sent
        part = sent.astype(F32) + gated(came, gate).astype(F32)
    for mask, bit in split[::-1]:
        sent = part.astype(BF)
        came = swap(sent, "ctx", mask)
        gate = yield sent
        part = joined(sent, gated(came, gate), bit, sizes.pop())
    other = swap(part, "ctx", 1)
    gate = yield part
    yield part, gated(other, gate)


def sum_all(value):
    got = swap(value, "ctx", 1)
    gate = yield value
    value = value + gated(got, gate)
    groups = [("dp", (1, 2, 3)), ("ctx", (2, 4, 6))]
    mask = 8
    while mask < lax.axis_size("ctx"):
        groups.append(("ctx", (mask,)))
        mask *= 2
    for axis, masks in groups:
        got = [value] + [swap(value, axis, m) for m in masks]
        gate = yield value
        if len(got) == 4:
            a, b = got[0] + got[1], got[2] + got[3]
            value = gated(a, gate) + b
        else:
            value = gated(got[0], gate) + got[1]
    yield value


class Stages:
    def __init__(self, stages):
        self.stages, self.value, self.left = stages, next(stages), True

    def step(self, gate):
        try:
            self.value = self.stages.send(gate)
        except StopIteration:
            self.left = False
        return self.value

    def result(self):
        while self.left:
            self.step(None)
        return self.value


def join_halves(mine, other, rows, row_dim, core):
    off, size = half_of(rows)
    low = jnp.where(core == 0, mine, other)
    high = jnp.where(core == 0, other, mine)
    return jnp.concatenate(
        [low, lax.slice_in_dim(high, size - off, size, axis=row_dim)], axis=row_dim
    )


def mm(left, right, dims=NN):
    return lax.dot_general(left, right, dims, preferred_element_type=F32)


def silu_of_half(y):
    return y * (1.0 + jnp.tanh(y))


def loop(count, body, unroll):
    lax.fori_loop(0, count, lambda i, _: (body(i), 0)[1], 0, unroll=unroll)


def full(shape):
    return pl.BlockSpec(shape, lambda s: (0,) * len(shape), pipeline_mode=pl.Buffered(1))


def seq(shape):
    return pl.BlockSpec((None,) + shape, lambda s: (s,) + (0,) * len(shape))


ANY = pl.BlockSpec(memory_space=pl.ANY)


def sds(shape, dtype):
    return jax.ShapeDtypeStruct(shape, dtype)


def rows_at(i, base=0):
    return pl.ds(pl.multiple_of(i * ROWS + base, ROWS), ROWS)


def lanes(tile, width):
    return jnp.concatenate([tile] * (width // 128), axis=1)


def col(ref, j, r, width):
    return lanes(ref[j, r, :], width)


def fold(v):
    t = v[:, 0:128]
    for j in range(1, v.shape[1] // 128):
        t = t + v[:, j * 128 : (j + 1) * 128]
    return t


def eight(v):
    return v[0:8] + v[8:16]


def spread(packs, out_ref, j, row, scale=1.0):
    own, near, far = packs
    me, core = lax.axis_index("dp"), lax.rem(lax.axis_index("ctx"), 2)
    part = out_ref.shape[1] // 4
    for mask, ref in ((0, own), (1 + core, near), (2 - core, far.at[0]), (3, far.at[1])):
        start = pl.multiple_of(jnp.bitwise_xor(me, mask) * part, 8)
        v = ref[...].astype(F32)[row : row + 1, 0:part] * scale
        out_ref[j, pl.ds(start, part), :] = jnp.broadcast_to(v, (128, part)).T


def gathered_row(sums):
    return jnp.sum(sums.T, axis=0, keepdims=True)


def row_stats(count, load, width, length):
    def total(i, a):
        return a + eight(load(i))

    zero = jnp.zeros((8, length), F32)
    a = lax.fori_loop(0, count, total, zero, unroll=5)
    mean = jnp.sum(a, axis=0, keepdims=True) * (1.0 / width)

    def squares(i, a):
        c = load(i) - mean
        return a + eight(c * c)

    a = lax.fori_loop(0, count, squares, zero, unroll=5)
    var = jnp.sum(a, axis=0, keepdims=True) * (1.0 / width)
    return mean, var


def start_load(pieces, dst, sems):
    shard, first, second, other_first, other_second = pieces
    rows = shard.shape[0]
    off, size = half_of(rows)
    me, core = lax.axis_index("dp"), lax.rem(lax.axis_index("ctx"), 2)
    near = jnp.bitwise_xor(me, 1 + core)
    far = jnp.bitwise_xor(me, 2 - core)
    both = jnp.bitwise_xor(me, 3)

    def at(device, half, count):
        return dst.at[pl.ds(pl.multiple_of(device * rows + half * off, 16), count), :]

    batch_one = [
        (shard, at(me, 0, rows)),
        (first.at[0:size], at(near, core, size)),
        (second.at[0, 0:size], at(far, core, size)),
        (second.at[1, 0:size], at(both, core, size)),
    ]
    batch_two = [
        (other_first.at[0:size], at(far, 1 - core, size)),
        (other_second.at[0, 0:size], at(near, 1 - core, size)),
        (other_second.at[1, 0:size], at(both, 1 - core, size)),
    ]
    copies = [
        pltpu.make_async_copy(src, to, sems.at[i])
        for i, (src, to) in enumerate(batch_one + batch_two)
    ]
    for c in copies[:4]:
        c.start()
    return copies


def finish_load(copies):
    for c in copies[:4]:
        c.wait()
    for c in copies[4:]:
        c.start()
    for c in copies[4:]:
        c.wait()


def assemble(shard, pieces, k, wide_s):
    first, second, other_first, other_second = pieces
    rows = shard.shape[0]
    off, _ = half_of(rows)
    me, core = lax.axis_index("dp"), lax.rem(lax.axis_index("ctx"), 2)
    near = jnp.bitwise_xor(me, 1 + core)
    far = jnp.bitwise_xor(me, 2 - core)
    both = jnp.bitwise_xor(me, 3)

    def put(device, half, piece):
        start = pl.ds(pl.multiple_of(device * rows + half * off, 8), piece.shape[0])
        wide_s[start, :] = piece.astype(F32)

    put(me, 0, shard)
    put(near, core, first[k])
    put(far, core, second[0, k])
    put(both, core, second[1, k])
    put(far, 1 - core, other_first[k])
    put(near, 1 - core, other_second[0, k])
    put(both, 1 - core, other_second[1, k])
    return wide_s[...].astype(BF)


def params(mib=60):
    return pltpu.CompilerParams(vmem_limit_bytes=mib * MIB)


def cost(products, entries):
    return pl.CostEstimate(
        flops=40 * products + 800 * entries, bytes_accessed=1, transcendentals=0
    )


def split_grad(acc_ref, keep_ref, send_ref, taps, first_block=None):
    me, core = lax.axis_index("dp"), lax.rem(lax.axis_index("ctx"), 2)
    block = acc_ref.shape[0] // taps
    width = keep_ref.shape[-1]
    rows = block // 4
    off, size = half_of(rows)
    mine = (0, 2 - core, 1 + core, 3)
    theirs = (0, 1 + core, 2 - core, 3)
    for j in range(4):
        for k in range(taps):
            a = jnp.bitwise_xor(me, mine[j]) * rows + core * off + k * block
            b = jnp.bitwise_xor(me, theirs[j]) * rows + (1 - core) * off + k * block
            for ref, begin in ((keep_ref, a), (send_ref, b)):
                v = acc_ref[pl.ds(pl.multiple_of(begin, 8), size), :].astype(BF)
                if taps > 1:
                    ref[j, k] = v
                elif first_block is None:
                    ref[j] = v
                else:
                    for h in range(v.shape[1] // width):
                        ref[j, first_block + h] = v[:, h * width : (h + 1) * width]


def prepare_in_body(*refs):
    w_ref, out_ref, rows_s = refs[0], refs[-2], refs[-1]
    off, size = half_of(w_ref.shape[0])
    core = lax.rem(lax.axis_index("ctx"), 2)
    out_ref[0:size, :] = w_ref[pl.ds(pl.multiple_of(core * off, 16), size), :]
    rows_s[...] = jnp.zeros_like(rows_s)
    for j, ref in enumerate(refs[1:-2]):
        n = ref.shape[0]
        rows_s[j : j + 1, 0:n] = ref[...].astype(F32).reshape(1, n)
    out_ref[size:, :] = rows_s[...].astype(BF)


def prepare_in(weight, vectors):
    rows, inner = weight.shape
    size = half_of(rows)[1]
    assert size % 16 == 0 and max(v.shape[0] for v in vectors) <= inner and len(vectors) <= 16
    vmem = pl.BlockSpec(memory_space=pltpu.VMEM)
    return pl.pallas_call(
        prepare_in_body,
        in_specs=[vmem] * (1 + len(vectors)),
        out_specs=vmem,
        out_shape=sds((size + 16, inner), BF),
        scratch_shapes=[pltpu.VMEM((16, inner), F32)],
        compiler_params=params(),
        name="prepare_in",
    )(weight, *vectors)


def prepare_rest_body(wc_ref, wo_ref, out_ref):
    inner = wc_ref.shape[2]
    off, size = half_of(wc_ref.shape[1])
    core = lax.rem(lax.axis_index("ctx"), 2)
    r = pl.ds(pl.multiple_of(core * off, 16), size)
    for k in range(3):
        out_ref[k] = wc_ref[k, r, :]
    half = wo_ref[r, :]
    out_ref[3] = half[:, 0:inner]
    out_ref[4] = half[:, inner:]


def prepare_rest(weight_conv, weight_out):
    inner = weight_conv.shape[2]
    vmem = pl.BlockSpec(memory_space=pltpu.VMEM)
    return pl.pallas_call(
        prepare_rest_body,
        in_specs=[vmem] * 2,
        out_specs=vmem,
        out_shape=sds((5, half_of(weight_conv.shape[1])[1], inner), BF),
        compiler_params=params(),
        name="prepare_rest",
    )(weight_conv, weight_out)


def vec_specs(packs):
    own, first, second = packs
    inner = own.shape[1]
    at = own.shape[0] // 16 - 1
    row = pl.BlockSpec((16, inner), lambda s: (at, 0))
    return [row, row, pl.BlockSpec((2, 16, inner), lambda s: (0, at, 0))]


def stats_body(x_ref, st_ref, sq_ref):
    wide, length = x_ref.shape

    @pl.when(pl.program_id(0) == 0)
    def _():
        sq_ref[...] = jnp.zeros_like(sq_ref)

    mean, var = row_stats(wide // ROWS, lambda i: x_ref[rows_at(i), :].astype(F32), wide, length)
    st_ref[0:1, :] = mean
    st_ref[1:2, :] = lax.rsqrt(var + EPS)
    sq_ref[0:1, :] += (var + mean * mean) * float(wide)


def input_stats(x):
    seqs, wide, length = x.shape
    return pl.pallas_call(
        stats_body,
        grid=(seqs,),
        in_specs=[seq((wide, length))],
        out_specs=[seq((8, length)), full((8, length))],
        out_shape=[sds((seqs, 8, length), F32), sds((8, length), F32)],
        compiler_params=params(),
        cost_estimate=cost(0, x.size // 4),
        name="input_stats",
    )(x)


def act_body(x_ref, st_ref, v0, v1, v2, a0_ref, vw_s):
    wide, length = x_ref.shape

    @pl.when(pl.program_id(0) == 0)
    def _():
        for j in range(2):
            spread((v0, v1, v2), vw_s, j, j, 0.5)

    mean = st_ref[0:1, :]
    inv = st_ref[1:2, :]

    def act0(i):
        r = rows_at(i)
        y = (x_ref[r, :].astype(F32) - mean) * inv * col(vw_s, 0, r, length)
        a0_ref[r, :] = silu_of_half(y + col(vw_s, 1, r, length)).astype(BF)

    loop(wide // ROWS, act0, 5)


def first_act(x, stats, packs):
    seqs, wide, length = x.shape
    return pl.pallas_call(
        act_body,
        grid=(seqs,),
        in_specs=[seq((wide, length)), seq((8, length))] + vec_specs(packs),
        out_specs=seq((wide, length)),
        out_shape=sds((seqs, wide, length), BF),
        scratch_shapes=[pltpu.VMEM((2, wide, 128), F32)],
        compiler_params=params(),
        cost_estimate=cost(0, x.size // 2),
        name="first_act",
    )(x, stats, *packs)


def first_body(
    a0_ref, p0, p1, p2, p3, p4, v0, v1, v2,
    h1_ref, a1_ref, edge_ref, sq_ref,
    w_s, wt_s, vi_s, sems,
):
    s = pl.program_id(0)
    inner, length = h1_ref.shape

    @pl.when(s == 0)
    def _():
        copies = start_load((p0, p1, p2, p3, p4), w_s, sems)
        sq_ref[...] = jnp.zeros_like(sq_ref)
        for j in range(3):
            spread((v0, v1, v2), vi_s, j, j + 3, (1.0, 0.5, 0.5)[j])
        finish_load(copies)
        wt_s[...] = w_s[...].T

    h1_ref[...] = mm(wt_s[...], a0_ref[...]) + lanes(vi_s[0], length)
    mean1, var1 = row_stats(inner // ROWS, lambda i: h1_ref[rows_at(i), :], inner, length)
    inv1 = lax.rsqrt(var1 + EPS)
    sq_ref[0:1, :] += (var1 + mean1 * mean1) * float(inner)

    def act1(i):
        r = rows_at(i)
        y = (h1_ref[r, :] - mean1) * inv1 * col(vi_s, 1, r, length) + col(vi_s, 2, r, length)
        a1_ref[r, :] = silu_of_half(y).astype(BF)

    loop(inner // ROWS, act1, 5)
    edge_ref[...] = a1_ref[:, length - 128 :].astype(F32).T[120:128, :].astype(BF)


def first(a0, pieces, packs):
    seqs, wide, length = a0.shape
    inner = pieces[0].shape[1]
    return pl.pallas_call(
        first_body,
        grid=(seqs,),
        in_specs=[seq((wide, length))] + [ANY] * 5 + vec_specs(packs),
        out_specs=[seq((inner, length)), seq((inner, length)), seq((8, inner)), full((8, length))],
        out_shape=[
            sds((seqs, inner, length), F32),
            sds((seqs, inner, length), BF),
            sds((seqs, 8, inner), BF),
            sds((8, length), F32),
        ],
        scratch_shapes=[
            pltpu.VMEM((wide, inner), BF),
            pltpu.VMEM((inner, wide), BF),
            pltpu.VMEM((3, inner, 128), F32),
            pltpu.SemaphoreType.DMA((7,)),
        ],
        compiler_params=params(),
        cost_estimate=cost(a0.size * inner, a0.size),
        name="first_product",
    )(a0, *pieces, *packs)


def assemble_body(wc_own, wo_own, f, g, of, og, wc_ref, wct_ref, wo_ref, tap_s):
    inner = wc_ref.shape[1]
    pieces = (f, g, of, og)
    for k in range(3):
        wc_ref[k] = assemble(wc_own[k], pieces, k, tap_s)
    wct_ref[...] = wc_ref[...].reshape(3 * inner, inner).T
    for k in range(2):
        wo_ref[k] = assemble(wo_own[:, k * inner : (k + 1) * inner], pieces, 3 + k, tap_s)


def assemble_weights(own_conv, own_out, pieces):
    inner = own_conv.shape[2]
    vmem = pl.BlockSpec(memory_space=pltpu.VMEM)
    return pl.pallas_call(
        assemble_body,
        in_specs=[vmem] * 6,
        out_specs=[vmem] * 3,
        out_shape=[
            sds((3, inner, inner), BF),
            sds((inner, 3 * inner), BF),
            sds((2, inner, inner), BF),
        ],
        scratch_shapes=[pltpu.VMEM((inner, inner), F32)],
        compiler_params=params(),
        cost_estimate=cost(0, 4 * inner * inner),
        name="assemble_weights",
    )(own_conv, own_out, *pieces)


def transpose_body(w_ref, wt_ref):
    inner = w_ref.shape[1]
    for k in range(2):
        wt_ref[k * inner : (k + 1) * inner, :] = w_ref[k].T


def transposed(w):
    inner = w.shape[1]
    vmem = pl.BlockSpec(memory_space=pltpu.VMEM)
    return pl.pallas_call(
        transpose_body,
        in_specs=[vmem],
        out_specs=vmem,
        out_shape=sds((2 * inner, inner), BF),
        compiler_params=params(),
        name="transpose_out",
    )(w)


def conv_body(
    a1_ref, halo_ref, dy_ref, dyp_ref, mk_ref, wct_ref, wo_ref, v0, v1, v2,
    a2_ref, dh2_ref, edge_ref, sums_ref, bo_ref, sq_ref, keep_ref, send_ref,
    st_s, a2_s, dh_s, h_s, d_s, hl_s, vi_s, sums_s, bo_s, acc_s, out_s, mi_s,
):
    s = pl.program_id(0)
    seqs = pl.num_programs(0) - 1
    inner, length = a1_ref.shape
    wide = dy_ref.shape[0]
    steps = inner // ROWS
    now, then = lax.rem(s, 2), lax.rem(s + 1, 2)

    @pl.when(s == 0)
    def _():
        sq_ref[...] = jnp.zeros_like(sq_ref)
        sums_s[...] = jnp.zeros_like(sums_s)
        bo_s[...] = jnp.zeros_like(bo_s)
        acc_s[...] = jnp.zeros_like(acc_s)
        out_s[...] = jnp.zeros_like(out_s)
        for j in range(3):
            spread((v0, v1, v2), vi_s, j, j + 6, (1.0, 0.5, 0.5)[j])

    @pl.when(s < seqs)
    def _():
        hl_s[...] = jnp.concatenate(
            [jnp.zeros((120, inner), F32), halo_ref[...].astype(F32)], axis=0
        ).T
        m1 = mk_ref[1:2, :]
        m2 = mk_ref[2:3, :]

        def build(i):
            r = rows_at(i)
            b = a1_ref[r, :]
            v = jnp.concatenate([b.astype(F32), hl_s[r, :]], axis=1)
            st_s[now, r, :] = b
            st_s[now, rows_at(i, inner), :] = (pltpu.roll(v, 2, 1)[:, 0:length] * m1).astype(BF)
            st_s[now, rows_at(i, 2 * inner), :] = (pltpu.roll(v, 4, 1)[:, 0:length] * m2).astype(BF)

        loop(steps, build, 10)
        h_s[...] = mm(wct_ref[...], st_s[now]) + lanes(vi_s[0], length)
        d_s[...] = mm(wo_ref[0], dy_ref[0:inner, :]) + mm(wo_ref[1], dy_ref[inner:, :])

        mean, var = row_stats(steps, lambda i: h_s[rows_at(i), :], inner, length)
        mi_s[0:1, :] = mean
        mi_s[1:2, :] = lax.rsqrt(var + EPS)
        sq_ref[0:1, :] += (var + mean * mean) * float(inner)

    mean = mi_s[0:1, :]
    inv = mi_s[1:2, :]
    zero = jnp.zeros((8, length), F32)

    def back(i, acc):
        r = rows_at(i)
        n = (h_s[r, :] - mean) * inv
        g = col(vi_s, 1, r, length)
        y = n * g + col(vi_s, 2, r, length)
        t = jnp.tanh(y)
        up = 1.0 + t
        a2 = (y * up).astype(BF)
        a2_ref[r, :] = a2
        a2_s[now, r, :] = a2
        e = d_s[r, :] * (up * (1.0 + y * (1.0 - t)))
        q = e * g
        d_s[r, :] = q
        h_s[r, :] = n
        sums_s[0, r, :] += fold(e * n)
        sums_s[1, r, :] += fold(e)
        return acc[0] + eight(q), acc[1] + eight(q * n)

    def means(acc):
        return [jnp.sum(a, axis=0, keepdims=True) * (1.0 / inner) for a in acc]

    def last(i, mq, mqn):
        r = rows_at(i)
        dh = ((d_s[r, :] - mq - h_s[r, :] * mqn) * inv).astype(BF)
        dh2_ref[r, :] = dh
        dh_s[now, r, :] = dh
        sums_s[2, r, :] += fold(dh.astype(F32))

    def block(j):
        return pl.ds(pl.multiple_of(j * inner, 16), inner)

    def grad_tap(j):
        acc_s[block(j), :] += mm(st_s[then, block(j), :], dh_s[then], NT)

    def grad_out(k):
        r = pl.ds(pl.multiple_of(k * (inner // 2), 16), inner // 2)
        out_s[r, :] += mm(a2_s[then, r, :], dyp_ref[...], NT)

    def bias(i):
        r = rows_at(i)
        bo_s[r, :] += fold(dyp_ref[r, :].astype(F32))

    @pl.when(s == 0)
    def _():
        acc = lax.fori_loop(0, steps, back, (zero, zero), unroll=5)
        mq, mqn = means(acc)
        loop(steps, lambda i: last(i, mq, mqn), 5)

    @pl.when(jnp.logical_and(s > 0, s < seqs))
    def _():
        each, some = steps // 3, wide // ROWS // 3
        acc = lax.fori_loop(3 * each, steps, back, (zero, zero), unroll=True)
        for i in range(3 * some, wide // ROWS):
            bias(i)

        def tap(j, acc):
            grad_tap(j)
            for c in range(each):
                acc = back(j * each + c, acc)
            for c in range(some):
                bias(j * some + c)
            return acc

        mq, mqn = means(lax.fori_loop(0, 3, tap, acc))

        def out(k):
            grad_out(k)
            for c in range(steps // 2):
                last(k * (steps // 2) + c, mq, mqn)

        loop(2, out, 1)

    @pl.when(s < seqs)
    def _():
        edge_ref[...] = dh2_ref[:, 0:128].astype(F32).T[0:8, :].astype(BF)

    @pl.when(s == seqs)
    def _():
        loop(3, grad_tap, 1)
        loop(2, grad_out, 1)
        loop(wide // ROWS, bias, 5)
        for j in range(3):
            sums_ref[j : j + 1, :] = gathered_row(sums_s[j]) * (0.5, 0.5, 1.0)[j]
        bo_ref[0:1, :] = gathered_row(bo_s[...])
        split_grad(acc_s, keep_ref, send_ref, 3)
        split_grad(out_s, keep_ref, send_ref, 1, 3)


def conv(a1, halo, dy, mk, wct, wo, packs):
    seqs, inner, length = a1.shape
    wide = dy.shape[1]
    assert inner % (2 * ROWS) == 0
    size = half_of(inner // 4)[1]

    this, previous = functools.partial(this_seq, seqs), previous_seq

    return pl.pallas_call(
        conv_body,
        grid=(seqs + 1,),
        in_specs=[
            this((inner, length)),
            this((8, inner)),
            this((wide, length)),
            previous((wide, length)),
            this((8, length)),
        ]
        + [full(p.shape) for p in (wct, wo)]
        + vec_specs(packs),
        out_specs=[
            this((inner, length)),
            this((inner, length)),
            this((8, inner)),
            full((8, inner)),
            full((8, wide)),
            full((8, length)),
            full((4, 5, size, inner)),
            full((4, 5, size, inner)),
        ],
        out_shape=[
            sds((seqs, inner, length), BF),
            sds((seqs, inner, length), BF),
            sds((seqs, 8, inner), BF),
            sds((8, inner), F32),
            sds((8, wide), F32),
            sds((8, length), F32),
            sds((4, 5, size, inner), BF),
            sds((4, 5, size, inner), BF),
        ],
        scratch_shapes=[
            pltpu.VMEM((2, 3 * inner, length), BF),
            pltpu.VMEM((2, inner, length), BF),
            pltpu.VMEM((2, inner, length), BF),
            pltpu.VMEM((inner, length), F32),
            pltpu.VMEM((inner, length), F32),
            pltpu.VMEM((inner, 128), F32),
            pltpu.VMEM((3, inner, 128), F32),
            pltpu.VMEM((3, inner, 128), F32),
            pltpu.VMEM((wide, 128), F32),
            pltpu.VMEM((3 * inner, inner), F32),
            pltpu.VMEM((inner, wide), F32),
            pltpu.VMEM((8, length), F32),
        ],
        compiler_params=params(),
        cost_estimate=cost(a1.size * (6 * inner + 2 * wide), 2 * a1.size),
        name="conv_and_third_norm",
    )(a1, halo, dy, dy, mk, wct, wo, *packs)


def grad_body(a_ref, b_ref, keep_ref, send_ref, acc_s):
    s = pl.program_id(0)

    @pl.when(s == 0)
    def _():
        acc_s[...] = mm(a_ref[...], b_ref[...], NT)

    @pl.when(s > 0)
    def _():
        acc_s[...] += mm(a_ref[...], b_ref[...], NT)

    @pl.when(s == pl.num_programs(0) - 1)
    def _():
        split_grad(acc_s, keep_ref, send_ref, 1)


def grad(a, b, name):
    seqs, m, length = a.shape
    n = b.shape[1]
    size = half_of(m // 4)[1]
    return pl.pallas_call(
        grad_body,
        grid=(seqs,),
        in_specs=[seq((m, length)), seq((n, length))],
        out_specs=[full((4, size, n)), full((4, size, n))],
        out_shape=[sds((4, size, n), BF), sds((4, size, n), BF)],
        scratch_shapes=[pltpu.VMEM((m, n), F32)],
        compiler_params=params(),
        cost_estimate=cost(a.size * n, 0),
        name=name,
    )(a, b)


def shift_back(dh2_ref, halo_ref, mk_ref, hl_s, t_s):
    inner, length = dh2_ref.shape
    hl_s[...] = jnp.concatenate(
        [halo_ref[...].astype(F32), jnp.zeros((120, inner), F32)], axis=0
    ).T
    f1 = mk_ref[3:4, :]
    f2 = mk_ref[4:5, :]

    def build(i):
        r = rows_at(i)
        b = dh2_ref[r, :]
        v = jnp.concatenate([b.astype(F32), hl_s[r, :]], axis=1)
        t_s[0, r, :] = b
        t_s[1, r, :] = (pltpu.roll(v, length + 126, 1)[:, 0:length] * f1).astype(BF)
        t_s[2, r, :] = (pltpu.roll(v, length + 124, 1)[:, 0:length] * f2).astype(BF)

    loop(inner // ROWS, build, 10)


def conv_back_body(
    dh2_ref, halo_ref, h1_ref, mk_ref, wc_ref, v0, v1, v2,
    dh1_ref, sums_ref,
    t_s, d_s, n_s, hl_s, vi_s, sums_s,
):
    s = pl.program_id(0)
    seqs = pl.num_programs(0) - 1
    inner, length = dh2_ref.shape
    steps = inner // ROWS
    now, then = lax.rem(s, 2), lax.rem(s + 1, 2)

    @pl.when(s == 0)
    def _():
        sums_s[...] = jnp.zeros_like(sums_s)
        for j in range(2):
            spread((v0, v1, v2), vi_s, j, j + 4, 0.5)

    @pl.when(s < seqs)
    def _():
        shift_back(dh2_ref, halo_ref, mk_ref, hl_s, t_s)

    def back_of(mean, inv):
        def back(i, acc):
            r = rows_at(i)
            n = (h1_ref[r, :] - mean) * inv
            g = col(vi_s, 0, r, length)
            y = n * g + col(vi_s, 1, r, length)
            t = jnp.tanh(y)
            e = d_s[then, r, :] * ((1.0 + t) * (1.0 + y * (1.0 - t)))
            q = e * g
            d_s[then, r, :] = q
            n_s[r, :] = n
            sums_s[0, r, :] += fold(e * n)
            sums_s[1, r, :] += fold(e)
            return acc[0] + eight(q), acc[1] + eight(q * n)

        return back

    def close(acc, inv):
        mq, mqn = [jnp.sum(a, axis=0, keepdims=True) * (1.0 / inner) for a in acc]

        def last(i):
            r = rows_at(i)
            dh = ((d_s[then, r, :] - mq - n_s[r, :] * mqn) * inv).astype(BF)
            dh1_ref[r, :] = dh
            sums_s[2, r, :] += fold(dh.astype(F32))

        loop(steps, last, 5)

    def stats():
        mean, var = row_stats(steps, lambda i: h1_ref[rows_at(i), :], inner, length)
        return mean, lax.rsqrt(var + EPS)

    zero = jnp.zeros((8, length), F32)

    @pl.when(s == 0)
    def _():
        d_s[now] = mm(wc_ref[0], t_s[0]) + mm(wc_ref[1], t_s[1]) + mm(wc_ref[2], t_s[2])

    @pl.when(jnp.logical_and(s > 0, s < seqs))
    def _():
        mean, inv = stats()
        back = back_of(mean, inv)
        each = steps // 3
        acc = lax.fori_loop(3 * each, steps, back, (zero, zero), unroll=True)
        for k in range(3):
            part = mm(wc_ref[k], t_s[k])
            d_s[now] = part if k == 0 else d_s[now] + part
            for c in range(each):
                acc = back(k * each + c, acc)
        close(acc, inv)

    @pl.when(s == seqs)
    def _():
        mean, inv = stats()
        close(lax.fori_loop(0, steps, back_of(mean, inv), (zero, zero), unroll=5), inv)
        for j in range(3):
            sums_ref[j : j + 1, :] = gathered_row(sums_s[j]) * (0.5, 0.5, 1.0)[j]


def seq_from(begin, shape):
    return pl.BlockSpec((None,) + shape, lambda s: (s + begin,) + (0,) * len(shape))


def this_seq(seqs, shape):
    return pl.BlockSpec((None,) + shape, lambda s: (jnp.minimum(s, seqs - 1),) + (0,) * len(shape))


def previous_seq(shape):
    return pl.BlockSpec((None,) + shape, lambda s: (jnp.maximum(s - 1, 0),) + (0,) * len(shape))


def conv_back(dh2, halo, h1, mk, wc, packs):
    seqs, inner, length = dh2.shape
    return pl.pallas_call(
        conv_back_body,
        grid=(seqs + 1,),
        in_specs=[
            this_seq(seqs, (inner, length)),
            this_seq(seqs, (8, inner)),
            previous_seq((inner, length)),
            this_seq(seqs, (8, length)),
            full(wc.shape),
        ]
        + vec_specs(packs),
        out_specs=[previous_seq((inner, length)), full((8, inner))],
        out_shape=[sds((seqs, inner, length), BF), sds((8, inner), F32)],
        scratch_shapes=[
            pltpu.VMEM((3, inner, length), BF),
            pltpu.VMEM((2, inner, length), F32),
            pltpu.VMEM((inner, length), F32),
            pltpu.VMEM((inner, 128), F32),
            pltpu.VMEM((2, inner, 128), F32),
            pltpu.VMEM((3, inner, 128), F32),
        ],
        compiler_params=params(),
        cost_estimate=cost(dh2.size * 3 * inner, 2 * dh2.size),
        name="conv_backward",
    )(dh2, halo, h1, mk, wc, *packs)


def stream_body(
    x_ref, st_ref, dy_ref, dh1_ref, p0, p1, p2, p3, p4, v0, v1, v2, before_ref,
    gs_ref, sums_ref,
    w_s, d_s, n_s, vw_s, sums_s, sems,
):
    s = pl.program_id(0)
    wide, length = x_ref.shape
    steps = wide // ROWS

    @pl.when(s == 0)
    def _():
        copies = start_load((p0, p1, p2, p3, p4), w_s, sems)
        sums_s[...] = jnp.zeros_like(sums_s)
        for j in range(2):
            spread((v0, v1, v2), vw_s, j, j, 0.5)
        finish_load(copies)

    d_s[...] = mm(w_s[...], dh1_ref[...])
    mean = st_ref[0:1, :]
    inv = st_ref[1:2, :]

    def back(i, acc):
        r = rows_at(i)
        n = (x_ref[r, :].astype(F32) - mean) * inv
        g = col(vw_s, 0, r, length)
        y = n * g + col(vw_s, 1, r, length)
        t = jnp.tanh(y)
        e = d_s[r, :] * ((1.0 + t) * (1.0 + y * (1.0 - t)))
        q = e * g
        d_s[r, :] = q
        n_s[r, :] = n
        sums_s[0, r, :] += fold(e * n)
        sums_s[1, r, :] += fold(e)
        return acc[0] + eight(q), acc[1] + eight(q * n)

    zero = jnp.zeros((8, length), F32)
    qa, qn = lax.fori_loop(0, steps, back, (zero, zero), unroll=5)
    mq = jnp.sum(qa, axis=0, keepdims=True) * (1.0 / wide)
    mqn = jnp.sum(qn, axis=0, keepdims=True) * (1.0 / wide)

    def last(i):
        r = rows_at(i)
        gs = dy_ref[r, :].astype(F32) + (d_s[r, :] - mq - n_s[r, :] * mqn) * inv
        gs_ref[r, :] = gs.astype(BF)

    loop(steps, last, 5)

    @pl.when(s == pl.num_programs(0) - 1)
    def _():
        for j in range(2):
            sums_ref[j : j + 1, :] = gathered_row(sums_s[j]) * 0.5


def stream_back(x, stats, dy, dh1, pieces, packs, begin, count, before):
    seqs, wide, length = x.shape
    inner = dh1.shape[1]
    aliases = {12: 0} if begin else {}
    return pl.pallas_call(
        stream_body,
        grid=(count,),
        in_specs=[
            seq_from(begin, (wide, length)),
            seq_from(begin, (8, length)),
            seq_from(begin, (wide, length)),
            seq_from(begin, (inner, length)),
        ]
        + [ANY] * 5
        + vec_specs(packs)
        + [ANY],
        out_specs=[seq_from(begin, (wide, length)), full((8, wide))],
        out_shape=[sds((seqs, wide, length), BF), sds((8, wide), F32)],
        input_output_aliases=aliases,
        scratch_shapes=[
            pltpu.VMEM((wide, inner), BF),
            pltpu.VMEM((wide, length), F32),
            pltpu.VMEM((wide, length), F32),
            pltpu.VMEM((2, wide, 128), F32),
            pltpu.VMEM((2, wide, 128), F32),
            pltpu.SemaphoreType.DMA((7,)),
        ],
        compiler_params=params(),
        cost_estimate=cost(dh1.size * wide * count // seqs, x.size * count // seqs),
        name="grad_stream",
    )(x, stats, dy, dh1, *pieces, *packs, before)


def output_body(x_ref, a2_ref, wt_ref, v0, v1, v2, before_ref, out_ref, sq_ref, o_s, vw_s):
    s = pl.program_id(0)
    wide, length = x_ref.shape

    @pl.when(s == 0)
    def _():
        sq_ref[...] = jnp.zeros_like(sq_ref)
        spread((v0, v1, v2), vw_s, 0, 2)

    o_s[...] = mm(wt_ref[...], a2_ref[...])

    def close(i, acc):
        r = rows_at(i)
        branch = o_s[r, :] + col(vw_s, 0, r, length)
        result = x_ref[r, :].astype(F32) + branch
        out_ref[r, :] = result.astype(BF)
        return acc[0] + eight(branch * branch), acc[1] + eight(result * result)

    zero = jnp.zeros((8, length), F32)
    b2, r2 = lax.fori_loop(0, wide // ROWS, close, (zero, zero), unroll=5)
    sq_ref[0:1, :] += jnp.sum(b2, axis=0, keepdims=True)
    sq_ref[1:2, :] += jnp.sum(r2, axis=0, keepdims=True)


def output_of(x, a2, wt, packs, begin, count, before):
    seqs, wide, length = x.shape
    inner = a2.shape[1]
    aliases = {6: 0} if begin else {}
    return pl.pallas_call(
        output_body,
        grid=(count,),
        in_specs=[seq_from(begin, (wide, length)), seq_from(begin, (inner, length))]
        + [full(wt.shape)]
        + vec_specs(packs)
        + [ANY],
        out_specs=[seq_from(begin, (wide, length)), full((8, length))],
        out_shape=[sds((seqs, wide, length), BF), sds((8, length), F32)],
        input_output_aliases=aliases,
        scratch_shapes=[
            pltpu.VMEM((wide, length), F32),
            pltpu.VMEM((1, wide, 128), F32),
        ],
        compiler_params=params(),
        cost_estimate=cost(a2.size * wide * count // seqs, x.size * count // (4 * seqs)),
        name="block_output",
    )(x, a2, wt, *packs, before)


def pack_sums_body(n_one, n_zero, n_out, *refs):
    refs, out_ref = list(refs[:-1]), refs[-1]
    bo, two, q_in, q_one, q_two = (refs.pop(0) for _ in range(5))
    one = sum(refs.pop(0)[0:3, :] for _ in range(n_one))
    zero = sum(refs.pop(0)[0:2, :] for _ in range(n_zero))
    out = sum(refs.pop(0)[0:2, :] for _ in range(n_out))
    inner = two.shape[1]
    out_ref[...] = jnp.zeros_like(out_ref)
    out_ref[0:2, :] = zero
    out_ref[2:3, :] = bo[0:1, :]
    out_ref[3:6, 0:inner] = one
    out_ref[3:6, inner : 2 * inner] = two[0:3, :]
    rows = (q_in[0:1, :], out[1:2, :], q_one[0:1, :], q_two[0:1, :], out[0:1, :])
    for j, row in enumerate(rows):
        total = jnp.sum(row, axis=1, keepdims=True)
        out_ref[6:7, j * 128 : (j + 1) * 128] = jnp.broadcast_to(total, (1, 128))


def pack_sums(bo, two, q_in, q_one, q_two, ones, zeros, outs):
    vmem = pl.BlockSpec(memory_space=pltpu.VMEM)
    args = (bo, two, q_in, q_one, q_two, *ones, *zeros, *outs)
    return pl.pallas_call(
        functools.partial(pack_sums_body, len(ones), len(zeros), len(outs)),
        in_specs=[vmem] * len(args),
        out_specs=vmem,
        out_shape=sds((8, bo.shape[1]), F32),
        compiler_params=params(16),
        name="pack_sums",
    )(*args)


def join_rest_body(mine_ref, other_ref, conv_ref, out_ref):
    core = lax.rem(lax.axis_index("ctx"), 2)
    rows, inner = conv_ref.shape[1:]
    off, size = half_of(rows)
    for k in range(5):
        a, b = mine_ref[k], other_ref[k]
        low = jnp.where(core == 0, a, b).astype(F32)
        high = jnp.where(core == 0, b, a).astype(F32)[size - off :]
        if k < 3:
            conv_ref[k, 0:size, :] = low
            conv_ref[k, size:rows, :] = high
        else:
            out_ref[0:size, (k - 3) * inner : (k - 2) * inner] = low
            out_ref[size:rows, (k - 3) * inner : (k - 2) * inner] = high


def join_rest(mine, other, rows):
    inner = mine.shape[2]
    vmem = pl.BlockSpec(memory_space=pltpu.VMEM)
    return pl.pallas_call(
        join_rest_body,
        in_specs=[vmem] * 2,
        out_specs=[vmem] * 2,
        out_shape=[sds((3, rows, inner), F32), sds((rows, 2 * inner), F32)],
        compiler_params=params(32),
        name="join_rest",
    )(mine, other)


def unpack_body(counts, s_ref, *outs):
    me = lax.axis_index("dp")
    wide = s_ref.shape[1]
    inner = wide // 2

    def part(row, begin, size):
        v = s_ref[row : row + 1, begin : begin + size]
        for d in range(1, 4):
            at = begin + d * size
            v = jnp.where(me == d, s_ref[row : row + 1, at : at + size], v)
        return v.reshape(size)

    for j in range(3):
        outs[j][...] = part(j, 0, wide // 4)
    for j in range(6):
        outs[3 + j][...] = part(3 + j % 3, (j // 3) * inner, inner // 4)
    for j, count in enumerate(counts):
        outs[9 + j][...] = jnp.sqrt(s_ref[6:7, j * 128 : (j + 1) * 128] / count)


def unpack_sums(sums, counts):
    wide = sums.shape[1]
    vmem = pl.BlockSpec(memory_space=pltpu.VMEM)
    return pl.pallas_call(
        functools.partial(unpack_body, counts),
        in_specs=[vmem],
        out_specs=[vmem] * 14,
        out_shape=[sds((wide // 4,), F32)] * 3
        + [sds((wide // 8,), F32)] * 6
        + [sds((1, 128), F32)] * 5,
        compiler_params=params(16),
        name="unpack_sums",
    )(sums)


def local(
    stream, segments, cotangent, gain_zero, shift_zero, weight_in, bias_in, gain_one, shift_one,
    weight_conv, bias_conv, gain_two, shift_two, weight_out, bias_out,
):
    n_dp, n_ctx = lax.axis_size("dp"), lax.axis_size("ctx")
    assert n_dp == 4 and n_ctx & (n_ctx - 1) == 0
    me, place = lax.axis_index("dp"), lax.axis_index("ctx")
    core = place % 2
    seqs, length, wide = stream.shape
    inner = weight_conv.shape[2]
    part_w, part_i = gain_zero.shape[0], bias_in.shape[0]

    x = jnp.swapaxes(stream, 1, 2)
    dy = jnp.swapaxes(cotangent, 1, 2)

    half_in = prepare_in(
        weight_in,
        [gain_zero, shift_zero, bias_out, bias_in, gain_one, shift_one, bias_conv, gain_two, shift_two],
    )
    part_in = gather_halves(half_in)
    sent = next(part_in)
    rest_half = prepare_rest(after(weight_conv, sent), weight_out)
    sent = part_in.send(rest_half)
    stats, sq_in = input_stats(after(x, sent))
    came = part_in.send(sq_in)
    part_rest = gather_halves(after(rest_half, came))
    sent = next(part_rest)
    piece_in = (weight_in, *next(part_in))
    packs = (half_in, *piece_in[1:3])
    act_zero = first_act(x, after(stats, sent), packs)
    sent = part_rest.send(act_zero)

    padded = jnp.pad(segments, ((0, 0), (4, 4)), constant_values=-1)
    near_segs = lax.dynamic_slice_in_dim(padded, place * length, length + 8, 1)
    here = near_segs[:, 4 : 4 + length]
    same = [(near_segs[:, 4 + j : 4 + j + length] == here).astype(F32) for j in (0, -2, -4, 2, 4)]
    masks = jnp.stack(same + same[:3], axis=1)

    hidden_one, act_one, edge, sq_one = first(
        act_zero, piece_in, (after(half_in, sent, masks), *packs[1:])
    )
    halo = shifted(edge, 1)
    part_rest.send(sq_one)
    full_conv, full_conv_t, full_out = assemble_weights(
        weight_conv, weight_out, next(part_rest)
    )
    act_two, d_hidden_two, edge_back, sums_two, sum_bo, sq_two, keep, send = conv(
        act_one, halo, dy, masks, full_conv_t, full_out, packs
    )
    halo_back = shifted(edge_back, -1)
    sum_rest = Stages(sum_shards(keep, send, True))
    own = after(half_in, sum_rest.value)
    full_out_t = transposed(after(full_out, edge_back))
    ones, zeros, outs = [], [], []
    output = grad_x = stats

    def run(what, begin, end):
        nonlocal output, grad_x
        vecs = (own, *packs[1:])
        if what == "out":
            output, sums = output_of(x, act_two, full_out_t, vecs, begin, end - begin, output)
            outs.append(sums)
        else:
            grad_x, sums = stream_back(
                x, stats, dy, d_hidden_one, piece_in, vecs, begin, end - begin, grad_x
            )
            zeros.append(sums)
        return sums

    sums = run("out", 0, 1)
    own = after(own, sum_rest.step(sums))
    d_hidden_one, sums = conv_back(
        d_hidden_two, halo_back, hidden_one, masks, full_conv, (own, *packs[1:])
    )
    ones.append(sums)
    own = after(own, sum_rest.step(sums))
    keep_in, send_in = grad(act_zero, after(d_hidden_one, own), "grad_weight_in")
    sum_in = Stages(sum_shards(keep_in, send_in, False))
    own = after(own, sum_in.value, sum_rest.step(send_in))
    sums = run("out", 1, 2)
    own = after(own, sum_in.step(sums))
    sums = run("stream", 0, 1)
    own = after(own, sum_in.step(sums), sum_rest.step(sums))
    sums = run("out", 2, seqs)
    own = after(own, sum_in.step(sums), sum_rest.step(sums))
    sums = run("stream", 1, 2)
    own = after(own, sum_in.step(sums), sum_rest.step(sums))
    sums = run("stream", 2, seqs)
    sum_rest.step(sums)
    sums = pack_sums(after(sum_bo, sum_in.step(sums)), sums_two, sq_in, sq_one, sq_two, ones, zeros, outs)
    count = float(seqs * length * n_dp * n_ctx)
    total = Stages(sum_all(sums))
    grad_weight_conv, grad_weight_out = join_rest(*sum_rest.result(), part_i)
    grad_weight_in = join_halves(*sum_in.result(), part_w, 0, core)
    total.step(None)
    total.step((grad_weight_out, grad_weight_in))
    sums = total.result()
    totals = unpack_sums(
        sums, (count * wide, count * wide, count * inner, count * inner, count * wide)
    )
    grad_gain_zero, grad_shift_zero, grad_bias_out = totals[0:3]
    grad_gain_one, grad_shift_one, grad_bias_in = totals[3:6]
    grad_gain_two, grad_shift_two, grad_bias_conv = totals[6:9]
    rms_in, rms_out, rms_hidden_one, rms_hidden_two, rms_branch = (v[0, 0] for v in totals[9:])
    return (
        jnp.swapaxes(output, 1, 2),
        jnp.swapaxes(grad_x, 1, 2),
        grad_gain_zero,
        grad_shift_zero,
        grad_weight_in,
        grad_bias_in,
        grad_gain_one,
        grad_shift_one,
        grad_weight_conv,
        grad_bias_conv,
        grad_gain_two,
        grad_shift_two,
        grad_weight_out,
        grad_bias_out,
        rms_in,
        rms_out,
        rms_hidden_one,
        rms_hidden_two,
        rms_branch,
    )


def solution(mesh):
    placed = (
        P("dp", "ctx", None),
        P("dp", None),
        P("dp", "ctx", None),
        P("dp"),
        P("dp"),
        P("dp", None),
        P("dp"),
        P("dp"),
        P("dp"),
        P(None, "dp", None),
        P("dp"),
        P("dp"),
        P("dp"),
        P("dp", None),
        P("dp"),
    )
    return jax.shard_map(
        local,
        mesh=mesh,
        in_specs=placed,
        out_specs=(
            P("dp", "ctx", None),
            P("dp", "ctx", None),
            P("dp"),
            P("dp"),
            P("dp", None),
            P("dp"),
            P("dp"),
            P("dp"),
            P(None, "dp", None),
            P("dp"),
            P("dp"),
            P("dp"),
            P("dp", None),
            P("dp"),
            P(),
            P(),
            P(),
            P(),
            P(),
        ),
        check_vma=False,
    )
```

profile of v0, /device:TPU:0, one launch (start us, length us, event | category | flops | bytes accessed | tf_op | source)
XLA Modules:
  0.0 301.6 jit_solution(13251730844147471321)
XLA Ops:
  2.6 2.9 collective-permute-start
  5.6 2.5 prepare_rest.1
  8.1 3.8 %collective-permute-done.v1.p1 = bf16[224,800]{1,0:T(8,128)(2,1)} collective-permute-done((bf16[224,800]{1,0:T(8,128)(2,1)}, bf16[224,800]{1,0:T(8,128)(2,1)}, u32[]{:S(2)}, u32[]{:S(2)}) %collective-permute-start) | collective-permute-done | bytes 358432 | tf_op jit(solution)/shard_map/ppermute | solution.py:25
  15.0 6.3 %input_stats.1 = (f32[4,8,512]{2,1,0:T(8,128)}, f32[8,512]{1,0:T(8,128)}) custom-call(bf16[4,1600,512]{2,1,0:T(8,128)(2,1)} %bitcast.34), custom_call_target="tpu_custom_call" | custom-call | flops 655360000 | bytes 1 | tf_op jit(solution)/shard_map/input_stats/pallas_call | solution.py:421
  21.3 4.0 %collective-permute-done.1.v2.p2 = bf16[2,224,800]{2,1,0:T(8,128)(2,1)} collective-permute-done((bf16[2,224,800]{2,1,0:T(8,128)(2,1)S(1)}, bf16[2,224,800]{2,1,0:T(8,128)(2,1)}, u32[]{:S(2)}, u32[]{:S(2)}) %collective-permute-start.1) | collective-permute-done | bytes 716832 | tf_op jit(solution)/shard_map/ppermute | solution.py:25
  28.6 8.9 %first_act.1.a0_ref.a_ref = bf16[4,1600,512]{2,1,0:T(8,128)(2,1)} custom-call(bf16[4,1600,512]{2,1,0:T(8,128)(2,1)} %bitcast.35, f32[4,8,512]{2,1,0:T(8,128)} %get-tuple-element.108.st_ref.before_ref, bf16[224,800]{1,0:T(8,128)(2,1)} %prepare_in.1.v0, bf16[224,800]{1,0:T(8,128)(2,1)} %collective-permute-done.v1.p1, ...), custom_call_target="tpu_custom_call" | custom-call | flops 1310720000 | bytes 1 | tf_op jit(solution)/shard_map/first_act/pallas_call | solution.py:454
  44.0 17.5 %first_product.1 = (f32[4,800,512]{2,1,0:T(8,128)}, bf16[4,800,512]{2,1,0:T(8,128)(2,1)}, bf16[4,8,800]{2,1,0:T(8,128)(2,1)}, f32[8,512]{1,0:T(8,128)}) custom-call(bf16[4,1600,512]{2,1,0:T(8,128)(2,1)} %first_act.1.a0_ref.a_ref, bf16[400,800]{1,0:T(8,128)(2,1)} %p0.7, bf16[224,800]{1,0:T(8,128)(2,1)} %collective-permute-done.v1.p1, ...), custom_call_target="tpu_custom_call" | custom-call | flops 107479040000 | bytes 1 | tf_op jit(solution)/shard_map/first_product/pallas_call | solution.py:501
  61.5 3.4 %collective-permute-done.6.g = bf16[2,5,104,800]{3,2,1,0:T(8,128)(2,1)} collective-permute-done((bf16[2,5,104,800]{3,2,1,0:T(8,128)(2,1)S(1)}, bf16[2,5,104,800]{3,2,1,0:T(8,128)(2,1)}, u32[]{:S(2)}, u32[]{:S(2)}) %collective-permute-start.6) | collective-permute-done | bytes 1664032 | tf_op jit(solution)/shard_map/ppermute | solution.py:25
  65.4 2.1 collective-permute-start.5
  67.5 2.3 collective-permute-done.7.of
  71.9 9.5 %assemble_weights.1 = (bf16[3,800,800]{2,1,0:T(8,128)(2,1)}, bf16[800,2400]{1,0:T(8,128)(2,1)}, bf16[2,800,800]{2,1,0:T(8,128)(2,1)}) custom-call(bf16[3,200,800]{2,1,0:T(8,128)(2,1)} %wc_own.1, bf16[200,1600]{1,0:T(8,128)(2,1)} %wo_own.1, bf16[5,104,800]{2,1,0:T(8,128)(2,1)} %copy-done.16, bf16[2,5,104,800]{3,2,1,0:T(8,128)(2,1)} %collective-permute-done.6.g, ...), custom_call_target="tpu_custom_call" | custom-call | flops 2048000000 | bytes 1 | tf_op jit(solution)/shard_map/assemble_weights/pallas_call | solution.py:537
  82.1 56.3 %conv_and_third_norm.1 = (bf16[4,800,512]{2,1,0:T(8,128)(2,1)}, bf16[4,800,512]{2,1,0:T(8,128)(2,1)}, bf16[4,8,800]{2,1,0:T(8,128)(2,1)}, f32[8,800]{1,0:T(8,128...) custom-call(bf16[4,800,512]{2,1,0:T(8,128)(2,1)} %get-tuple-element., ...), custom_call_target="tpu_custom_call" | custom-call | flops 526909440000 | bytes 1 | tf_op jit(solution)/shard_map/conv_and_third_norm/pallas_call | solution.py:719
  140.1 4.2 %transpose_out.1.wt_ref = bf16[1600,800]{1,0:T(8,128)(2,1)} custom-call(bf16[2,800,800]{2,1,0:T(8,128)(2,1)} %get-tuple-element.119.wo_ref.w_ref), custom_call_target="tpu_custom_call" | custom-call | tf_op jit(solution)/shard_map/transpose_out/pallas_call | solution.py:562
  144.3 7.1 %block_output.3 = (bf16[4,1600,512]{2,1,0:T(8,128)(2,1)}, f32[8,512]{1,0:T(8,128)}) custom-call(bf16[4,1600,512]{2,1,0:T(8,128)(2,1)} %bitcast.36, bf16[4,800,512]{2,1,0:T(8,128)(2,1)} %get-tuple-element.117.a2_ref, bf16[1600,800]{1,0:T(8,128)(2,1)} %transpose_out.1.wt_ref, bf16[224,800]{1,0:T(8,128)(2,1)} %prepare_in.1.v0, ...), custom_call_target="tpu_custom_call" | custom-call | flops 26378240000 | bytes 1 | tf_op jit(solution)/shard_map/block_output/pallas_call | solution.py:1058
  151.4 3.2 %add_convert_fusion = bf16[2,5,104,800]{3,2,1,0:T(8,128)(2,1)} fusion(bf16[4,5,104,800]{3,2,1,0:T(8,128)(2,1)} %collective-permute-done.9, bf16[4,5,104,800]{3,2,1,0:T(8,128)(2,1)S(1)} %copy-done.13), kind=kLoop, calls=%fused_computation | loop fusion | flops 3328000 | bytes 4992000 | tf_op jit(solution)/shard_map/convert_element_type | solution.py:86
  157.3 27.2 %conv_backward.1 = (bf16[4,800,512]{2,1,0:T(8,128)(2,1)}, f32[8,800]{1,0:T(8,128)}) custom-call(bf16[4,800,512]{2,1,0:T(8,128)(2,1)} %get-tuple-element.126.dh2_ref, bf16[4,8,800]{2,1,0:T(8,128)(2,1)} %copy-done.23, f32[4,800,512]{2,1,0:T(8,128)} %get-tuple-element.127.h1_ref, f32[4,8,512]{2,1,0:T(8,128)} %stack.63.mk_ref, ...), custom_call_target="tpu_custom_call" | custom-call | flops 159907840000 | bytes 1 | tf_op jit(solution)/shard_map/conv_backward/pallas_call | solution.py:917
  184.4 2.1 fusion
  188.1 11.3 %grad_weight_in.1 = (bf16[4,208,800]{2,1,0:T(8,128)(2,1)}, bf16[4,208,800]{2,1,0:T(8,128)(2,1)}) custom-call(bf16[4,1600,512]{2,1,0:T(8,128)(2,1)} %first_act.1.a0_ref.a_ref, bf16[4,800,512]{2,1,0:T(8,128)(2,1)} %get-tuple-element.133.b_ref.dh1_ref), custom_call_target="tpu_custom_call" | custom-call | flops 104857600000 | bytes 1 | tf_op jit(solution)/shard_map/grad_weight_in/pallas_call | solution.py:791
  200.1 2.2 bitcast_add_fusion
  203.2 2.4 collective-permute-start.15
  205.5 6.8 %block_output.4 = (bf16[4,1600,512]{2,1,0:T(8,128)(2,1)}, f32[8,512]{1,0:T(8,128)}) custom-call(bf16[4,1600,512]{2,1,0:T(8,128)(2,1)} %bitcast.37, bf16[4,800,512]{2,1,0:T(8,128)(2,1)} %get-tuple-element.117.a2_ref, bf16[1600,800]{1,0:T(8,128)(2,1)} %transpose_out.1.wt_ref, bf16[224,800]{1,0:T(8,128)(2,1)} %prepare_in.1.v0, ...), custom_call_target="tpu_custom_call", output_to_operand_aliasing={{0}: (6, {})} | custom-call | flops 26378240000 | bytes 1 | tf_op jit(solution)/shard_map/block_output/pallas_call | solution.py:1058
  212.4 2.2 add_convert_fusion.2
  214.9 11.4 %grad_stream.3 = (bf16[4,1600,512]{2,1,0:T(8,128)(2,1)}, f32[8,1600]{1,0:T(8,128)}) custom-call(bf16[4,1600,512]{2,1,0:T(8,128)(2,1)} %bitcast.38, f32[4,8,512]{2,1,0:T(8,128)} %get-tuple-element.108.st_ref.before_ref, bf16[4,1600,512]{2,1,0:T(8,128)(2,1)} %bitcast.47, bf16[4,800,512]{2,1,0:T(8,128)(2,1)} %get-tuple-element.133.b_ref.dh1_ref, ...), custom_call_target="tpu_custom_call" | custom-call | flops 26869760000 | bytes 1 | tf_op jit(solution)/shard_map/grad_stream/pallas_call | solution.py:1001
  226.5 2.9 collective-permute-start.17
  232.2 9.7 %block_output.5 = (bf16[4,1600,512]{2,1,0:T(8,128)(2,1)}, f32[8,512]{1,0:T(8,128)}) custom-call(bf16[4,1600,512]{2,1,0:T(8,128)(2,1)} %bitcast.39, bf16[4,800,512]{2,1,0:T(8,128)(2,1)} %get-tuple-element.117.a2_ref, bf16[1600,800]{1,0:T(8,128)(2,1)} %transpose_out.1.wt_ref, bf16[224,800]{1,0:T(8,128)(2,1)} %prepare_in.1.v0, ...), custom_call_target="tpu_custom_call", output_to_operand_aliasing={{0}: (6, {})} | custom-call | flops 52756480000 | bytes 1 | tf_op jit(solution)/shard_map/block_output/pallas_call | solution.py:1058
  243.7 2.6 collective-permute-start.18
  246.2 11.4 %grad_stream.4 = (bf16[4,1600,512]{2,1,0:T(8,128)(2,1)}, f32[8,1600]{1,0:T(8,128)}) custom-call(bf16[4,1600,512]{2,1,0:T(8,128)(2,1)} %bitcast.40, f32[4,8,512]{2,1,0:T(8,128)} %get-tuple-element.108.st_ref.before_ref, bf16[4,1600,512]{2,1,0:T(8,128)(2,1)} %bitcast.48, ...), custom_call_target="tpu_custom_call", output_to_operand_aliasing={{0}: (12, {})} | custom-call | flops 26869760000 | bytes 1 | tf_op jit(solution)/shard_map/grad_stream/pallas_call | solution.py:1001
  257.9 2.4 collective-permute-done.18
  260.8 17.4 %grad_stream.5 = (bf16[4,1600,512]{2,1,0:T(8,128)(2,1)}, f32[8,1600]{1,0:T(8,128)}) custom-call(bf16[4,1600,512]{2,1,0:T(8,128)(2,1)} %bitcast.41, f32[4,8,512]{2,1,0:T(8,128)} %get-tuple-element.108.st_ref.before_ref, bf16[4,1600,512]{2,1,0:T(8,128)(2,1)} %bitcast.49, ...), custom_call_target="tpu_custom_call", output_to_operand_aliasing={{0}: (12, {})} | custom-call | flops 53739520000 | bytes 1 | tf_op jit(solution)/shard_map/grad_stream/pallas_call | solution.py:1001
  287.0 2.2 join_rest.1
  291.7 2.2 collective-permute-start.28
  296.3 3.0 %collective-permute-done.29 = f32[8,1600]{1,0:T(8,128)S(1)} collective-permute-done((f32[8,1600]{1,0:T(8,128)S(1)}, f32[8,1600]{1,0:T(8,128)S(1)}, u32[]{:S(2)}, u32[]{:S(2)}) %collective-permute-start.29) | collective-permute-done | bytes 51232 | tf_op jit(solution)/shard_map/ppermute | solution.py:29
  (131 shorter events, 47.0 us)
Async XLA Ops:
  2.6 9.2 %collective-permute-start = (bf16[224,800]{1,0:T(8,128)(2,1)}, bf16[224,800]{1,0:T(8,128)(2,1)}, u32[]{:S(2)}, u32[]{:S(2)}) collective-permute-start(bf16[224,800]{1,0:T(8,128)(2,1)} %prepare_in.1.v0), channel_id=1, source_target_pairs={{0,8},{1,17},{2,10},{3,19},{4,12},{5,21},{6,14},{7,23},{8,0},{9,25... | collective-permute-start | bytes 1075208 | tf_op jit(solution)/shard_map/ppermute | solution.py:25
  12.9 12.3 %collective-permute-start.1 = (bf16[2,224,800]{2,1,0:T(8,128)(2,1)S(1)}, bf16[2,224,800]{2,1,0:T(8,128)(2,1)}, u32[]{:S(2)}, u32[]{:S(2)}) collective-permute-start(bf16[2,224,800]{2,1,0:T(8,128)(2,1)S(1)} %pad_maximum_fusion.3), channel_id=1, source_target_pairs={{0,16},{1,9},{2,18},{3,11},{4,20},{5,13},{6,22},{7,15},{8,24},{9,1... | collective-permute-start | bytes 2150408 | tf_op jit(solution)/shard_map/ppermute | solution.py:25
  25.3 13.5 %collective-permute-start.4 = (bf16[5,104,800]{2,1,0:T(8,128)(2,1)S(1)}, bf16[5,104,800]{2,1,0:T(8,128)(2,1)S(1)}, u32[]{:S(2)}, u32[]{:S(2)}) collective-permute-start(bf16[5,104,800]{2,1,0:T(8,128)(2,1)S(1)} %copy-done.12), channel_id=1, source_target_pairs={{0,8},{1,17},{2,10},{3,19},{4,12},{5,21},{6,14},{7,23},{8,0},{9,25... | collective-permute-start | bytes 2496008 | tf_op jit(solution)/shard_map/ppermute | solution.py:25
  27.2 16.0 %collective-permute-start.3 = (bf16[2,224,800]{2,1,0:T(8,128)(2,1)}, bf16[2,224,800]{2,1,0:T(8,128)(2,1)}, u32[]{:S(2)}, u32[]{:S(2)}) collective-permute-start(bf16[2,224,800]{2,1,0:T(8,128)(2,1)} %collective-permute-done.1.v2.p2), channel_id=1, source_target_pairs={{0,1},{1,0},{2,3},{3,2},{4,5},{5,4},{6,7},{7,6},{8,9},{9,8},{10,11... | collective-permute-start | bytes 2150408 | tf_op jit(solution)/shard_map/ppermute | solution.py:29
  27.2 16.0 %collective-permute-start.2 = (bf16[224,800]{1,0:T(8,128)(2,1)}, bf16[224,800]{1,0:T(8,128)(2,1)S(1)}, u32[]{:S(2)}, u32[]{:S(2)}) collective-permute-start(bf16[224,800]{1,0:T(8,128)(2,1)} %collective-permute-done.v1.p1), channel_id=1, source_target_pairs={{0,1},{1,0},{2,3},{3,2},{4,5},{5,4},{6,7},{7,6},{8,9},{9,8},{10,11... | collective-permute-start | bytes 1075208 | tf_op jit(solution)/shard_map/ppermute | solution.py:29
  41.2 23.7 %copy-start.17 = (bf16[5,104,800]{2,1,0:T(8,128)(2,1)S(1)}, bf16[5,104,800]{2,1,0:T(8,128)(2,1)}, u32[]{:S(2)}) copy-start(bf16[5,104,800]{2,1,0:T(8,128)(2,1)} %copy-done.16) | copy-start | bytes 2496004
  41.2 23.7 %collective-permute-start.6 = (bf16[2,5,104,800]{3,2,1,0:T(8,128)(2,1)S(1)}, bf16[2,5,104,800]{3,2,1,0:T(8,128)(2,1)}, u32[]{:S(2)}, u32[]{:S(2)}) collective-permute-start(bf16[2,5,104,800]{3,2,1,0:T(8,128)(2,1)S(1)} %pad_maximum_fusion), channel_id=1, source_target_pairs={{0,16},{1,9},{2,18},{3,11},{4,20},{5,13},{6,22},{7,15},{8,24},{9,1... | collective-permute-start | bytes 4992008 | tf_op jit(solution)/shard_map/ppermute | solution.py:25
  64.9 5.4 %collective-permute-start.8 = (bf16[2,5,104,800]{3,2,1,0:T(8,128)(2,1)}, bf16[2,5,104,800]{3,2,1,0:T(8,128)(2,1)S(1)}, u32[]{:S(2)}, u32[]{:S(2)}) collective-permute-start(bf16[2,5,104,800]{3,2,1,0:T(8,128)(2,1)} %collective-permute-done.6.g), channel_id=1, source_target_pairs={{0,1},{1,0},{2,3},{3,2},{4,5},{5,4},{6,7},{7,6},{8,9},{9,8},{10,11... | collective-permute-start | bytes 4992008 | tf_op jit(solution)/shard_map/ppermute | solution.py:29
  64.9 4.9 %collective-permute-start.7 = (bf16[5,104,800]{2,1,0:T(8,128)(2,1)S(1)}, bf16[5,104,800]{2,1,0:T(8,128)(2,1)S(1)}, u32[]{:S(2)}, u32[]{:S(2)}) collective-permute-start(bf16[5,104,800]{2,1,0:T(8,128)(2,1)S(1)} %copy-done.17), channel_id=1, source_target_pairs={{0,1},{1,0},{2,3},{3,2},{4,5},{5,4},{6,7},{7,6},{8,9},{9,8},{10,11... | collective-permute-start | bytes 2496008 | tf_op jit(solution)/shard_map/ppermute | solution.py:29
  65.4 16.1 %collective-permute-start.5 = (bf16[4,8,800]{2,1,0:T(8,128)(2,1)}, bf16[4,8,800]{2,1,0:T(8,128)(2,1)S(1)}, u32[]{:S(2)}, u32[]{:S(2)}) collective-permute-start(bf16[4,8,800]{2,1,0:T(8,128)(2,1)} %get-tuple-element.112), channel_id=1, source_target_pairs={{0,1},{1,2},{2,3},{3,4},{4,5},{5,6},{6,7},{8,9},{9,10},{10,11},{11... | collective-permute-start | bytes 153608 | tf_op jit(solution)/shard_map/ppermute | solution.py:34
  138.4 13.0 %collective-permute-start.9 = (bf16[4,5,104,800]{3,2,1,0:T(8,128)(2,1)}, bf16[4,5,104,800]{3,2,1,0:T(8,128)(2,1)}, u32[]{:S(2)}, u32[]{:S(2)}) collective-permute-start(bf16[4,5,104,800]{3,2,1,0:T(8,128)(2,1)} %get-tuple-element.120), channel_id=1, source_target_pairs={{0,1},{1,0},{2,3},{3,2},{4,5},{5,4},{6,7},{7,6},{8,9},{9,8},{10,11... | collective-permute-start | bytes 9984008 | tf_op jit(solution)/shard_map/ppermute | solution.py:29
  138.8 17.8 %collective-permute-start.11 = (bf16[4,8,800]{2,1,0:T(8,128)(2,1)}, bf16[4,8,800]{2,1,0:T(8,128)(2,1)S(1)}, u32[]{:S(2)}, u32[]{:S(2)}) collective-permute-start(bf16[4,8,800]{2,1,0:T(8,128)(2,1)} %get-tuple-element.118), channel_id=1, source_target_pairs={{1,0},{2,1},{3,2},{4,3},{5,4},{6,5},{7,6},{9,8},{10,9},{11,10},{12... | collective-permute-start | bytes 153608 | tf_op jit(solution)/shard_map/ppermute | solution.py:34
  154.6 29.8 %collective-permute-start.10 = (bf16[2,5,104,800]{3,2,1,0:T(8,128)(2,1)}, bf16[2,5,104,800]{3,2,1,0:T(8,128)(2,1)}, u32[]{:S(2)}, u32[]{:S(2)}) collective-permute-start(bf16[2,5,104,800]{3,2,1,0:T(8,128)(2,1)} %add_convert_fusion), channel_id=1, source_target_pairs={{0,8},{1,17},{2,10},{3,19},{4,12},{5,21},{6,14},{7,23},{8,0},{9,25... | collective-permute-start | bytes 4992008 | tf_op jit(solution)/shard_map/ppermute | solution.py:25
  186.5 13.6 %collective-permute-start.12 = (bf16[5,104,800]{2,1,0:T(8,128)(2,1)S(1)}, bf16[5,104,800]{2,1,0:T(8,128)(2,1)S(1)}, u32[]{:S(2)}, u32[]{:S(2)}) collective-permute-start(bf16[5,104,800]{2,1,0:T(8,128)(2,1)S(1)} %fusion), channel_id=1, source_target_pairs={{0,16},{1,9},{2,18},{3,11},{4,20},{5,13},{6,22},{7,15},{8,24},{9,1... | collective-permute-start | bytes 2496008 | tf_op jit(solution)/shard_map/ppermute | solution.py:25
  199.4 12.9 %collective-permute-start.13 = (bf16[4,208,800]{2,1,0:T(8,128)(2,1)}, bf16[4,208,800]{2,1,0:T(8,128)(2,1)}, u32[]{:S(2)}, u32[]{:S(2)}) collective-permute-start(bf16[4,208,800]{2,1,0:T(8,128)(2,1)} %get-tuple-element.134), channel_id=1, source_target_pairs={{0,1},{1,0},{2,3},{3,2},{4,5},{5,4},{6,7},{7,6},{8,9},{9,8},{10,11... | collective-permute-start | bytes 3993608 | tf_op jit(solution)/shard_map/ppermute | solution.py:29
  203.2 23.2 %collective-permute-start.15 = (bf16[5,56,800]{2,1,0:T(8,128)(2,1)}, bf16[5,56,800]{2,1,0:T(8,128)(2,1)S(1)}, u32[]{:S(2)}, u32[]{:S(2)}) collective-permute-start(bf16[5,56,800]{2,1,0:T(8,128)(2,1)} %dynamic-slice_convert_fusion), channel_id=1, source_target_pairs={{0,2},{1,3},{2,0},{3,1},{4,6},{5,7},{6,4},{7,5},{8,10},{9,11},{10,... | collective-permute-start | bytes 1344008 | tf_op jit(solution)/shard_map/ppermute | solution.py:29
  214.6 14.8 %collective-permute-start.14 = (bf16[2,208,800]{2,1,0:T(8,128)(2,1)}, bf16[2,208,800]{2,1,0:T(8,128)(2,1)S(1)}, u32[]{:S(2)}, u32[]{:S(2)}) collective-permute-start(bf16[2,208,800]{2,1,0:T(8,128)(2,1)} %add_convert_fusion.2), channel_id=1, source_target_pairs={{0,8},{1,17},{2,10},{3,19},{4,12},{5,21},{6,14},{7,23},{8,0},{9,25... | collective-permute-start | bytes 1996808 | tf_op jit(solution)/shard_map/ppermute | solution.py:25
  226.5 15.4 %collective-permute-start.17 = (bf16[5,32,800]{2,1,0:T(8,128)(2,1)S(1)}, bf16[5,32,800]{2,1,0:T(8,128)(2,1)S(1)}, u32[]{:S(2)}, u32[]{:S(2)}) collective-permute-start(bf16[5,32,800]{2,1,0:T(8,128)(2,1)S(1)} %dynamic-slice_convert_fusion.1), channel_id=1, source_target_pairs={{0,4},{1,5},{2,6},{3,7},{4,0},{5,1},{6,2},{7,3},{8,12},{9,13},{10,... | collective-permute-start | bytes 768008 | tf_op jit(solution)/shard_map/ppermute | solution.py:29
  230.6 11.8 %collective-permute-start.16 = (bf16[208,800]{1,0:T(8,128)(2,1)S(1)}, bf16[208,800]{1,0:T(8,128)(2,1)S(1)}, u32[]{:S(2)}, u32[]{:S(2)}) collective-permute-start(bf16[208,800]{1,0:T(8,128)(2,1)S(1)} %fusion.4), channel_id=1, source_target_pairs={{0,16},{1,9},{2,18},{3,11},{4,20},{5,13},{6,22},{7,15},{8,24},{9,1... | collective-permute-start | bytes 998408 | tf_op jit(solution)/shard_map/ppermute | solution.py:25
  242.0 15.7 %collective-permute-start.19 = (bf16[5,32,800]{2,1,0:T(8,128)(2,1)S(1)}, bf16[5,32,800]{2,1,0:T(8,128)(2,1)S(1)}, u32[]{:S(2)}, u32[]{:S(2)}) collective-permute-start(bf16[5,32,800]{2,1,0:T(8,128)(2,1)S(1)} %add_convert_fusion.5), channel_id=1, source_target_pairs={{0,4},{1,5},{2,6},{3,7},{4,0},{5,1},{6,2},{7,3},{8,12},{9,13},{10,... | collective-permute-start | bytes 768008 | tf_op jit(solution)/shard_map/ppermute | solution.py:29
  243.7 16.7 %collective-permute-start.18 = (bf16[208,800]{1,0:T(8,128)(2,1)S(1)}, bf16[208,800]{1,0:T(8,128)(2,1)S(1)}, u32[]{:S(2)}, u32[]{:S(2)}) collective-permute-start(bf16[208,800]{1,0:T(8,128)(2,1)S(1)} %fusion.1), channel_id=1, source_target_pairs={{0,2},{1,3},{2,0},{3,1},{4,6},{5,7},{6,4},{7,5},{8,10},{9,11},{10,... | collective-permute-start | bytes 998408 | tf_op jit(solution)/shard_map/ppermute | solution.py:29
  257.8 20.7 %collective-permute-start.23 = (bf16[5,56,800]{2,1,0:T(8,128)(2,1)S(1)}, bf16[5,56,800]{2,1,0:T(8,128)(2,1)S(1)}, u32[]{:S(2)}, u32[]{:S(2)}) collective-permute-start(bf16[5,56,800]{2,1,0:T(8,128)(2,1)S(1)} %pad_maximum_fusion.4), channel_id=1, source_target_pairs={{0,2},{1,3},{2,0},{3,1},{4,6},{5,7},{6,4},{7,5},{8,10},{9,11},{10,... | collective-permute-start | bytes 1344008 | tf_op jit(solution)/shard_map/ppermute | solution.py:29
  260.4 18.7 %collective-permute-start.20 = (bf16[208,800]{1,0:T(8,128)(2,1)S(1)}, bf16[208,800]{1,0:T(8,128)(2,1)S(1)}, u32[]{:S(2)}, u32[]{:S(2)}) collective-permute-start(bf16[208,800]{1,0:T(8,128)(2,1)S(1)} %add_convert_fusion.3), channel_id=1, source_target_pairs={{0,4},{1,5},{2,6},{3,7},{4,0},{5,1},{6,2},{7,3},{8,12},{9,13},{10,... | collective-permute-start | bytes 998408 | tf_op jit(solution)/shard_map/ppermute | solution.py:29
  279.0 7.9 %collective-permute-start.24 = (bf16[5,104,800]{2,1,0:T(8,128)(2,1)S(1)}, bf16[5,104,800]{2,1,0:T(8,128)(2,1)S(1)}, u32[]{:S(2)}, u32[]{:S(2)}) collective-permute-start(bf16[5,104,800]{2,1,0:T(8,128)(2,1)S(1)} %pad_maximum_fusion.2.mine_ref), channel_id=1, source_target_pairs={{0,1},{1,0},{2,3},{3,2},{4,5},{5,4},{6,7},{7,6},{8,9},{9,8},{10,11... | collective-permute-start | bytes 2496008 | tf_op jit(solution)/shard_map/ppermute | solution.py:29
  280.1 9.0 %collective-permute-start.25 = (f32[208,800]{1,0:T(8,128)}, f32[208,800]{1,0:T(8,128)S(1)}, u32[]{:S(2)}, u32[]{:S(2)}) collective-permute-start(f32[208,800]{1,0:T(8,128)} %convert_add_fusion.1), channel_id=1, source_target_pairs={{0,1},{1,0},{2,3},{3,2},{4,5},{5,4},{6,7},{7,6},{8,9},{9,8},{10,11... | collective-permute-start | bytes 1996808 | tf_op jit(solution)/shard_map/ppermute | solution.py:29
  280.8 2.0 collective-permute-start.21
  282.7 4.2 %collective-permute-start.22 = (f32[8,1600]{1,0:T(8,128)S(1)}, f32[8,1600]{1,0:T(8,128)S(1)}, u32[]{:S(2)}, u32[]{:S(2)}) collective-permute-start(f32[8,1600]{1,0:T(8,128)S(1)} %add.135), channel_id=1, source_target_pairs={{0,8},{8,0},{16,24},{24,16},{1,9},{9,1},{17,25},{25,17},{2,10},{10... | collective-permute-start | bytes 153608 | tf_op jit(solution)/shard_map/ppermute | solution.py:29
  283.7 7.9 %collective-permute-start.26 = (f32[8,1600]{1,0:T(8,128)S(1)}, f32[8,1600]{1,0:T(8,128)S(1)}, u32[]{:S(2)}, u32[]{:S(2)}) collective-permute-start(f32[8,1600]{1,0:T(8,128)S(1)} %add.135), channel_id=1, source_target_pairs={{0,16},{8,24},{16,0},{24,8},{1,17},{9,25},{17,1},{25,9},{2,18},{10... | collective-permute-start | bytes 153608 | tf_op jit(solution)/shard_map/ppermute | solution.py:29
  285.2 6.5 %collective-permute-start.27 = (f32[8,1600]{1,0:T(8,128)S(1)}, f32[8,1600]{1,0:T(8,128)S(1)}, u32[]{:S(2)}, u32[]{:S(2)}) collective-permute-start(f32[8,1600]{1,0:T(8,128)S(1)} %add.135), channel_id=1, source_target_pairs={{0,24},{8,16},{16,8},{24,0},{1,25},{9,17},{17,9},{25,1},{2,26},{10... | collective-permute-start | bytes 153608 | tf_op jit(solution)/shard_map/ppermute | solution.py:29
  291.7 4.6 %collective-permute-start.28 = (f32[8,1600]{1,0:T(8,128)S(1)}, f32[8,1600]{1,0:T(8,128)S(1)}, u32[]{:S(2)}, u32[]{:S(2)}) collective-permute-start(f32[8,1600]{1,0:T(8,128)S(1)} %add_add_fusion.1), channel_id=1, source_target_pairs={{0,2},{1,3},{2,0},{3,1},{4,6},{5,7},{6,4},{7,5},{8,10},{9,11},{10,... | collective-permute-start | bytes 153608 | tf_op jit(solution)/shard_map/ppermute | solution.py:29
  293.9 5.5 %collective-permute-start.29 = (f32[8,1600]{1,0:T(8,128)S(1)}, f32[8,1600]{1,0:T(8,128)S(1)}, u32[]{:S(2)}, u32[]{:S(2)}) collective-permute-start(f32[8,1600]{1,0:T(8,128)S(1)} %add_add_fusion.1), channel_id=1, source_target_pairs={{0,4},{1,5},{2,6},{3,7},{4,0},{5,1},{6,2},{7,3},{8,12},{9,13},{10,... | collective-permute-start | bytes 153608 | tf_op jit(solution)/shard_map/ppermute | solution.py:29
  294.6 5.9 %collective-permute-start.30 = (f32[8,1600]{1,0:T(8,128)S(1)}, f32[8,1600]{1,0:T(8,128)S(1)}, u32[]{:S(2)}, u32[]{:S(2)}) collective-permute-start(f32[8,1600]{1,0:T(8,128)S(1)} %add_add_fusion.1), channel_id=1, source_target_pairs={{0,6},{1,7},{2,4},{3,5},{4,2},{5,3},{6,0},{7,1},{8,14},{9,15},{10,... | collective-permute-start | bytes 153608 | tf_op jit(solution)/shard_map/ppermute | solution.py:29
  (23 other events, 72.0 us)
where the time goes:
time: 306 us; the launch traced here: 302 us
  Pallas kernels  213 us (70%)
  starting transfers between devices  37.3 us (12%)
  waiting for transfers between devices  24.8 us (8%)
  other arithmetic  19.1 us (6%)
  local copies, waits for them, and re-layouts  6.31 us (2%)
    pallas_call x1, Pallas kernels, conv(): pl.pallas_call(conv_body, grid=(seqs + 1,), in_specs=[this((inner, length...  56.3 us
    pallas_call x3, Pallas kernels, stream_back(): pl.pallas_call(stream_body, grid=(count,), in_specs=[seq_from(begin, (wid...  40.2 us
    pallas_call x1, Pallas kernels, conv_back(): pl.pallas_call(conv_back_body, grid=(seqs + 1,), in_specs=[this_seq(seqs,...  27.2 us
    pallas_call x3, Pallas kernels, output_of(): pl.pallas_call(output_body, grid=(count,), in_specs=[seq_from(begin, (wid...  23.6 us
    ppermute x21, starting transfers between devices, swap(): lax.ppermute(value, axis, [(i, i ^ mask) for i in range(lax.axis_size(axi...  19.4 us
    pallas_call x1, Pallas kernels, first(): pl.pallas_call(first_body, grid=(seqs,), in_specs=[seq((wide, length))] +...  17.5 us
    ppermute x8, starting transfers between devices, by_core(): return lax.ppermute(value, ('dp', 'ctx'), pairs)  14.5 us
    ppermute x8, waiting for transfers between devices, by_core(): return lax.ppermute(value, ('dp', 'ctx'), pairs)  12.5 us
  transfers between devices with their start and end apart: 31, of which 13 were waited for; matrix products, arithmetic and copies ran while one was open for 6% of the time, Pallas kernels for 51%

commit v1 on v0

--- a/solution.py
+++ b/solution.py
@@ -155,15 +155,6 @@
         return self.value
 
 
-def join_halves(mine, other, rows, row_dim, core):
-    off, size = half_of(rows)
-    low = jnp.where(core == 0, mine, other)
-    high = jnp.where(core == 0, other, mine)
-    return jnp.concatenate(
-        [low, lax.slice_in_dim(high, size - off, size, axis=row_dim)], axis=row_dim
-    )
-
-
 def mm(left, right, dims=NN):
     return lax.dot_general(left, right, dims, preferred_element_type=F32)
 
@@ -466,8 +457,8 @@
 
 def first_body(
     a0_ref, p0, p1, p2, p3, p4, v0, v1, v2,
-    h1_ref, a1_ref, edge_ref, sq_ref,
-    w_s, wt_s, vi_s, sems,
+    h1_ref, a1_ref, edge_ref, sq_ref, st_ref, w_ref,
+    w_s, wt_s, vi_s, sems, out_sem,
 ):
     s = pl.program_id(0)
     inner, length = h1_ref.shape
@@ -479,11 +470,14 @@
         for j in range(3):
             spread((v0, v1, v2), vi_s, j, j + 3, (1.0, 0.5, 0.5)[j])
         finish_load(copies)
+        pltpu.make_async_copy(w_s, w_ref, out_sem).start()
         wt_s[...] = w_s[...].T
 
     h1_ref[...] = mm(wt_s[...], a0_ref[...]) + lanes(vi_s[0], length)
     mean1, var1 = row_stats(inner // ROWS, lambda i: h1_ref[rows_at(i), :], inner, length)
     inv1 = lax.rsqrt(var1 + EPS)
+    st_ref[0:1, :] = mean1
+    st_ref[1:2, :] = inv1
     sq_ref[0:1, :] += (var1 + mean1 * mean1) * float(inner)
 
     def act1(i):
@@ -494,6 +488,10 @@
     loop(inner // ROWS, act1, 5)
     edge_ref[...] = a1_ref[:, length - 128 :].astype(F32).T[120:128, :].astype(BF)
 
+    @pl.when(s == pl.num_programs(0) - 1)
+    def _():
+        pltpu.make_async_copy(w_s, w_ref, out_sem).wait()
+
 
 def first(a0, pieces, packs):
     seqs, wide, length = a0.shape
@@ -502,18 +500,28 @@
         first_body,
         grid=(seqs,),
         in_specs=[seq((wide, length))] + [ANY] * 5 + vec_specs(packs),
-        out_specs=[seq((inner, length)), seq((inner, length)), seq((8, inner)), full((8, length))],
+        out_specs=[
+            seq((inner, length)),
+            seq((inner, length)),
+            seq((8, inner)),
+            full((8, length)),
+            seq((8, length)),
+            ANY,
+        ],
         out_shape=[
             sds((seqs, inner, length), F32),
             sds((seqs, inner, length), BF),
             sds((seqs, 8, inner), BF),
             sds((8, length), F32),
+            sds((seqs, 8, length), F32),
+            sds((wide, inner), BF),
         ],
         scratch_shapes=[
             pltpu.VMEM((wide, inner), BF),
             pltpu.VMEM((inner, wide), BF),
             pltpu.VMEM((3, inner, 128), F32),
             pltpu.SemaphoreType.DMA((7,)),
+            pltpu.SemaphoreType.DMA,
         ],
         compiler_params=params(),
         cost_estimate=cost(a0.size * inner, a0.size),
@@ -821,7 +829,7 @@
 
 
 def conv_back_body(
-    dh2_ref, halo_ref, h1_ref, mk_ref, wc_ref, v0, v1, v2,
+    dh2_ref, halo_ref, h1_ref, st_ref, mk_ref, wc_ref, v0, v1, v2,
     dh1_ref, sums_ref,
     t_s, d_s, n_s, hl_s, vi_s, sums_s,
 ):
@@ -870,8 +878,7 @@
         loop(steps, last, 5)
 
     def stats():
-        mean, var = row_stats(steps, lambda i: h1_ref[rows_at(i), :], inner, length)
-        return mean, lax.rsqrt(var + EPS)
+        return st_ref[0:1, :], st_ref[1:2, :]
 
     zero = jnp.zeros((8, length), F32)
 
@@ -912,7 +919,7 @@
     return pl.BlockSpec((None,) + shape, lambda s: (jnp.maximum(s - 1, 0),) + (0,) * len(shape))
 
 
-def conv_back(dh2, halo, h1, mk, wc, packs):
+def conv_back(dh2, halo, h1, stats, mk, wc, packs):
     seqs, inner, length = dh2.shape
     return pl.pallas_call(
         conv_back_body,
@@ -921,6 +928,7 @@
             this_seq(seqs, (inner, length)),
             this_seq(seqs, (8, inner)),
             previous_seq((inner, length)),
+            previous_seq((8, length)),
             this_seq(seqs, (8, length)),
             full(wc.shape),
         ]
@@ -938,13 +946,13 @@
         compiler_params=params(),
         cost_estimate=cost(dh2.size * 3 * inner, 2 * dh2.size),
         name="conv_backward",
-    )(dh2, halo, h1, mk, wc, *packs)
+    )(dh2, halo, h1, stats, mk, wc, *packs)
 
 
 def stream_body(
-    x_ref, st_ref, dy_ref, dh1_ref, p0, p1, p2, p3, p4, v0, v1, v2, before_ref,
+    x_ref, st_ref, dy_ref, dh1_ref, w_ref, v0, v1, v2, before_ref,
     gs_ref, sums_ref,
-    w_s, d_s, n_s, vw_s, sums_s, sems,
+    d_s, n_s, vw_s, sums_s,
 ):
     s = pl.program_id(0)
     wide, length = x_ref.shape
@@ -952,13 +960,11 @@
 
     @pl.when(s == 0)
     def _():
-        copies = start_load((p0, p1, p2, p3, p4), w_s, sems)
         sums_s[...] = jnp.zeros_like(sums_s)
         for j in range(2):
             spread((v0, v1, v2), vw_s, j, j, 0.5)
-        finish_load(copies)
-
-    d_s[...] = mm(w_s[...], dh1_ref[...])
+
+    d_s[...] = mm(w_ref[...], dh1_ref[...])
     mean = st_ref[0:1, :]
     inv = st_ref[1:2, :]
 
@@ -994,10 +1000,10 @@
             sums_ref[j : j + 1, :] = gathered_row(sums_s[j]) * 0.5
 
 
-def stream_back(x, stats, dy, dh1, pieces, packs, begin, count, before):
+def stream_back(x, stats, dy, dh1, w, packs, begin, count, before):
     seqs, wide, length = x.shape
     inner = dh1.shape[1]
-    aliases = {12: 0} if begin else {}
+    aliases = {8: 0} if begin else {}
     return pl.pallas_call(
         stream_body,
         grid=(count,),
@@ -1006,25 +1012,23 @@
             seq_from(begin, (8, length)),
             seq_from(begin, (wide, length)),
             seq_from(begin, (inner, length)),
+            full(w.shape),
         ]
-        + [ANY] * 5
         + vec_specs(packs)
         + [ANY],
         out_specs=[seq_from(begin, (wide, length)), full((8, wide))],
         out_shape=[sds((seqs, wide, length), BF), sds((8, wide), F32)],
         input_output_aliases=aliases,
         scratch_shapes=[
-            pltpu.VMEM((wide, inner), BF),
             pltpu.VMEM((wide, length), F32),
             pltpu.VMEM((wide, length), F32),
             pltpu.VMEM((2, wide, 128), F32),
             pltpu.VMEM((2, wide, 128), F32),
-            pltpu.SemaphoreType.DMA((7,)),
         ],
         compiler_params=params(),
         cost_estimate=cost(dh1.size * wide * count // seqs, x.size * count // seqs),
         name="grad_stream",
-    )(x, stats, dy, dh1, *pieces, *packs, before)
+    )(x, stats, dy, dh1, w, *packs, before)
 
 
 def output_body(x_ref, a2_ref, wt_ref, v0, v1, v2, before_ref, out_ref, sq_ref, o_s, vw_s):
@@ -1106,33 +1110,44 @@
     )(*args)
 
 
-def join_rest_body(mine_ref, other_ref, conv_ref, out_ref):
+def join_body(mine_ref, other_ref, mine_in, other_in, conv_ref, out_ref, in_ref):
     core = lax.rem(lax.axis_index("ctx"), 2)
     rows, inner = conv_ref.shape[1:]
-    off, size = half_of(rows)
+
+    def halves(a, b, total):
+        off, size = half_of(total)
+        low = jnp.where(core == 0, a, b).astype(F32)
+        high = jnp.where(core == 0, b, a).astype(F32)
+        return size, low, high[size - off :]
+
     for k in range(5):
-        a, b = mine_ref[k], other_ref[k]
-        low = jnp.where(core == 0, a, b).astype(F32)
-        high = jnp.where(core == 0, b, a).astype(F32)[size - off :]
+        size, low, high = halves(mine_ref[k], other_ref[k], rows)
         if k < 3:
             conv_ref[k, 0:size, :] = low
             conv_ref[k, size:rows, :] = high
         else:
             out_ref[0:size, (k - 3) * inner : (k - 2) * inner] = low
             out_ref[size:rows, (k - 3) * inner : (k - 2) * inner] = high
-
-
-def join_rest(mine, other, rows):
-    inner = mine.shape[2]
+    size, low, high = halves(mine_in[...], other_in[...], in_ref.shape[0])
+    in_ref[0:size, :] = low
+    in_ref[size:, :] = high
+
+
+def join_grads(rest, rows, of_in, rows_in):
+    inner = of_in[0].shape[1]
     vmem = pl.BlockSpec(memory_space=pltpu.VMEM)
     return pl.pallas_call(
-        join_rest_body,
-        in_specs=[vmem] * 2,
-        out_specs=[vmem] * 2,
-        out_shape=[sds((3, rows, inner), F32), sds((rows, 2 * inner), F32)],
+        join_body,
+        in_specs=[vmem] * 4,
+        out_specs=[vmem] * 3,
+        out_shape=[
+            sds((3, rows, inner), F32),
+            sds((rows, 2 * inner), F32),
+            sds((rows_in, inner), F32),
+        ],
         compiler_params=params(32),
-        name="join_rest",
-    )(mine, other)
+        name="join_grads",
+    )(*rest, *of_in)
 
 
 def unpack_body(counts, s_ref, *outs):
@@ -1177,7 +1192,6 @@
     n_dp, n_ctx = lax.axis_size("dp"), lax.axis_size("ctx")
     assert n_dp == 4 and n_ctx & (n_ctx - 1) == 0
     me, place = lax.axis_index("dp"), lax.axis_index("ctx")
-    core = place % 2
     seqs, length, wide = stream.shape
     inner = weight_conv.shape[2]
     part_w, part_i = gain_zero.shape[0], bias_in.shape[0]
@@ -1208,7 +1222,7 @@
     same = [(near_segs[:, 4 + j : 4 + j + length] == here).astype(F32) for j in (0, -2, -4, 2, 4)]
     masks = jnp.stack(same + same[:3], axis=1)
 
-    hidden_one, act_one, edge, sq_one = first(
+    hidden_one, act_one, edge, sq_one, stats_one, full_in = first(
         act_zero, piece_in, (after(half_in, sent, masks), *packs[1:])
     )
     halo = shifted(edge, 1)
@@ -1234,7 +1248,7 @@
             outs.append(sums)
         else:
             grad_x, sums = stream_back(
-                x, stats, dy, d_hidden_one, piece_in, vecs, begin, end - begin, grad_x
+                x, stats, dy, d_hidden_one, full_in, vecs, begin, end - begin, grad_x
             )
             zeros.append(sums)
         return sums
@@ -1242,7 +1256,7 @@
     sums = run("out", 0, 1)
     own = after(own, sum_rest.step(sums))
     d_hidden_one, sums = conv_back(
-        d_hidden_two, halo_back, hidden_one, masks, full_conv, (own, *packs[1:])
+        d_hidden_two, halo_back, hidden_one, stats_one, masks, full_conv, (own, *packs[1:])
     )
     ones.append(sums)
     own = after(own, sum_rest.step(sums))
@@ -1262,8 +1276,9 @@
     sums = pack_sums(after(sum_bo, sum_in.step(sums)), sums_two, sq_in, sq_one, sq_two, ones, zeros, outs)
     count = float(seqs * length * n_dp * n_ctx)
     total = Stages(sum_all(sums))
-    grad_weight_conv, grad_weight_out = join_rest(*sum_rest.result(), part_i)
-    grad_weight_in = join_halves(*sum_in.result(), part_w, 0, core)
+    grad_weight_conv, grad_weight_out, grad_weight_in = join_grads(
+        sum_rest.result(), part_i, sum_in.result(), part_w
+    )
     total.step(None)
     total.step((grad_weight_out, grad_weight_in))
     sums = total.result()

time: 306 us -> 301 us (0.984)
  Pallas kernels: 213 us -> 206 us
  waiting for transfers between devices: 24.8 us -> 30.2 us
  other arithmetic: 19.1 us -> 15.7 us
    pallas_call x3, Pallas kernels: 40.2 us -> 34.5 us  [stream_back(): pl.pallas_call(stream_body, grid=(count,), in_specs=[seq_from(begin, (wid...]
    ppermute x21, waiting for transfers between devices: 12.3 us -> 17.9 us  [swap(): lax.ppermute(value, axis, [(i, i ^ mask) for i in range(lax.axis_size(axi...]
  transfers between devices with their start and end apart: 31 -> 31, of which waited for: 13 -> 15; matrix products, arithmetic and copies ran while one was open for 6% -> 5% of each run, Pallas kernels for 51% -> 49%
where the time goes in v1:
time: 301 us; the launch traced here: 297 us
  Pallas kernels  206 us (68%)
  starting transfers between devices  37.6 us (12%)
  waiting for transfers between devices  30.2 us (10%)
  other arithmetic  15.7 us (5%)
  local copies, waits for them, and re-layouts  6.32 us (2%)
    pallas_call x1, Pallas kernels, conv(): pl.pallas_call(conv_body, grid=(seqs + 1,), in_specs=[this((inner, length...  56.5 us
    pallas_call x3, Pallas kernels, stream_back(): pl.pallas_call(stream_body, grid=(count,), in_specs=[seq_from(begin, (wid...  34.5 us
    pallas_call x1, Pallas kernels, conv_back(): pl.pallas_call(conv_back_body, grid=(seqs + 1,), in_specs=[this_seq(seqs,...  25.5 us
    pallas_call x3, Pallas kernels, output_of(): pl.pallas_call(output_body, grid=(count,), in_specs=[seq_from(begin, (wid...  23.2 us
    ppermute x21, starting transfers between devices, swap(): lax.ppermute(value, axis, [(i, i ^ mask) for i in range(lax.axis_size(axi...  19.3 us
    ppermute x21, waiting for transfers between devices, swap(): lax.ppermute(value, axis, [(i, i ^ mask) for i in range(lax.axis_size(axi...  17.9 us
    pallas_call x1, Pallas kernels, first(): pl.pallas_call(first_body, grid=(seqs,), in_specs=[seq((wide, length))] +...  17.7 us
    ppermute x8, starting transfers between devices, by_core(): return lax.ppermute(value, ('dp', 'ctx'), pairs)  14.5 us
  transfers between devices with their start and end apart: 31, of which 15 were waited for; matrix products, arithmetic and copies ran while one was open for 5% of the time, Pallas kernels for 49%

profile of v1, /device:TPU:0, one launch (start us, length us, event | category | flops | bytes accessed | tf_op | source)
XLA Modules:
  0.0 296.8 jit_solution(1492007192539452338)
XLA Ops:
  2.6 2.9 collective-permute-start
  5.6 2.5 prepare_rest.1
  8.0 3.8 %collective-permute-done.v1.p1 = bf16[224,800]{1,0:T(8,128)(2,1)} collective-permute-done((bf16[224,800]{1,0:T(8,128)(2,1)}, bf16[224,800]{1,0:T(8,128)(2,1)}, u32[]{:S(2)}, u32[]{:S(2)}) %collective-permute-start) | collective-permute-done | bytes 358432 | tf_op jit(solution)/shard_map/ppermute | solution.py:25
  15.0 6.3 %input_stats.1 = (f32[4,8,512]{2,1,0:T(8,128)}, f32[8,512]{1,0:T(8,128)}) custom-call(bf16[4,1600,512]{2,1,0:T(8,128)(2,1)} %bitcast.34), custom_call_target="tpu_custom_call" | custom-call | flops 655360000 | bytes 1 | tf_op jit(solution)/shard_map/input_stats/pallas_call | solution.py:412
  21.3 4.0 %collective-permute-done.1.v2.p2 = bf16[2,224,800]{2,1,0:T(8,128)(2,1)} collective-permute-done((bf16[2,224,800]{2,1,0:T(8,128)(2,1)S(1)}, bf16[2,224,800]{2,1,0:T(8,128)(2,1)}, u32[]{:S(2)}, u32[]{:S(2)}) %collective-permute-start.1) | collective-permute-done | bytes 716832 | tf_op jit(solution)/shard_map/ppermute | solution.py:25
  28.7 8.9 %first_act.1.a0_ref.a_ref = bf16[4,1600,512]{2,1,0:T(8,128)(2,1)} custom-call(bf16[4,1600,512]{2,1,0:T(8,128)(2,1)} %bitcast.35, f32[4,8,512]{2,1,0:T(8,128)} %get-tuple-element.111.st_ref.before_ref, bf16[224,800]{1,0:T(8,128)(2,1)} %prepare_in.1.v0, bf16[224,800]{1,0:T(8,128)(2,1)} %collective-permute-done.v1.p1, ...), custom_call_target="tpu_custom_call" | custom-call | flops 1310720000 | bytes 1 | tf_op jit(solution)/shard_map/first_act/pallas_call | solution.py:445
  44.0 17.7 %first_product.1 = (f32[4,800,512]{2,1,0:T(8,128)}, bf16[4,800,512]{2,1,0:T(8,128)(2,1)}, bf16[4,8,800]{2,1,0:T(8,128)(2,1)}, f32[8,512]{1,0:T(8,128)}, f32[4,8,512]{2,1,0:T(8,128)}, /*index=5*/bf16[1600,800]{1,0:T(8,128)(2,1)}) custom-call(bf16[4,1600,512]{2,1,0:T(8,128)(2,1)} %first_act.1.a0_ref.a_ref, bf16[400,800]{1,0:T(8,128)(2,1)} %p0.1, ...), custom_call_target="tpu_custom_call" | custom-call | flops 107479040000 | bytes 1 | tf_op jit(solution)/shard_map/first_product/pallas_call | solution.py:499
  61.7 3.2 %collective-permute-done.6.g = bf16[2,5,104,800]{3,2,1,0:T(8,128)(2,1)} collective-permute-done((bf16[2,5,104,800]{3,2,1,0:T(8,128)(2,1)S(1)}, bf16[2,5,104,800]{3,2,1,0:T(8,128)(2,1)}, u32[]{:S(2)}, u32[]{:S(2)}) %collective-permute-start.6) | collective-permute-done | bytes 1664032 | tf_op jit(solution)/shard_map/ppermute | solution.py:25
  67.5 2.3 collective-permute-done.7.of
  71.9 9.6 %assemble_weights.1 = (bf16[3,800,800]{2,1,0:T(8,128)(2,1)}, bf16[800,2400]{1,0:T(8,128)(2,1)}, bf16[2,800,800]{2,1,0:T(8,128)(2,1)}) custom-call(bf16[3,200,800]{2,1,0:T(8,128)(2,1)} %wc_own.1, bf16[200,1600]{1,0:T(8,128)(2,1)} %wo_own.1, bf16[5,104,800]{2,1,0:T(8,128)(2,1)} %copy-done.16, bf16[2,5,104,800]{3,2,1,0:T(8,128)(2,1)} %collective-permute-done.6.g, ...), custom_call_target="tpu_custom_call" | custom-call | flops 2048000000 | bytes 1 | tf_op jit(solution)/shard_map/assemble_weights/pallas_call | solution.py:545
  82.1 56.5 %conv_and_third_norm.1 = (bf16[4,800,512]{2,1,0:T(8,128)(2,1)}, bf16[4,800,512]{2,1,0:T(8,128)(2,1)}, bf16[4,8,800]{2,1,0:T(8,128)(2,1)}, f32[8,800]{1,0:T(8,128...) custom-call(bf16[4,800,512]{2,1,0:T(8,128)(2,1)} %get-tuple-element., ...), custom_call_target="tpu_custom_call" | custom-call | flops 526909440000 | bytes 1 | tf_op jit(solution)/shard_map/conv_and_third_norm/pallas_call | solution.py:727
  140.8 4.2 %transpose_out.1.wt_ref = bf16[1600,800]{1,0:T(8,128)(2,1)} custom-call(bf16[2,800,800]{2,1,0:T(8,128)(2,1)} %get-tuple-element.122.wo_ref.w_ref), custom_call_target="tpu_custom_call" | custom-call | tf_op jit(solution)/shard_map/transpose_out/pallas_call | solution.py:570
  145.0 6.7 %block_output.3 = (bf16[4,1600,512]{2,1,0:T(8,128)(2,1)}, f32[8,512]{1,0:T(8,128)}) custom-call(bf16[4,1600,512]{2,1,0:T(8,128)(2,1)} %bitcast.36, bf16[4,800,512]{2,1,0:T(8,128)(2,1)} %get-tuple-element.120.a2_ref, bf16[1600,800]{1,0:T(8,128)(2,1)} %transpose_out.1.wt_ref, bf16[224,800]{1,0:T(8,128)(2,1)} %prepare_in.1.v0, ...), custom_call_target="tpu_custom_call" | custom-call | flops 26378240000 | bytes 1 | tf_op jit(solution)/shard_map/block_output/pallas_call | solution.py:1062
  151.7 3.2 %add_convert_fusion = bf16[2,5,104,800]{3,2,1,0:T(8,128)(2,1)} fusion(bf16[4,5,104,800]{3,2,1,0:T(8,128)(2,1)} %collective-permute-done.9, bf16[4,5,104,800]{3,2,1,0:T(8,128)(2,1)S(1)} %copy-done.13), kind=kLoop, calls=%fused_computation | loop fusion | flops 3328000 | bytes 4992000 | tf_op jit(solution)/shard_map/convert_element_type | solution.py:86
  157.5 25.5 %conv_backward.1 = (bf16[4,800,512]{2,1,0:T(8,128)(2,1)}, f32[8,800]{1,0:T(8,128)}) custom-call(bf16[4,800,512]{2,1,0:T(8,128)(2,1)} %get-tuple-element.129.dh2_ref, bf16[4,8,800]{2,1,0:T(8,128)(2,1)} %copy-done.23, f32[4,800,512]{2,1,0:T(8,128)} %get-tuple-element.130.h1_ref, f32[4,8,512]{2,1,0:T(8,128)} %get-tuple-element.131.st_ref, ...), custom_call_target="tpu_custom_call" | custom-call | flops 159907840000 | bytes 1 | tf_op jit(solution)/shard_map/conv_backward/pallas_call | solution.py:924
  183.0 2.1 fusion
  186.7 11.3 %grad_weight_in.1 = (bf16[4,208,800]{2,1,0:T(8,128)(2,1)}, bf16[4,208,800]{2,1,0:T(8,128)(2,1)}) custom-call(bf16[4,1600,512]{2,1,0:T(8,128)(2,1)} %first_act.1.a0_ref.a_ref, bf16[4,800,512]{2,1,0:T(8,128)(2,1)} %get-tuple-element.137.b_ref.dh1_ref), custom_call_target="tpu_custom_call" | custom-call | flops 104857600000 | bytes 1 | tf_op jit(solution)/shard_map/grad_weight_in/pallas_call | solution.py:799
  198.7 2.2 bitcast_add_fusion
  201.8 2.4 collective-permute-start.15
  204.1 6.8 %block_output.4 = (bf16[4,1600,512]{2,1,0:T(8,128)(2,1)}, f32[8,512]{1,0:T(8,128)}) custom-call(bf16[4,1600,512]{2,1,0:T(8,128)(2,1)} %bitcast.37, bf16[4,800,512]{2,1,0:T(8,128)(2,1)} %get-tuple-element.120.a2_ref, bf16[1600,800]{1,0:T(8,128)(2,1)} %transpose_out.1.wt_ref, bf16[224,800]{1,0:T(8,128)(2,1)} %prepare_in.1.v0, ...), custom_call_target="tpu_custom_call", output_to_operand_aliasing={{0}: (6, {})} | custom-call | flops 26378240000 | bytes 1 | tf_op jit(solution)/shard_map/block_output/pallas_call | solution.py:1062
  211.0 2.2 add_convert_fusion.2
  213.5 9.4 %grad_stream.3 = (bf16[4,1600,512]{2,1,0:T(8,128)(2,1)}, f32[8,1600]{1,0:T(8,128)}) custom-call(bf16[4,1600,512]{2,1,0:T(8,128)(2,1)} %bitcast.38, f32[4,8,512]{2,1,0:T(8,128)} %get-tuple-element.111.st_ref.before_ref, bf16[4,1600,512]{2,1,0:T(8,128)(2,1)} %bitcast.47, bf16[4,800,512]{2,1,0:T(8,128)(2,1)} %get-tuple-element.137.b_ref.dh1_ref, ...), custom_call_target="tpu_custom_call" | custom-call | flops 26869760000 | bytes 1 | tf_op jit(solution)/shard_map/grad_stream/pallas_call | solution.py:1007
  223.1 2.9 collective-permute-start.17
  228.8 9.7 %block_output.5 = (bf16[4,1600,512]{2,1,0:T(8,128)(2,1)}, f32[8,512]{1,0:T(8,128)}) custom-call(bf16[4,1600,512]{2,1,0:T(8,128)(2,1)} %bitcast.39, bf16[4,800,512]{2,1,0:T(8,128)(2,1)} %get-tuple-element.120.a2_ref, bf16[1600,800]{1,0:T(8,128)(2,1)} %transpose_out.1.wt_ref, bf16[224,800]{1,0:T(8,128)(2,1)} %prepare_in.1.v0, ...), custom_call_target="tpu_custom_call", output_to_operand_aliasing={{0}: (6, {})} | custom-call | flops 52756480000 | bytes 1 | tf_op jit(solution)/shard_map/block_output/pallas_call | solution.py:1062
  242.8 9.4 %grad_stream.4 = (bf16[4,1600,512]{2,1,0:T(8,128)(2,1)}, f32[8,1600]{1,0:T(8,128)}) custom-call(bf16[4,1600,512]{2,1,0:T(8,128)(2,1)} %bitcast.40, f32[4,8,512]{2,1,0:T(8,128)} %get-tuple-element.111.st_ref.before_ref, bf16[4,1600,512]{2,1,0:T(8,128)(2,1)} %bitcast.48, ...), custom_call_target="tpu_custom_call", output_to_operand_aliasing={{0}: (8, {})} | custom-call | flops 26869760000 | bytes 1 | tf_op jit(solution)/shard_map/grad_stream/pallas_call | solution.py:1007
  253.3 3.7 %collective-permute-done.18 = bf16[208,800]{1,0:T(8,128)(2,1)S(1)} collective-permute-done((bf16[208,800]{1,0:T(8,128)(2,1)S(1)}, bf16[208,800]{1,0:T(8,128)(2,1)S(1)}, u32[]{:S(2)}, u32[]{:S(2)}) %collective-permute-start.18) | collective-permute-done | bytes 332832 | tf_op jit(solution)/shard_map/ppermute | solution.py:29
  257.4 15.6 %grad_stream.5 = (bf16[4,1600,512]{2,1,0:T(8,128)(2,1)}, f32[8,1600]{1,0:T(8,128)}) custom-call(bf16[4,1600,512]{2,1,0:T(8,128)(2,1)} %bitcast.41, f32[4,8,512]{2,1,0:T(8,128)} %get-tuple-element.111.st_ref.before_ref, bf16[4,1600,512]{2,1,0:T(8,128)(2,1)} %bitcast.49, ...), custom_call_target="tpu_custom_call", output_to_operand_aliasing={{0}: (8, {})} | custom-call | flops 53739520000 | bytes 1 | tf_op jit(solution)/shard_map/grad_stream/pallas_call | solution.py:1007
  273.0 2.2 collective-permute-done.23
  276.6 2.7 collective-permute-done.21
  283.6 2.5 join_grads.1
  287.2 2.5 collective-permute-start.29
  292.8 2.8 collective-permute-done.30
  (128 shorter events, 47.9 us)
Async XLA Ops:
  2.6 9.2 %collective-permute-start = (bf16[224,800]{1,0:T(8,128)(2,1)}, bf16[224,800]{1,0:T(8,128)(2,1)}, u32[]{:S(2)}, u32[]{:S(2)}) collective-permute-start(bf16[224,800]{1,0:T(8,128)(2,1)} %prepare_in.1.v0), channel_id=1, source_target_pairs={{0,8},{1,17},{2,10},{3,19},{4,12},{5,21},{6,14},{7,23},{8,0},{9,25... | collective-permute-start | bytes 1075208 | tf_op jit(solution)/shard_map/ppermute | solution.py:25
  12.9 12.3 %collective-permute-start.1 = (bf16[2,224,800]{2,1,0:T(8,128)(2,1)S(1)}, bf16[2,224,800]{2,1,0:T(8,128)(2,1)}, u32[]{:S(2)}, u32[]{:S(2)}) collective-permute-start(bf16[2,224,800]{2,1,0:T(8,128)(2,1)S(1)} %pad_maximum_fusion.2), channel_id=1, source_target_pairs={{0,16},{1,9},{2,18},{3,11},{4,20},{5,13},{6,22},{7,15},{8,24},{9,1... | collective-permute-start | bytes 2150408 | tf_op jit(solution)/shard_map/ppermute | solution.py:25
  25.3 13.5 %collective-permute-start.4 = (bf16[5,104,800]{2,1,0:T(8,128)(2,1)S(1)}, bf16[5,104,800]{2,1,0:T(8,128)(2,1)S(1)}, u32[]{:S(2)}, u32[]{:S(2)}) collective-permute-start(bf16[5,104,800]{2,1,0:T(8,128)(2,1)S(1)} %copy-done.12), channel_id=1, source_target_pairs={{0,8},{1,17},{2,10},{3,19},{4,12},{5,21},{6,14},{7,23},{8,0},{9,25... | collective-permute-start | bytes 2496008 | tf_op jit(solution)/shard_map/ppermute | solution.py:25
  27.2 16.0 %collective-permute-start.3 = (bf16[2,224,800]{2,1,0:T(8,128)(2,1)}, bf16[2,224,800]{2,1,0:T(8,128)(2,1)}, u32[]{:S(2)}, u32[]{:S(2)}) collective-permute-start(bf16[2,224,800]{2,1,0:T(8,128)(2,1)} %collective-permute-done.1.v2.p2), channel_id=1, source_target_pairs={{0,1},{1,0},{2,3},{3,2},{4,5},{5,4},{6,7},{7,6},{8,9},{9,8},{10,11... | collective-permute-start | bytes 2150408 | tf_op jit(solution)/shard_map/ppermute | solution.py:29
  27.2 16.0 %collective-permute-start.2 = (bf16[224,800]{1,0:T(8,128)(2,1)}, bf16[224,800]{1,0:T(8,128)(2,1)S(1)}, u32[]{:S(2)}, u32[]{:S(2)}) collective-permute-start(bf16[224,800]{1,0:T(8,128)(2,1)} %collective-permute-done.v1.p1), channel_id=1, source_target_pairs={{0,1},{1,0},{2,3},{3,2},{4,5},{5,4},{6,7},{7,6},{8,9},{9,8},{10,11... | collective-permute-start | bytes 1075208 | tf_op jit(solution)/shard_map/ppermute | solution.py:29
  41.2 23.7 %copy-start.17 = (bf16[5,104,800]{2,1,0:T(8,128)(2,1)S(1)}, bf16[5,104,800]{2,1,0:T(8,128)(2,1)}, u32[]{:S(2)}) copy-start(bf16[5,104,800]{2,1,0:T(8,128)(2,1)} %copy-done.16) | copy-start | bytes 2496004
  41.2 23.7 %collective-permute-start.6 = (bf16[2,5,104,800]{3,2,1,0:T(8,128)(2,1)S(1)}, bf16[2,5,104,800]{3,2,1,0:T(8,128)(2,1)}, u32[]{:S(2)}, u32[]{:S(2)}) collective-permute-start(bf16[2,5,104,800]{3,2,1,0:T(8,128)(2,1)S(1)} %pad_maximum_fusion), channel_id=1, source_target_pairs={{0,16},{1,9},{2,18},{3,11},{4,20},{5,13},{6,22},{7,15},{8,24},{9,1... | collective-permute-start | bytes 4992008 | tf_op jit(solution)/shard_map/ppermute | solution.py:25
  64.9 5.4 %collective-permute-start.8 = (bf16[2,5,104,800]{3,2,1,0:T(8,128)(2,1)}, bf16[2,5,104,800]{3,2,1,0:T(8,128)(2,1)S(1)}, u32[]{:S(2)}, u32[]{:S(2)}) collective-permute-start(bf16[2,5,104,800]{3,2,1,0:T(8,128)(2,1)} %collective-permute-done.6.g), channel_id=1, source_target_pairs={{0,1},{1,0},{2,3},{3,2},{4,5},{5,4},{6,7},{7,6},{8,9},{9,8},{10,11... | collective-permute-start | bytes 4992008 | tf_op jit(solution)/shard_map/ppermute | solution.py:29
  64.9 4.9 %collective-permute-start.7 = (bf16[5,104,800]{2,1,0:T(8,128)(2,1)S(1)}, bf16[5,104,800]{2,1,0:T(8,128)(2,1)S(1)}, u32[]{:S(2)}, u32[]{:S(2)}) collective-permute-start(bf16[5,104,800]{2,1,0:T(8,128)(2,1)S(1)} %copy-done.17), channel_id=1, source_target_pairs={{0,1},{1,0},{2,3},{3,2},{4,5},{5,4},{6,7},{7,6},{8,9},{9,8},{10,11... | collective-permute-start | bytes 2496008 | tf_op jit(solution)/shard_map/ppermute | solution.py:29
  65.4 16.1 %collective-permute-start.5 = (bf16[4,8,800]{2,1,0:T(8,128)(2,1)}, bf16[4,8,800]{2,1,0:T(8,128)(2,1)S(1)}, u32[]{:S(2)}, u32[]{:S(2)}) collective-permute-start(bf16[4,8,800]{2,1,0:T(8,128)(2,1)} %get-tuple-element.115), channel_id=1, source_target_pairs={{0,1},{1,2},{2,3},{3,4},{4,5},{5,6},{6,7},{8,9},{9,10},{10,11},{11... | collective-permute-start | bytes 153608 | tf_op jit(solution)/shard_map/ppermute | solution.py:34
  138.7 13.0 %collective-permute-start.9 = (bf16[4,5,104,800]{3,2,1,0:T(8,128)(2,1)}, bf16[4,5,104,800]{3,2,1,0:T(8,128)(2,1)}, u32[]{:S(2)}, u32[]{:S(2)}) collective-permute-start(bf16[4,5,104,800]{3,2,1,0:T(8,128)(2,1)} %get-tuple-element.123), channel_id=1, source_target_pairs={{0,1},{1,0},{2,3},{3,2},{4,5},{5,4},{6,7},{7,6},{8,9},{9,8},{10,11... | collective-permute-start | bytes 9984008 | tf_op jit(solution)/shard_map/ppermute | solution.py:29
  139.1 17.8 %collective-permute-start.11 = (bf16[4,8,800]{2,1,0:T(8,128)(2,1)}, bf16[4,8,800]{2,1,0:T(8,128)(2,1)S(1)}, u32[]{:S(2)}, u32[]{:S(2)}) collective-permute-start(bf16[4,8,800]{2,1,0:T(8,128)(2,1)} %get-tuple-element.121), channel_id=1, source_target_pairs={{1,0},{2,1},{3,2},{4,3},{5,4},{6,5},{7,6},{9,8},{10,9},{11,10},{12... | collective-permute-start | bytes 153608 | tf_op jit(solution)/shard_map/ppermute | solution.py:34
  154.9 28.1 %collective-permute-start.10 = (bf16[2,5,104,800]{3,2,1,0:T(8,128)(2,1)}, bf16[2,5,104,800]{3,2,1,0:T(8,128)(2,1)}, u32[]{:S(2)}, u32[]{:S(2)}) collective-permute-start(bf16[2,5,104,800]{3,2,1,0:T(8,128)(2,1)} %add_convert_fusion), channel_id=1, source_target_pairs={{0,8},{1,17},{2,10},{3,19},{4,12},{5,21},{6,14},{7,23},{8,0},{9,25... | collective-permute-start | bytes 4992008 | tf_op jit(solution)/shard_map/ppermute | solution.py:25
  185.1 13.6 %collective-permute-start.12 = (bf16[5,104,800]{2,1,0:T(8,128)(2,1)S(1)}, bf16[5,104,800]{2,1,0:T(8,128)(2,1)S(1)}, u32[]{:S(2)}, u32[]{:S(2)}) collective-permute-start(bf16[5,104,800]{2,1,0:T(8,128)(2,1)S(1)} %fusion), channel_id=1, source_target_pairs={{0,16},{1,9},{2,18},{3,11},{4,20},{5,13},{6,22},{7,15},{8,24},{9,1... | collective-permute-start | bytes 2496008 | tf_op jit(solution)/shard_map/ppermute | solution.py:25
  198.0 12.9 %collective-permute-start.13 = (bf16[4,208,800]{2,1,0:T(8,128)(2,1)}, bf16[4,208,800]{2,1,0:T(8,128)(2,1)}, u32[]{:S(2)}, u32[]{:S(2)}) collective-permute-start(bf16[4,208,800]{2,1,0:T(8,128)(2,1)} %get-tuple-element.138), channel_id=1, source_target_pairs={{0,1},{1,0},{2,3},{3,2},{4,5},{5,4},{6,7},{7,6},{8,9},{9,8},{10,11... | collective-permute-start | bytes 3993608 | tf_op jit(solution)/shard_map/ppermute | solution.py:29
  201.8 21.2 %collective-permute-start.15 = (bf16[5,56,800]{2,1,0:T(8,128)(2,1)}, bf16[5,56,800]{2,1,0:T(8,128)(2,1)S(1)}, u32[]{:S(2)}, u32[]{:S(2)}) collective-permute-start(bf16[5,56,800]{2,1,0:T(8,128)(2,1)} %dynamic-slice_convert_fusion), channel_id=1, source_target_pairs={{0,2},{1,3},{2,0},{3,1},{4,6},{5,7},{6,4},{7,5},{8,10},{9,11},{10,... | collective-permute-start | bytes 1344008 | tf_op jit(solution)/shard_map/ppermute | solution.py:29
  213.2 12.8 %collective-permute-start.14 = (bf16[2,208,800]{2,1,0:T(8,128)(2,1)}, bf16[2,208,800]{2,1,0:T(8,128)(2,1)S(1)}, u32[]{:S(2)}, u32[]{:S(2)}) collective-permute-start(bf16[2,208,800]{2,1,0:T(8,128)(2,1)} %add_convert_fusion.2), channel_id=1, source_target_pairs={{0,8},{1,17},{2,10},{3,19},{4,12},{5,21},{6,14},{7,23},{8,0},{9,25... | collective-permute-start | bytes 1996808 | tf_op jit(solution)/shard_map/ppermute | solution.py:25
  223.1 15.4 %collective-permute-start.17 = (bf16[5,32,800]{2,1,0:T(8,128)(2,1)S(1)}, bf16[5,32,800]{2,1,0:T(8,128)(2,1)S(1)}, u32[]{:S(2)}, u32[]{:S(2)}) collective-permute-start(bf16[5,32,800]{2,1,0:T(8,128)(2,1)S(1)} %dynamic-slice_convert_fusion.1), channel_id=1, source_target_pairs={{0,4},{1,5},{2,6},{3,7},{4,0},{5,1},{6,2},{7,3},{8,12},{9,13},{10,... | collective-permute-start | bytes 768008 | tf_op jit(solution)/shard_map/ppermute | solution.py:29
  227.2 13.0 %collective-permute-start.16 = (bf16[208,800]{1,0:T(8,128)(2,1)S(1)}, bf16[208,800]{1,0:T(8,128)(2,1)S(1)}, u32[]{:S(2)}, u32[]{:S(2)}) collective-permute-start(bf16[208,800]{1,0:T(8,128)(2,1)S(1)} %fusion.4), channel_id=1, source_target_pairs={{0,16},{1,9},{2,18},{3,11},{4,20},{5,13},{6,22},{7,15},{8,24},{9,1... | collective-permute-start | bytes 998408 | tf_op jit(solution)/shard_map/ppermute | solution.py:25
  238.6 14.5 %collective-permute-start.19 = (bf16[5,32,800]{2,1,0:T(8,128)(2,1)S(1)}, bf16[5,32,800]{2,1,0:T(8,128)(2,1)S(1)}, u32[]{:S(2)}, u32[]{:S(2)}) collective-permute-start(bf16[5,32,800]{2,1,0:T(8,128)(2,1)S(1)} %add_convert_fusion.5), channel_id=1, source_target_pairs={{0,4},{1,5},{2,6},{3,7},{4,0},{5,1},{6,2},{7,3},{8,12},{9,13},{10,... | collective-permute-start | bytes 768008 | tf_op jit(solution)/shard_map/ppermute | solution.py:29
  241.5 15.4 %collective-permute-start.18 = (bf16[208,800]{1,0:T(8,128)(2,1)S(1)}, bf16[208,800]{1,0:T(8,128)(2,1)S(1)}, u32[]{:S(2)}, u32[]{:S(2)}) collective-permute-start(bf16[208,800]{1,0:T(8,128)(2,1)S(1)} %fusion.1), channel_id=1, source_target_pairs={{0,2},{1,3},{2,0},{3,1},{4,6},{5,7},{6,4},{7,5},{8,10},{9,11},{10,... | collective-permute-start | bytes 998408 | tf_op jit(solution)/shard_map/ppermute | solution.py:29
  253.2 21.9 %collective-permute-start.23 = (bf16[5,56,800]{2,1,0:T(8,128)(2,1)S(1)}, bf16[5,56,800]{2,1,0:T(8,128)(2,1)S(1)}, u32[]{:S(2)}, u32[]{:S(2)}) collective-permute-start(bf16[5,56,800]{2,1,0:T(8,128)(2,1)S(1)} %pad_maximum_fusion.3), channel_id=1, source_target_pairs={{0,2},{1,3},{2,0},{3,1},{4,6},{5,7},{6,4},{7,5},{8,10},{9,11},{10,... | collective-permute-start | bytes 1344008 | tf_op jit(solution)/shard_map/ppermute | solution.py:29
  257.0 18.7 %collective-permute-start.20 = (bf16[208,800]{1,0:T(8,128)(2,1)S(1)}, bf16[208,800]{1,0:T(8,128)(2,1)S(1)}, u32[]{:S(2)}, u32[]{:S(2)}) collective-permute-start(bf16[208,800]{1,0:T(8,128)(2,1)S(1)} %add_convert_fusion.3), channel_id=1, source_target_pairs={{0,4},{1,5},{2,6},{3,7},{4,0},{5,1},{6,2},{7,3},{8,12},{9,13},{10,... | collective-permute-start | bytes 998408 | tf_op jit(solution)/shard_map/ppermute | solution.py:29
  275.6 7.9 %collective-permute-start.24 = (bf16[5,104,800]{2,1,0:T(8,128)(2,1)S(1)}, bf16[5,104,800]{2,1,0:T(8,128)(2,1)S(1)}, u32[]{:S(2)}, u32[]{:S(2)}) collective-permute-start(bf16[5,104,800]{2,1,0:T(8,128)(2,1)S(1)} %pad_maximum_fusion.1.mine_ref), channel_id=1, source_target_pairs={{0,1},{1,0},{2,3},{3,2},{4,5},{5,4},{6,7},{7,6},{8,9},{9,8},{10,11... | collective-permute-start | bytes 2496008 | tf_op jit(solution)/shard_map/ppermute | solution.py:29
  275.8 7.8 %collective-permute-start.25 = (f32[208,800]{1,0:T(8,128)S(1)}, f32[208,800]{1,0:T(8,128)S(1)}, u32[]{:S(2)}, u32[]{:S(2)}) collective-permute-start(f32[208,800]{1,0:T(8,128)S(1)} %convert_add_fusion.1.mine_in), channel_id=1, source_target_pairs={{0,1},{1,0},{2,3},{3,2},{4,5},{5,4},{6,7},{7,6},{8,9},{9,8},{10,11... | collective-permute-start | bytes 1996808 | tf_op jit(solution)/shard_map/ppermute | solution.py:29
  276.5 2.8 collective-permute-start.21
  279.3 4.2 %collective-permute-start.22 = (f32[8,1600]{1,0:T(8,128)S(1)}, f32[8,1600]{1,0:T(8,128)S(1)}, u32[]{:S(2)}, u32[]{:S(2)}) collective-permute-start(f32[8,1600]{1,0:T(8,128)S(1)} %add.132), channel_id=1, source_target_pairs={{0,8},{8,0},{16,24},{24,16},{1,9},{9,1},{17,25},{25,17},{2,10},{10... | collective-permute-start | bytes 153608 | tf_op jit(solution)/shard_map/ppermute | solution.py:29
  280.4 5.6 %collective-permute-start.26 = (f32[8,1600]{1,0:T(8,128)S(1)}, f32[8,1600]{1,0:T(8,128)S(1)}, u32[]{:S(2)}, u32[]{:S(2)}) collective-permute-start(f32[8,1600]{1,0:T(8,128)S(1)} %add.132), channel_id=1, source_target_pairs={{0,16},{8,24},{16,0},{24,8},{1,17},{9,25},{17,1},{25,9},{2,18},{10... | collective-permute-start | bytes 153608 | tf_op jit(solution)/shard_map/ppermute | solution.py:29
  281.8 5.0 %collective-permute-start.27 = (f32[8,1600]{1,0:T(8,128)S(1)}, f32[8,1600]{1,0:T(8,128)S(1)}, u32[]{:S(2)}, u32[]{:S(2)}) collective-permute-start(f32[8,1600]{1,0:T(8,128)S(1)} %add.132), channel_id=1, source_target_pairs={{0,24},{8,16},{16,8},{24,0},{1,25},{9,17},{17,9},{25,1},{2,26},{10... | collective-permute-start | bytes 153608 | tf_op jit(solution)/shard_map/ppermute | solution.py:29
  286.8 4.5 %collective-permute-start.28 = (f32[8,1600]{1,0:T(8,128)S(1)}, f32[8,1600]{1,0:T(8,128)S(1)}, u32[]{:S(2)}, u32[]{:S(2)}) collective-permute-start(f32[8,1600]{1,0:T(8,128)S(1)} %add_add_fusion.1), channel_id=1, source_target_pairs={{0,2},{1,3},{2,0},{3,1},{4,6},{5,7},{6,4},{7,5},{8,10},{9,11},{10,... | collective-permute-start | bytes 153608 | tf_op jit(solution)/shard_map/ppermute | solution.py:29
  287.2 5.6 %collective-permute-start.29 = (f32[8,1600]{1,0:T(8,128)S(1)}, f32[8,1600]{1,0:T(8,128)S(1)}, u32[]{:S(2)}, u32[]{:S(2)}) collective-permute-start(f32[8,1600]{1,0:T(8,128)S(1)} %add_add_fusion.1), channel_id=1, source_target_pairs={{0,4},{1,5},{2,6},{3,7},{4,0},{5,1},{6,2},{7,3},{8,12},{9,13},{10,... | collective-permute-start | bytes 153608 | tf_op jit(solution)/shard_map/ppermute | solution.py:29
  289.7 5.9 %collective-permute-start.30 = (f32[8,1600]{1,0:T(8,128)S(1)}, f32[8,1600]{1,0:T(8,128)S(1)}, u32[]{:S(2)}, u32[]{:S(2)}) collective-permute-start(f32[8,1600]{1,0:T(8,128)S(1)} %add_add_fusion.1), channel_id=1, source_target_pairs={{0,6},{1,7},{2,4},{3,5},{4,2},{5,3},{6,0},{7,1},{8,14},{9,15},{10,... | collective-permute-start | bytes 153608 | tf_op jit(solution)/shard_map/ppermute | solution.py:29
  (23 other events, 61.8 us)

commit v2 on v1

--- a/solution.py
+++ b/solution.py
@@ -224,14 +224,14 @@
         return a + eight(load(i))
 
     zero = jnp.zeros((8, length), F32)
-    a = lax.fori_loop(0, count, total, zero, unroll=5)
+    a = lax.fori_loop(0, count, total, zero, unroll=10)
     mean = jnp.sum(a, axis=0, keepdims=True) * (1.0 / width)
 
     def squares(i, a):
         c = load(i) - mean
         return a + eight(c * c)
 
-    a = lax.fori_loop(0, count, squares, zero, unroll=5)
+    a = lax.fori_loop(0, count, squares, zero, unroll=10)
     var = jnp.sum(a, axis=0, keepdims=True) * (1.0 / width)
     return mean, var
 
@@ -437,7 +437,7 @@
         y = (x_ref[r, :].astype(F32) - mean) * inv * col(vw_s, 0, r, length)
         a0_ref[r, :] = silu_of_half(y + col(vw_s, 1, r, length)).astype(BF)
 
-    loop(wide // ROWS, act0, 5)
+    loop(wide // ROWS, act0, 10)
 
 
 def first_act(x, stats, packs):
@@ -485,7 +485,7 @@
         y = (h1_ref[r, :] - mean1) * inv1 * col(vi_s, 1, r, length) + col(vi_s, 2, r, length)
         a1_ref[r, :] = silu_of_half(y).astype(BF)
 
-    loop(inner // ROWS, act1, 5)
+    loop(inner // ROWS, act1, 10)
     edge_ref[...] = a1_ref[:, length - 128 :].astype(F32).T[120:128, :].astype(BF)
 
     @pl.when(s == pl.num_programs(0) - 1)
@@ -615,7 +615,7 @@
             st_s[now, rows_at(i, inner), :] = (pltpu.roll(v, 2, 1)[:, 0:length] * m1).astype(BF)
             st_s[now, rows_at(i, 2 * inner), :] = (pltpu.roll(v, 4, 1)[:, 0:length] * m2).astype(BF)
 
-        loop(steps, build, 10)
+        loop(steps, build, 25)
         h_s[...] = mm(wct_ref[...], st_s[now]) + lanes(vi_s[0], length)
         d_s[...] = mm(wo_ref[0], dy_ref[0:inner, :]) + mm(wo_ref[1], dy_ref[inner:, :])
 
@@ -672,7 +672,7 @@
 
     @pl.when(s == 0)
     def _():
-        acc = lax.fori_loop(0, steps, back, (zero, zero), unroll=5)
+        acc = lax.fori_loop(0, steps, back, (zero, zero), unroll=10)
         mq, mqn = means(acc)
         loop(steps, lambda i: last(i, mq, mqn), 5)
 
@@ -825,7 +825,7 @@
         t_s[1, r, :] = (pltpu.roll(v, length + 126, 1)[:, 0:length] * f1).astype(BF)
         t_s[2, r, :] = (pltpu.roll(v, length + 124, 1)[:, 0:length] * f2).astype(BF)
 
-    loop(inner // ROWS, build, 10)
+    loop(inner // ROWS, build, 25)
 
 
 def conv_back_body(
@@ -875,7 +875,7 @@
             dh1_ref[r, :] = dh
             sums_s[2, r, :] += fold(dh.astype(F32))
 
-        loop(steps, last, 5)
+        loop(steps, last, 10)
 
     def stats():
         return st_ref[0:1, :], st_ref[1:2, :]
@@ -983,7 +983,7 @@
         return acc[0] + eight(q), acc[1] + eight(q * n)
 
     zero = jnp.zeros((8, length), F32)
-    qa, qn = lax.fori_loop(0, steps, back, (zero, zero), unroll=5)
+    qa, qn = lax.fori_loop(0, steps, back, (zero, zero), unroll=10)
     mq = jnp.sum(qa, axis=0, keepdims=True) * (1.0 / wide)
     mqn = jnp.sum(qn, axis=0, keepdims=True) * (1.0 / wide)
 
@@ -992,7 +992,7 @@
         gs = dy_ref[r, :].astype(F32) + (d_s[r, :] - mq - n_s[r, :] * mqn) * inv
         gs_ref[r, :] = gs.astype(BF)
 
-    loop(steps, last, 5)
+    loop(steps, last, 10)
 
     @pl.when(s == pl.num_programs(0) - 1)
     def _():
@@ -1050,7 +1050,7 @@
         return acc[0] + eight(branch * branch), acc[1] + eight(result * result)
 
     zero = jnp.zeros((8, length), F32)
-    b2, r2 = lax.fori_loop(0, wide // ROWS, close, (zero, zero), unroll=5)
+    b2, r2 = lax.fori_loop(0, wide // ROWS, close, (zero, zero), unroll=10)
     sq_ref[0:1, :] += jnp.sum(b2, axis=0, keepdims=True)
     sq_ref[1:2, :] += jnp.sum(r2, axis=0, keepdims=True)
 

time: 301 us -> 299 us (level)
  Pallas kernels: 206 us -> 202 us
where the time goes in v2:
time: 299 us; the launch traced here: 295 us
  Pallas kernels  202 us (68%)
  starting transfers between devices  37.6 us (13%)
  waiting for transfers between devices  31.7 us (11%)
  other arithmetic  15.7 us (5%)
  local copies, waits for them, and re-layouts  6.32 us (2%)
    pallas_call x1, Pallas kernels, conv(): pl.pallas_call(conv_body, grid=(seqs + 1,), in_specs=[this((inner, length...  55.4 us
    pallas_call x3, Pallas kernels, stream_back(): pl.pallas_call(stream_body, grid=(count,), in_specs=[seq_from(begin, (wid...  34 us
    pallas_call x1, Pallas kernels, conv_back(): pl.pallas_call(conv_back_body, grid=(seqs + 1,), in_specs=[this_seq(seqs,...  24.8 us
    pallas_call x3, Pallas kernels, output_of(): pl.pallas_call(output_body, grid=(count,), in_specs=[seq_from(begin, (wid...  23.1 us
    ppermute x21, starting transfers between devices, swap(): lax.ppermute(value, axis, [(i, i ^ mask) for i in range(lax.axis_size(axi...  19.3 us
    ppermute x21, waiting for transfers between devices, swap(): lax.ppermute(value, axis, [(i, i ^ mask) for i in range(lax.axis_size(axi...  18.3 us
    pallas_call x1, Pallas kernels, first(): pl.pallas_call(first_body, grid=(seqs,), in_specs=[seq((wide, length))] +...  17.3 us
    ppermute x8, starting transfers between devices, by_core(): return lax.ppermute(value, ('dp', 'ctx'), pairs)  14.5 us
  transfers between devices with their start and end apart: 31, of which 15 were waited for; matrix products, arithmetic and copies ran while one was open for 5% of the time, Pallas kernels for 49%

profile of v2, /device:TPU:0, one launch (start us, length us, event | category | flops | bytes accessed | tf_op | source)
XLA Modules:
  0.0 294.7 jit_solution(2502645151901862091)
XLA Ops:
  2.6 2.9 collective-permute-start
  5.6 2.5 prepare_rest.1
  8.0 3.8 %collective-permute-done.v1.p1 = bf16[224,800]{1,0:T(8,128)(2,1)} collective-permute-done((bf16[224,800]{1,0:T(8,128)(2,1)}, bf16[224,800]{1,0:T(8,128)(2,1)}, u32[]{:S(2)}, u32[]{:S(2)}) %collective-permute-start) | collective-permute-done | bytes 358432 | tf_op jit(solution)/shard_map/ppermute | solution.py:25
  15.0 6.0 %input_stats.1 = (f32[4,8,512]{2,1,0:T(8,128)}, f32[8,512]{1,0:T(8,128)}) custom-call(bf16[4,1600,512]{2,1,0:T(8,128)(2,1)} %bitcast.34), custom_call_target="tpu_custom_call" | custom-call | flops 655360000 | bytes 1 | tf_op jit(solution)/shard_map/input_stats/pallas_call | solution.py:412
  20.9 4.3 %collective-permute-done.1.v2.p2 = bf16[2,224,800]{2,1,0:T(8,128)(2,1)} collective-permute-done((bf16[2,224,800]{2,1,0:T(8,128)(2,1)S(1)}, bf16[2,224,800]{2,1,0:T(8,128)(2,1)}, u32[]{:S(2)}, u32[]{:S(2)}) %collective-permute-start.1) | collective-permute-done | bytes 716832 | tf_op jit(solution)/shard_map/ppermute | solution.py:25
  28.7 8.5 %first_act.1.a0_ref.a_ref = bf16[4,1600,512]{2,1,0:T(8,128)(2,1)} custom-call(bf16[4,1600,512]{2,1,0:T(8,128)(2,1)} %bitcast.35, f32[4,8,512]{2,1,0:T(8,128)} %get-tuple-element.111.st_ref.before_ref, bf16[224,800]{1,0:T(8,128)(2,1)} %prepare_in.1.v0, bf16[224,800]{1,0:T(8,128)(2,1)} %collective-permute-done.v1.p1, ...), custom_call_target="tpu_custom_call" | custom-call | flops 1310720000 | bytes 1 | tf_op jit(solution)/shard_map/first_act/pallas_call | solution.py:445
  44.0 17.3 %first_product.1 = (f32[4,800,512]{2,1,0:T(8,128)}, bf16[4,800,512]{2,1,0:T(8,128)(2,1)}, bf16[4,8,800]{2,1,0:T(8,128)(2,1)}, f32[8,512]{1,0:T(8,128)}, f32[4,8,512]{2,1,0:T(8,128)}, /*index=5*/bf16[1600,800]{1,0:T(8,128)(2,1)}) custom-call(bf16[4,1600,512]{2,1,0:T(8,128)(2,1)} %first_act.1.a0_ref.a_ref, bf16[400,800]{1,0:T(8,128)(2,1)} %p0.1, ...), custom_call_target="tpu_custom_call" | custom-call | flops 107479040000 | bytes 1 | tf_op jit(solution)/shard_map/first_product/pallas_call | solution.py:499
  61.3 3.6 %collective-permute-done.6.g = bf16[2,5,104,800]{3,2,1,0:T(8,128)(2,1)} collective-permute-done((bf16[2,5,104,800]{3,2,1,0:T(8,128)(2,1)S(1)}, bf16[2,5,104,800]{3,2,1,0:T(8,128)(2,1)}, u32[]{:S(2)}, u32[]{:S(2)}) %collective-permute-start.6) | collective-permute-done | bytes 1664032 | tf_op jit(solution)/shard_map/ppermute | solution.py:25
  67.5 2.3 collective-permute-done.7.of
  71.9 9.6 %assemble_weights.1 = (bf16[3,800,800]{2,1,0:T(8,128)(2,1)}, bf16[800,2400]{1,0:T(8,128)(2,1)}, bf16[2,800,800]{2,1,0:T(8,128)(2,1)}) custom-call(bf16[3,200,800]{2,1,0:T(8,128)(2,1)} %wc_own.1, bf16[200,1600]{1,0:T(8,128)(2,1)} %wo_own.1, bf16[5,104,800]{2,1,0:T(8,128)(2,1)} %copy-done.16, bf16[2,5,104,800]{3,2,1,0:T(8,128)(2,1)} %collective-permute-done.6.g, ...), custom_call_target="tpu_custom_call" | custom-call | flops 2048000000 | bytes 1 | tf_op jit(solution)/shard_map/assemble_weights/pallas_call | solution.py:545
  82.1 55.4 %conv_and_third_norm.1 = (bf16[4,800,512]{2,1,0:T(8,128)(2,1)}, bf16[4,800,512]{2,1,0:T(8,128)(2,1)}, bf16[4,8,800]{2,1,0:T(8,128)(2,1)}, f32[8,800]{1,0:T(8,128...) custom-call(bf16[4,800,512]{2,1,0:T(8,128)(2,1)} %get-tuple-element., ...), custom_call_target="tpu_custom_call" | custom-call | flops 526909440000 | bytes 1 | tf_op jit(solution)/shard_map/conv_and_third_norm/pallas_call | solution.py:727
  139.6 4.2 %transpose_out.1.wt_ref = bf16[1600,800]{1,0:T(8,128)(2,1)} custom-call(bf16[2,800,800]{2,1,0:T(8,128)(2,1)} %get-tuple-element.122.wo_ref.w_ref), custom_call_target="tpu_custom_call" | custom-call | tf_op jit(solution)/shard_map/transpose_out/pallas_call | solution.py:570
  143.9 6.7 %block_output.3 = (bf16[4,1600,512]{2,1,0:T(8,128)(2,1)}, f32[8,512]{1,0:T(8,128)}) custom-call(bf16[4,1600,512]{2,1,0:T(8,128)(2,1)} %bitcast.36, bf16[4,800,512]{2,1,0:T(8,128)(2,1)} %get-tuple-element.120.a2_ref, bf16[1600,800]{1,0:T(8,128)(2,1)} %transpose_out.1.wt_ref, bf16[224,800]{1,0:T(8,128)(2,1)} %prepare_in.1.v0, ...), custom_call_target="tpu_custom_call" | custom-call | flops 26378240000 | bytes 1 | tf_op jit(solution)/shard_map/block_output/pallas_call | solution.py:1062
  150.5 3.2 %add_convert_fusion = bf16[2,5,104,800]{3,2,1,0:T(8,128)(2,1)} fusion(bf16[4,5,104,800]{3,2,1,0:T(8,128)(2,1)} %collective-permute-done.9, bf16[4,5,104,800]{3,2,1,0:T(8,128)(2,1)S(1)} %copy-done.13), kind=kLoop, calls=%fused_computation | loop fusion | flops 3328000 | bytes 4992000 | tf_op jit(solution)/shard_map/convert_element_type | solution.py:86
  156.4 24.8 %conv_backward.1 = (bf16[4,800,512]{2,1,0:T(8,128)(2,1)}, f32[8,800]{1,0:T(8,128)}) custom-call(bf16[4,800,512]{2,1,0:T(8,128)(2,1)} %get-tuple-element.129.dh2_ref, bf16[4,8,800]{2,1,0:T(8,128)(2,1)} %copy-done.23, f32[4,800,512]{2,1,0:T(8,128)} %get-tuple-element.130.h1_ref, f32[4,8,512]{2,1,0:T(8,128)} %get-tuple-element.131.st_ref, ...), custom_call_target="tpu_custom_call" | custom-call | flops 159907840000 | bytes 1 | tf_op jit(solution)/shard_map/conv_backward/pallas_call | solution.py:924
  181.2 2.1 fusion
  184.8 11.3 %grad_weight_in.1 = (bf16[4,208,800]{2,1,0:T(8,128)(2,1)}, bf16[4,208,800]{2,1,0:T(8,128)(2,1)}) custom-call(bf16[4,1600,512]{2,1,0:T(8,128)(2,1)} %first_act.1.a0_ref.a_ref, bf16[4,800,512]{2,1,0:T(8,128)(2,1)} %get-tuple-element.137.b_ref.dh1_ref), custom_call_target="tpu_custom_call" | custom-call | flops 104857600000 | bytes 1 | tf_op jit(solution)/shard_map/grad_weight_in/pallas_call | solution.py:799
  196.9 2.2 bitcast_add_fusion
  199.9 2.4 collective-permute-start.15
  202.3 6.8 %block_output.4 = (bf16[4,1600,512]{2,1,0:T(8,128)(2,1)}, f32[8,512]{1,0:T(8,128)}) custom-call(bf16[4,1600,512]{2,1,0:T(8,128)(2,1)} %bitcast.37, bf16[4,800,512]{2,1,0:T(8,128)(2,1)} %get-tuple-element.120.a2_ref, bf16[1600,800]{1,0:T(8,128)(2,1)} %transpose_out.1.wt_ref, bf16[224,800]{1,0:T(8,128)(2,1)} %prepare_in.1.v0, ...), custom_call_target="tpu_custom_call", output_to_operand_aliasing={{0}: (6, {})} | custom-call | flops 26378240000 | bytes 1 | tf_op jit(solution)/shard_map/block_output/pallas_call | solution.py:1062
  209.1 2.2 add_convert_fusion.2
  211.6 9.3 %grad_stream.3 = (bf16[4,1600,512]{2,1,0:T(8,128)(2,1)}, f32[8,1600]{1,0:T(8,128)}) custom-call(bf16[4,1600,512]{2,1,0:T(8,128)(2,1)} %bitcast.38, f32[4,8,512]{2,1,0:T(8,128)} %get-tuple-element.111.st_ref.before_ref, bf16[4,1600,512]{2,1,0:T(8,128)(2,1)} %bitcast.47, bf16[4,800,512]{2,1,0:T(8,128)(2,1)} %get-tuple-element.137.b_ref.dh1_ref, ...), custom_call_target="tpu_custom_call" | custom-call | flops 26869760000 | bytes 1 | tf_op jit(solution)/shard_map/grad_stream/pallas_call | solution.py:1007
  221.1 2.8 collective-permute-start.17
  226.7 9.7 %block_output.5 = (bf16[4,1600,512]{2,1,0:T(8,128)(2,1)}, f32[8,512]{1,0:T(8,128)}) custom-call(bf16[4,1600,512]{2,1,0:T(8,128)(2,1)} %bitcast.39, bf16[4,800,512]{2,1,0:T(8,128)(2,1)} %get-tuple-element.120.a2_ref, bf16[1600,800]{1,0:T(8,128)(2,1)} %transpose_out.1.wt_ref, bf16[224,800]{1,0:T(8,128)(2,1)} %prepare_in.1.v0, ...), custom_call_target="tpu_custom_call", output_to_operand_aliasing={{0}: (6, {})} | custom-call | flops 52756480000 | bytes 1 | tf_op jit(solution)/shard_map/block_output/pallas_call | solution.py:1062
  240.8 9.3 %grad_stream.4 = (bf16[4,1600,512]{2,1,0:T(8,128)(2,1)}, f32[8,1600]{1,0:T(8,128)}) custom-call(bf16[4,1600,512]{2,1,0:T(8,128)(2,1)} %bitcast.40, f32[4,8,512]{2,1,0:T(8,128)} %get-tuple-element.111.st_ref.before_ref, bf16[4,1600,512]{2,1,0:T(8,128)(2,1)} %bitcast.48, ...), custom_call_target="tpu_custom_call", output_to_operand_aliasing={{0}: (8, {})} | custom-call | flops 26869760000 | bytes 1 | tf_op jit(solution)/shard_map/grad_stream/pallas_call | solution.py:1007
  251.2 3.7 %collective-permute-done.18 = bf16[208,800]{1,0:T(8,128)(2,1)S(1)} collective-permute-done((bf16[208,800]{1,0:T(8,128)(2,1)S(1)}, bf16[208,800]{1,0:T(8,128)(2,1)S(1)}, u32[]{:S(2)}, u32[]{:S(2)}) %collective-permute-start.18) | collective-permute-done | bytes 332832 | tf_op jit(solution)/shard_map/ppermute | solution.py:29
  255.3 15.4 %grad_stream.5 = (bf16[4,1600,512]{2,1,0:T(8,128)(2,1)}, f32[8,1600]{1,0:T(8,128)}) custom-call(bf16[4,1600,512]{2,1,0:T(8,128)(2,1)} %bitcast.41, f32[4,8,512]{2,1,0:T(8,128)} %get-tuple-element.111.st_ref.before_ref, bf16[4,1600,512]{2,1,0:T(8,128)(2,1)} %bitcast.49, ...), custom_call_target="tpu_custom_call", output_to_operand_aliasing={{0}: (8, {})} | custom-call | flops 53739520000 | bytes 1 | tf_op jit(solution)/shard_map/grad_stream/pallas_call | solution.py:1007
  270.7 2.4 collective-permute-done.23
  274.6 2.7 collective-permute-done.21
  281.5 2.5 join_grads.1
  285.0 2.7 collective-permute-start.29
  290.0 3.6 %collective-permute-done.30 = f32[8,1600]{1,0:T(8,128)S(1)} collective-permute-done((f32[8,1600]{1,0:T(8,128)S(1)}, f32[8,1600]{1,0:T(8,128)S(1)}, u32[]{:S(2)}, u32[]{:S(2)}) %collective-permute-start.30) | collective-permute-done | bytes 51232 | tf_op jit(solution)/shard_map/ppermute | solution.py:29
  (128 shorter events, 47.5 us)
Async XLA Ops:
  2.6 9.2 %collective-permute-start = (bf16[224,800]{1,0:T(8,128)(2,1)}, bf16[224,800]{1,0:T(8,128)(2,1)}, u32[]{:S(2)}, u32[]{:S(2)}) collective-permute-start(bf16[224,800]{1,0:T(8,128)(2,1)} %prepare_in.1.v0), channel_id=1, source_target_pairs={{0,8},{1,17},{2,10},{3,19},{4,12},{5,21},{6,14},{7,23},{8,0},{9,25... | collective-permute-start | bytes 1075208 | tf_op jit(solution)/shard_map/ppermute | solution.py:25
  12.9 12.3 %collective-permute-start.1 = (bf16[2,224,800]{2,1,0:T(8,128)(2,1)S(1)}, bf16[2,224,800]{2,1,0:T(8,128)(2,1)}, u32[]{:S(2)}, u32[]{:S(2)}) collective-permute-start(bf16[2,224,800]{2,1,0:T(8,128)(2,1)S(1)} %pad_maximum_fusion.2), channel_id=1, source_target_pairs={{0,16},{1,9},{2,18},{3,11},{4,20},{5,13},{6,22},{7,15},{8,24},{9,1... | collective-permute-start | bytes 2150408 | tf_op jit(solution)/shard_map/ppermute | solution.py:25
  25.3 13.5 %collective-permute-start.4 = (bf16[5,104,800]{2,1,0:T(8,128)(2,1)S(1)}, bf16[5,104,800]{2,1,0:T(8,128)(2,1)S(1)}, u32[]{:S(2)}, u32[]{:S(2)}) collective-permute-start(bf16[5,104,800]{2,1,0:T(8,128)(2,1)S(1)} %copy-done.12), channel_id=1, source_target_pairs={{0,8},{1,17},{2,10},{3,19},{4,12},{5,21},{6,14},{7,23},{8,0},{9,25... | collective-permute-start | bytes 2496008 | tf_op jit(solution)/shard_map/ppermute | solution.py:25
  27.2 16.0 %collective-permute-start.3 = (bf16[2,224,800]{2,1,0:T(8,128)(2,1)}, bf16[2,224,800]{2,1,0:T(8,128)(2,1)}, u32[]{:S(2)}, u32[]{:S(2)}) collective-permute-start(bf16[2,224,800]{2,1,0:T(8,128)(2,1)} %collective-permute-done.1.v2.p2), channel_id=1, source_target_pairs={{0,1},{1,0},{2,3},{3,2},{4,5},{5,4},{6,7},{7,6},{8,9},{9,8},{10,11... | collective-permute-start | bytes 2150408 | tf_op jit(solution)/shard_map/ppermute | solution.py:29
  27.2 16.0 %collective-permute-start.2 = (bf16[224,800]{1,0:T(8,128)(2,1)}, bf16[224,800]{1,0:T(8,128)(2,1)S(1)}, u32[]{:S(2)}, u32[]{:S(2)}) collective-permute-start(bf16[224,800]{1,0:T(8,128)(2,1)} %collective-permute-done.v1.p1), channel_id=1, source_target_pairs={{0,1},{1,0},{2,3},{3,2},{4,5},{5,4},{6,7},{7,6},{8,9},{9,8},{10,11... | collective-permute-start | bytes 1075208 | tf_op jit(solution)/shard_map/ppermute | solution.py:29
  41.2 23.7 %copy-start.17 = (bf16[5,104,800]{2,1,0:T(8,128)(2,1)S(1)}, bf16[5,104,800]{2,1,0:T(8,128)(2,1)}, u32[]{:S(2)}) copy-start(bf16[5,104,800]{2,1,0:T(8,128)(2,1)} %copy-done.16) | copy-start | bytes 2496004
  41.2 23.7 %collective-permute-start.6 = (bf16[2,5,104,800]{3,2,1,0:T(8,128)(2,1)S(1)}, bf16[2,5,104,800]{3,2,1,0:T(8,128)(2,1)}, u32[]{:S(2)}, u32[]{:S(2)}) collective-permute-start(bf16[2,5,104,800]{3,2,1,0:T(8,128)(2,1)S(1)} %pad_maximum_fusion), channel_id=1, source_target_pairs={{0,16},{1,9},{2,18},{3,11},{4,20},{5,13},{6,22},{7,15},{8,24},{9,1... | collective-permute-start | bytes 4992008 | tf_op jit(solution)/shard_map/ppermute | solution.py:25
  64.9 5.4 %collective-permute-start.8 = (bf16[2,5,104,800]{3,2,1,0:T(8,128)(2,1)}, bf16[2,5,104,800]{3,2,1,0:T(8,128)(2,1)S(1)}, u32[]{:S(2)}, u32[]{:S(2)}) collective-permute-start(bf16[2,5,104,800]{3,2,1,0:T(8,128)(2,1)} %collective-permute-done.6.g), channel_id=1, source_target_pairs={{0,1},{1,0},{2,3},{3,2},{4,5},{5,4},{6,7},{7,6},{8,9},{9,8},{10,11... | collective-permute-start | bytes 4992008 | tf_op jit(solution)/shard_map/ppermute | solution.py:29
  64.9 4.9 %collective-permute-start.7 = (bf16[5,104,800]{2,1,0:T(8,128)(2,1)S(1)}, bf16[5,104,800]{2,1,0:T(8,128)(2,1)S(1)}, u32[]{:S(2)}, u32[]{:S(2)}) collective-permute-start(bf16[5,104,800]{2,1,0:T(8,128)(2,1)S(1)} %copy-done.17), channel_id=1, source_target_pairs={{0,1},{1,0},{2,3},{3,2},{4,5},{5,4},{6,7},{7,6},{8,9},{9,8},{10,11... | collective-permute-start | bytes 2496008 | tf_op jit(solution)/shard_map/ppermute | solution.py:29
  65.4 16.1 %collective-permute-start.5 = (bf16[4,8,800]{2,1,0:T(8,128)(2,1)}, bf16[4,8,800]{2,1,0:T(8,128)(2,1)S(1)}, u32[]{:S(2)}, u32[]{:S(2)}) collective-permute-start(bf16[4,8,800]{2,1,0:T(8,128)(2,1)} %get-tuple-element.115), channel_id=1, source_target_pairs={{0,1},{1,2},{2,3},{3,4},{4,5},{5,6},{6,7},{8,9},{9,10},{10,11},{11... | collective-permute-start | bytes 153608 | tf_op jit(solution)/shard_map/ppermute | solution.py:34
  137.5 13.0 %collective-permute-start.9 = (bf16[4,5,104,800]{3,2,1,0:T(8,128)(2,1)}, bf16[4,5,104,800]{3,2,1,0:T(8,128)(2,1)}, u32[]{:S(2)}, u32[]{:S(2)}) collective-permute-start(bf16[4,5,104,800]{3,2,1,0:T(8,128)(2,1)} %get-tuple-element.123), channel_id=1, source_target_pairs={{0,1},{1,0},{2,3},{3,2},{4,5},{5,4},{6,7},{7,6},{8,9},{9,8},{10,11... | collective-permute-start | bytes 9984008 | tf_op jit(solution)/shard_map/ppermute | solution.py:29
  138.0 17.8 %collective-permute-start.11 = (bf16[4,8,800]{2,1,0:T(8,128)(2,1)}, bf16[4,8,800]{2,1,0:T(8,128)(2,1)S(1)}, u32[]{:S(2)}, u32[]{:S(2)}) collective-permute-start(bf16[4,8,800]{2,1,0:T(8,128)(2,1)} %get-tuple-element.121), channel_id=1, source_target_pairs={{1,0},{2,1},{3,2},{4,3},{5,4},{6,5},{7,6},{9,8},{10,9},{11,10},{12... | collective-permute-start | bytes 153608 | tf_op jit(solution)/shard_map/ppermute | solution.py:34
  153.7 27.4 %collective-permute-start.10 = (bf16[2,5,104,800]{3,2,1,0:T(8,128)(2,1)}, bf16[2,5,104,800]{3,2,1,0:T(8,128)(2,1)}, u32[]{:S(2)}, u32[]{:S(2)}) collective-permute-start(bf16[2,5,104,800]{3,2,1,0:T(8,128)(2,1)} %add_convert_fusion), channel_id=1, source_target_pairs={{0,8},{1,17},{2,10},{3,19},{4,12},{5,21},{6,14},{7,23},{8,0},{9,25... | collective-permute-start | bytes 4992008 | tf_op jit(solution)/shard_map/ppermute | solution.py:25
  183.3 13.6 %collective-permute-start.12 = (bf16[5,104,800]{2,1,0:T(8,128)(2,1)S(1)}, bf16[5,104,800]{2,1,0:T(8,128)(2,1)S(1)}, u32[]{:S(2)}, u32[]{:S(2)}) collective-permute-start(bf16[5,104,800]{2,1,0:T(8,128)(2,1)S(1)} %fusion), channel_id=1, source_target_pairs={{0,16},{1,9},{2,18},{3,11},{4,20},{5,13},{6,22},{7,15},{8,24},{9,1... | collective-permute-start | bytes 2496008 | tf_op jit(solution)/shard_map/ppermute | solution.py:25
  196.1 12.9 %collective-permute-start.13 = (bf16[4,208,800]{2,1,0:T(8,128)(2,1)}, bf16[4,208,800]{2,1,0:T(8,128)(2,1)}, u32[]{:S(2)}, u32[]{:S(2)}) collective-permute-start(bf16[4,208,800]{2,1,0:T(8,128)(2,1)} %get-tuple-element.138), channel_id=1, source_target_pairs={{0,1},{1,0},{2,3},{3,2},{4,5},{5,4},{6,7},{7,6},{8,9},{9,8},{10,11... | collective-permute-start | bytes 3993608 | tf_op jit(solution)/shard_map/ppermute | solution.py:29
  199.9 21.0 %collective-permute-start.15 = (bf16[5,56,800]{2,1,0:T(8,128)(2,1)}, bf16[5,56,800]{2,1,0:T(8,128)(2,1)S(1)}, u32[]{:S(2)}, u32[]{:S(2)}) collective-permute-start(bf16[5,56,800]{2,1,0:T(8,128)(2,1)} %dynamic-slice_convert_fusion), channel_id=1, source_target_pairs={{0,2},{1,3},{2,0},{3,1},{4,6},{5,7},{6,4},{7,5},{8,10},{9,11},{10,... | collective-permute-start | bytes 1344008 | tf_op jit(solution)/shard_map/ppermute | solution.py:29
  211.2 12.7 %collective-permute-start.14 = (bf16[2,208,800]{2,1,0:T(8,128)(2,1)}, bf16[2,208,800]{2,1,0:T(8,128)(2,1)S(1)}, u32[]{:S(2)}, u32[]{:S(2)}) collective-permute-start(bf16[2,208,800]{2,1,0:T(8,128)(2,1)} %add_convert_fusion.2), channel_id=1, source_target_pairs={{0,8},{1,17},{2,10},{3,19},{4,12},{5,21},{6,14},{7,23},{8,0},{9,25... | collective-permute-start | bytes 1996808 | tf_op jit(solution)/shard_map/ppermute | solution.py:25
  221.1 15.4 %collective-permute-start.17 = (bf16[5,32,800]{2,1,0:T(8,128)(2,1)S(1)}, bf16[5,32,800]{2,1,0:T(8,128)(2,1)S(1)}, u32[]{:S(2)}, u32[]{:S(2)}) collective-permute-start(bf16[5,32,800]{2,1,0:T(8,128)(2,1)S(1)} %dynamic-slice_convert_fusion.1), channel_id=1, source_target_pairs={{0,4},{1,5},{2,6},{3,7},{4,0},{5,1},{6,2},{7,3},{8,12},{9,13},{10,... | collective-permute-start | bytes 768008 | tf_op jit(solution)/shard_map/ppermute | solution.py:29
  225.2 13.1 %collective-permute-start.16 = (bf16[208,800]{1,0:T(8,128)(2,1)S(1)}, bf16[208,800]{1,0:T(8,128)(2,1)S(1)}, u32[]{:S(2)}, u32[]{:S(2)}) collective-permute-start(bf16[208,800]{1,0:T(8,128)(2,1)S(1)} %fusion.4), channel_id=1, source_target_pairs={{0,16},{1,9},{2,18},{3,11},{4,20},{5,13},{6,22},{7,15},{8,24},{9,1... | collective-permute-start | bytes 998408 | tf_op jit(solution)/shard_map/ppermute | solution.py:25
  236.5 14.5 %collective-permute-start.19 = (bf16[5,32,800]{2,1,0:T(8,128)(2,1)S(1)}, bf16[5,32,800]{2,1,0:T(8,128)(2,1)S(1)}, u32[]{:S(2)}, u32[]{:S(2)}) collective-permute-start(bf16[5,32,800]{2,1,0:T(8,128)(2,1)S(1)} %add_convert_fusion.5), channel_id=1, source_target_pairs={{0,4},{1,5},{2,6},{3,7},{4,0},{5,1},{6,2},{7,3},{8,12},{9,13},{10,... | collective-permute-start | bytes 768008 | tf_op jit(solution)/shard_map/ppermute | solution.py:29
  239.6 15.3 %collective-permute-start.18 = (bf16[208,800]{1,0:T(8,128)(2,1)S(1)}, bf16[208,800]{1,0:T(8,128)(2,1)S(1)}, u32[]{:S(2)}, u32[]{:S(2)}) collective-permute-start(bf16[208,800]{1,0:T(8,128)(2,1)S(1)} %fusion.1), channel_id=1, source_target_pairs={{0,2},{1,3},{2,0},{3,1},{4,6},{5,7},{6,4},{7,5},{8,10},{9,11},{10,... | collective-permute-start | bytes 998408 | tf_op jit(solution)/shard_map/ppermute | solution.py:29
  251.2 21.9 %collective-permute-start.23 = (bf16[5,56,800]{2,1,0:T(8,128)(2,1)S(1)}, bf16[5,56,800]{2,1,0:T(8,128)(2,1)S(1)}, u32[]{:S(2)}, u32[]{:S(2)}) collective-permute-start(bf16[5,56,800]{2,1,0:T(8,128)(2,1)S(1)} %pad_maximum_fusion.3), channel_id=1, source_target_pairs={{0,2},{1,3},{2,0},{3,1},{4,6},{5,7},{6,4},{7,5},{8,10},{9,11},{10,... | collective-permute-start | bytes 1344008 | tf_op jit(solution)/shard_map/ppermute | solution.py:29
  255.0 18.7 %collective-permute-start.20 = (bf16[208,800]{1,0:T(8,128)(2,1)S(1)}, bf16[208,800]{1,0:T(8,128)(2,1)S(1)}, u32[]{:S(2)}, u32[]{:S(2)}) collective-permute-start(bf16[208,800]{1,0:T(8,128)(2,1)S(1)} %add_convert_fusion.3), channel_id=1, source_target_pairs={{0,4},{1,5},{2,6},{3,7},{4,0},{5,1},{6,2},{7,3},{8,12},{9,13},{10,... | collective-permute-start | bytes 998408 | tf_op jit(solution)/shard_map/ppermute | solution.py:29
  273.6 7.9 %collective-permute-start.24 = (bf16[5,104,800]{2,1,0:T(8,128)(2,1)S(1)}, bf16[5,104,800]{2,1,0:T(8,128)(2,1)S(1)}, u32[]{:S(2)}, u32[]{:S(2)}) collective-permute-start(bf16[5,104,800]{2,1,0:T(8,128)(2,1)S(1)} %pad_maximum_fusion.1.mine_ref), channel_id=1, source_target_pairs={{0,1},{1,0},{2,3},{3,2},{4,5},{5,4},{6,7},{7,6},{8,9},{9,8},{10,11... | collective-permute-start | bytes 2496008 | tf_op jit(solution)/shard_map/ppermute | solution.py:29
  273.8 7.8 %collective-permute-start.25 = (f32[208,800]{1,0:T(8,128)S(1)}, f32[208,800]{1,0:T(8,128)S(1)}, u32[]{:S(2)}, u32[]{:S(2)}) collective-permute-start(f32[208,800]{1,0:T(8,128)S(1)} %convert_add_fusion.1.mine_in), channel_id=1, source_target_pairs={{0,1},{1,0},{2,3},{3,2},{4,5},{5,4},{6,7},{7,6},{8,9},{9,8},{10,11... | collective-permute-start | bytes 1996808 | tf_op jit(solution)/shard_map/ppermute | solution.py:29
  274.5 2.8 collective-permute-start.21
  277.3 4.2 %collective-permute-start.22 = (f32[8,1600]{1,0:T(8,128)S(1)}, f32[8,1600]{1,0:T(8,128)S(1)}, u32[]{:S(2)}, u32[]{:S(2)}) collective-permute-start(f32[8,1600]{1,0:T(8,128)S(1)} %add.132), channel_id=1, source_target_pairs={{0,8},{8,0},{16,24},{24,16},{1,9},{9,1},{17,25},{25,17},{2,10},{10... | collective-permute-start | bytes 153608 | tf_op jit(solution)/shard_map/ppermute | solution.py:29
  278.3 5.7 %collective-permute-start.26 = (f32[8,1600]{1,0:T(8,128)S(1)}, f32[8,1600]{1,0:T(8,128)S(1)}, u32[]{:S(2)}, u32[]{:S(2)}) collective-permute-start(f32[8,1600]{1,0:T(8,128)S(1)} %add.132), channel_id=1, source_target_pairs={{0,16},{8,24},{16,0},{24,8},{1,17},{9,25},{17,1},{25,9},{2,18},{10... | collective-permute-start | bytes 153608 | tf_op jit(solution)/shard_map/ppermute | solution.py:29
  279.8 5.0 %collective-permute-start.27 = (f32[8,1600]{1,0:T(8,128)S(1)}, f32[8,1600]{1,0:T(8,128)S(1)}, u32[]{:S(2)}, u32[]{:S(2)}) collective-permute-start(f32[8,1600]{1,0:T(8,128)S(1)} %add.132), channel_id=1, source_target_pairs={{0,24},{8,16},{16,8},{24,0},{1,25},{9,17},{17,9},{25,1},{2,26},{10... | collective-permute-start | bytes 153608 | tf_op jit(solution)/shard_map/ppermute | solution.py:29
  284.8 4.5 %collective-permute-start.28 = (f32[8,1600]{1,0:T(8,128)S(1)}, f32[8,1600]{1,0:T(8,128)S(1)}, u32[]{:S(2)}, u32[]{:S(2)}) collective-permute-start(f32[8,1600]{1,0:T(8,128)S(1)} %add_add_fusion.1), channel_id=1, source_target_pairs={{0,2},{1,3},{2,0},{3,1},{4,6},{5,7},{6,4},{7,5},{8,10},{9,11},{10,... | collective-permute-start | bytes 153608 | tf_op jit(solution)/shard_map/ppermute | solution.py:29
  285.0 5.0 %collective-permute-start.29 = (f32[8,1600]{1,0:T(8,128)S(1)}, f32[8,1600]{1,0:T(8,128)S(1)}, u32[]{:S(2)}, u32[]{:S(2)}) collective-permute-start(f32[8,1600]{1,0:T(8,128)S(1)} %add_add_fusion.1), channel_id=1, source_target_pairs={{0,4},{1,5},{2,6},{3,7},{4,0},{5,1},{6,2},{7,3},{8,12},{9,13},{10,... | collective-permute-start | bytes 153608 | tf_op jit(solution)/shard_map/ppermute | solution.py:29
  287.7 5.9 %collective-permute-start.30 = (f32[8,1600]{1,0:T(8,128)S(1)}, f32[8,1600]{1,0:T(8,128)S(1)}, u32[]{:S(2)}, u32[]{:S(2)}) collective-permute-start(f32[8,1600]{1,0:T(8,128)S(1)} %add_add_fusion.1), channel_id=1, source_target_pairs={{0,6},{1,7},{2,4},{3,5},{4,2},{5,3},{6,0},{7,1},{8,14},{9,15},{10,... | collective-permute-start | bytes 153608 | tf_op jit(solution)/shard_map/ppermute | solution.py:29
  (23 other events, 61.7 us)

commit v3 on v2

--- a/solution.py
+++ b/solution.py
@@ -277,7 +277,7 @@
         c.wait()
 
 
-def assemble(shard, pieces, k, wide_s):
+def assemble(shard, pieces, wide_s):
     first, second, other_first, other_second = pieces
     rows = shard.shape[0]
     off, _ = half_of(rows)
@@ -291,12 +291,12 @@
         wide_s[start, :] = piece.astype(F32)
 
     put(me, 0, shard)
-    put(near, core, first[k])
-    put(far, core, second[0, k])
-    put(both, core, second[1, k])
-    put(far, 1 - core, other_first[k])
-    put(near, 1 - core, other_second[0, k])
-    put(both, 1 - core, other_second[1, k])
+    put(near, core, first[...])
+    put(far, core, second[0])
+    put(both, core, second[1])
+    put(far, 1 - core, other_first[...])
+    put(near, 1 - core, other_second[0])
+    put(both, 1 - core, other_second[1])
     return wide_s[...].astype(BF)
 
 
@@ -310,7 +310,7 @@
     )
 
 
-def split_grad(acc_ref, keep_ref, send_ref, taps, first_block=None):
+def split_grad(acc_ref, keep_ref, send_ref, taps, first_block=None, slots=(0, 1, 2, 3)):
     me, core = lax.axis_index("dp"), lax.rem(lax.axis_index("ctx"), 2)
     block = acc_ref.shape[0] // taps
     width = keep_ref.shape[-1]
@@ -318,7 +318,7 @@
     off, size = half_of(rows)
     mine = (0, 2 - core, 1 + core, 3)
     theirs = (0, 1 + core, 2 - core, 3)
-    for j in range(4):
+    for j in slots:
         for k in range(taps):
             a = jnp.bitwise_xor(me, mine[j]) * rows + core * off + k * block
             b = jnp.bitwise_xor(me, theirs[j]) * rows + (1 - core) * off + k * block
@@ -530,29 +530,56 @@
 
 
 def assemble_body(wc_own, wo_own, f, g, of, og, wc_ref, wct_ref, wo_ref, tap_s):
-    inner = wc_ref.shape[1]
-    pieces = (f, g, of, og)
-    for k in range(3):
-        wc_ref[k] = assemble(wc_own[k], pieces, k, tap_s)
-    wct_ref[...] = wc_ref[...].reshape(3 * inner, inner).T
+    step = pl.program_id(0)
+    inner = wc_ref.shape[0]
+
+    @pl.when(step < 3)
+    def _():
+        w = assemble(wc_own[...], (f, g, of, og), tap_s)
+        wc_ref[...] = w
+        t = w.T
+        for k in range(3):
+
+            @pl.when(step == k)
+            def _():
+                wct_ref[:, k * inner : (k + 1) * inner] = t
+
     for k in range(2):
-        wo_ref[k] = assemble(wo_own[:, k * inner : (k + 1) * inner], pieces, 3 + k, tap_s)
+
+        @pl.when(step == 3 + k)
+        def _():
+            own = wo_own[:, k * inner : (k + 1) * inner]
+            wo_ref[...] = assemble(own, (f, g, of, og), tap_s)
 
 
 def assemble_weights(own_conv, own_out, pieces):
     inner = own_conv.shape[2]
-    vmem = pl.BlockSpec(memory_space=pltpu.VMEM)
+    rows, size = own_conv.shape[1], pieces[0].shape[1]
+    one = pl.BlockSpec((None, size, inner), lambda k: (k, 0, 0))
+    two = pl.BlockSpec((2, None, size, inner), lambda k: (0, k, 0, 0))
     return pl.pallas_call(
         assemble_body,
-        in_specs=[vmem] * 6,
-        out_specs=[vmem] * 3,
+        grid=(5,),
+        in_specs=[
+            pl.BlockSpec((None, rows, inner), lambda k: (jnp.minimum(k, 2), 0, 0)),
+            full(own_out.shape),
+            one,
+            two,
+            one,
+            two,
+        ],
+        out_specs=[
+            pl.BlockSpec((None, inner, inner), lambda k: (jnp.minimum(k, 2), 0, 0)),
+            full((inner, 3 * inner)),
+            pl.BlockSpec((None, inner, inner), lambda k: (jnp.maximum(k - 3, 0), 0, 0)),
+        ],
         out_shape=[
             sds((3, inner, inner), BF),
             sds((inner, 3 * inner), BF),
             sds((2, inner, inner), BF),
         ],
         scratch_shapes=[pltpu.VMEM((inner, inner), F32)],
-        compiler_params=params(),
+        compiler_params=params(30),
         cost_estimate=cost(0, 4 * inner * inner),
         name="assemble_weights",
     )(own_conv, own_out, *pieces)
@@ -580,7 +607,7 @@
 def conv_body(
     a1_ref, halo_ref, dy_ref, dyp_ref, mk_ref, wct_ref, wo_ref, v0, v1, v2,
     a2_ref, dh2_ref, edge_ref, sums_ref, bo_ref, sq_ref, keep_ref, send_ref,
-    st_s, a2_s, dh_s, h_s, d_s, hl_s, vi_s, sums_s, bo_s, acc_s, out_s, mi_s,
+    st_s, a2_s, dh_s, h_s, d_s, hl_s, vi_s, sums_s, bo_s, acc_s, out_s, mi_s, keep_s, send_s, gsem,
 ):
     s = pl.program_id(0)
     seqs = pl.num_programs(0) - 1
@@ -712,8 +739,15 @@
         for j in range(3):
             sums_ref[j : j + 1, :] = gathered_row(sums_s[j]) * (0.5, 0.5, 1.0)[j]
         bo_ref[0:1, :] = gathered_row(bo_s[...])
-        split_grad(acc_s, keep_ref, send_ref, 3)
-        split_grad(out_s, keep_ref, send_ref, 1, 3)
+        copies = []
+        for j in range(4):
+            split_grad(acc_s, keep_s, send_s, 3, slots=(j,))
+            split_grad(out_s, keep_s, send_s, 1, 3, slots=(j,))
+            for i, (src, dst) in enumerate(((send_s, send_ref), (keep_s, keep_ref))):
+                copies.append(pltpu.make_async_copy(src.at[j], dst.at[j], gsem.at[2 * j + i]))
+                copies[-1].start()
+        for c in copies:
+            c.wait()
 
 
 def conv(a1, halo, dy, mk, wct, wo, packs):
@@ -743,8 +777,8 @@
             full((8, inner)),
             full((8, wide)),
             full((8, length)),
-            full((4, 5, size, inner)),
-            full((4, 5, size, inner)),
+            ANY,
+            ANY,
         ],
         out_shape=[
             sds((seqs, inner, length), BF),
@@ -769,6 +803,9 @@
             pltpu.VMEM((3 * inner, inner), F32),
             pltpu.VMEM((inner, wide), F32),
             pltpu.VMEM((8, length), F32),
+            pltpu.VMEM((4, 5, size, inner), BF),
+            pltpu.VMEM((4, 5, size, inner), BF),
+            pltpu.SemaphoreType.DMA((8,)),
         ],
         compiler_params=params(),
         cost_estimate=cost(a1.size * (6 * inner + 2 * wide), 2 * a1.size),

time: 299 us -> 297 us (level)
  Pallas kernels: 202 us -> 199 us
    pallas_call x1, Pallas kernels: 9.59 us -> 5.81 us  [assemble_weights(): pl.pallas_call(assemble_body, grid=(5,), in_specs=[pl.BlockSpec((None, ro...]
    unnamed x48 -> x52, local copies, waits for them, and re-layouts: 4.66 us -> 7.63 us
  transfers between devices with their start and end apart: 31 -> 31, of which waited for: 15 -> 15; matrix products, arithmetic and copies ran while one was open for 5% -> 5% of each run, Pallas kernels for 49% -> 48%
where the time goes in v3:
time: 297 us; the launch traced here: 293 us
  Pallas kernels  199 us (67%)
  starting transfers between devices  37.1 us (12%)
  waiting for transfers between devices  31.7 us (11%)
  other arithmetic  14.8 us (5%)
  local copies, waits for them, and re-layouts  9.29 us (3%)
    pallas_call x1, Pallas kernels, conv(): pl.pallas_call(conv_body, grid=(seqs + 1,), in_specs=[this((inner, length...  55.4 us
    pallas_call x3, Pallas kernels, stream_back(): pl.pallas_call(stream_body, grid=(count,), in_specs=[seq_from(begin, (wid...  33.9 us
    pallas_call x1, Pallas kernels, conv_back(): pl.pallas_call(conv_back_body, grid=(seqs + 1,), in_specs=[this_seq(seqs,...  24.8 us
    pallas_call x3, Pallas kernels, output_of(): pl.pallas_call(output_body, grid=(count,), in_specs=[seq_from(begin, (wid...  23.6 us
    ppermute x21, starting transfers between devices, swap(): lax.ppermute(value, axis, [(i, i ^ mask) for i in range(lax.axis_size(axi...  19.6 us
    ppermute x21, waiting for transfers between devices, swap(): lax.ppermute(value, axis, [(i, i ^ mask) for i in range(lax.axis_size(axi...  18.1 us
    pallas_call x1, Pallas kernels, first(): pl.pallas_call(first_body, grid=(seqs,), in_specs=[seq((wide, length))] +...  17.3 us
    ppermute x8, starting transfers between devices, by_core(): return lax.ppermute(value, ('dp', 'ctx'), pairs)  14.2 us
  transfers between devices with their start and end apart: 31, of which 15 were waited for; matrix products, arithmetic and copies ran while one was open for 5% of the time, Pallas kernels for 48%

profile of v3, /device:TPU:0, one launch (start us, length us, event | category | flops | bytes accessed | tf_op | source)
XLA Modules:
  0.0 292.9 jit_solution(14890283069567001252)
XLA Ops:
  2.6 2.9 %collective-permute-start = (bf16[224,800]{1,0:T(8,128)(2,1)}, bf16[224,800]{1,0:T(8,128)(2,1)S(1)}, u32[]{:S(2)}, u32[]{:S(2)}) collective-permute-start(bf16[224,800]{1,0:T(8,128)(2,1)} %prepare_in.1.v0), channel_id=1, source_target_pairs={{0,8},{1,17},{2,10},{3,19},{4,12},{5,21},{6,14},{7,23},{8,0},{9,25... | collective-permute-start | bytes 1075208 | tf_op jit(solution)/shard_map/ppermute | solution.py:25
  5.6 2.5 prepare_rest.1
  8.1 3.7 %collective-permute-done.v1.p1 = bf16[224,800]{1,0:T(8,128)(2,1)S(1)} collective-permute-done((bf16[224,800]{1,0:T(8,128)(2,1)}, bf16[224,800]{1,0:T(8,128)(2,1)S(1)}, u32[]{:S(2)}, u32[]{:S(2)}) %collective-permute-start) | collective-permute-done | bytes 358432 | tf_op jit(solution)/shard_map/ppermute | solution.py:25
  13.9 6.0 %input_stats.1 = (f32[4,8,512]{2,1,0:T(8,128)}, f32[8,512]{1,0:T(8,128)}) custom-call(bf16[4,1600,512]{2,1,0:T(8,128)(2,1)} %bitcast.35), custom_call_target="tpu_custom_call" | custom-call | flops 655360000 | bytes 1 | tf_op jit(solution)/shard_map/input_stats/pallas_call | solution.py:412
  19.8 4.3 %collective-permute-done.1.v2.p2 = bf16[2,224,800]{2,1,0:T(8,128)(2,1)} collective-permute-done((bf16[2,224,800]{2,1,0:T(8,128)(2,1)S(1)}, bf16[2,224,800]{2,1,0:T(8,128)(2,1)}, u32[]{:S(2)}, u32[]{:S(2)}) %collective-permute-start.1) | collective-permute-done | bytes 716832 | tf_op jit(solution)/shard_map/ppermute | solution.py:25
  27.6 8.5 %first_act.1.a0_ref.a_ref = bf16[4,1600,512]{2,1,0:T(8,128)(2,1)} custom-call(bf16[4,1600,512]{2,1,0:T(8,128)(2,1)} %bitcast.36, f32[4,8,512]{2,1,0:T(8,128)} %get-tuple-element.111.st_ref.before_ref, bf16[224,800]{1,0:T(8,128)(2,1)} %prepare_in.1.v0, bf16[224,800]{1,0:T(8,128)(2,1)} %copy-done.20, bf16[2,224,800]{2,1,0:T(8,128)(2,1)} %collective-permute-done.1.v2.p2), custom_call_target="tpu_custom_call" | custom-call | flops 1310720000 | bytes 1 | tf_op jit(solution)/shard_map/first_act/pallas_call | solution.py:445
  41.9 17.3 %first_product.1 = (f32[4,800,512]{2,1,0:T(8,128)}, bf16[4,800,512]{2,1,0:T(8,128)(2,1)}, bf16[4,8,800]{2,1,0:T(8,128)(2,1)}, f32[8,512]{1,0:T(8,128)}, f32[4,8,512]{2,1,0:T(8,128)}, /*index=5*/bf16[1600,800]{1,0:T(8,128)(2,1)}) custom-call(bf16[4,1600,512]{2,1,0:T(8,128)(2,1)} %first_act.1.a0_ref.a_ref, bf16[400,800]{1,0:T(8,128)(2,1)} %p0.1, ...), custom_call_target="tpu_custom_call" | custom-call | flops 107479040000 | bytes 1 | tf_op jit(solution)/shard_map/first_product/pallas_call | solution.py:499
  59.3 3.8 %collective-permute-done.6.g = bf16[2,5,104,800]{3,2,1,0:T(8,128)(2,1)} collective-permute-done((bf16[2,5,104,800]{3,2,1,0:T(8,128)(2,1)}, bf16[2,5,104,800]{3,2,1,0:T(8,128)(2,1)}, u32[]{:S(2)}, u32[]{:S(2)}) %collective-permute-start.6) | collective-permute-done | bytes 1664032 | tf_op jit(solution)/shard_map/ppermute | solution.py:25
  65.6 2.3 collective-permute-done.7.of
  68.4 5.8 %assemble_weights.1 = (bf16[3,800,800]{2,1,0:T(8,128)(2,1)S(1)}, bf16[800,2400]{1,0:T(8,128)(2,1)S(1)}, bf16[2,800,800]{2,1,0:T(8,128)(2,1)S(1)}) custom-call(bf16[3,200,800]{2,1,0:T(8,128)(2,1)S(1)} %copy-done.1, bf16[200,1600]{1,0:T(8,128)(2,1)S(1)} %copy-done.2, bf16[5,104,800]{2,1,0:T(8,128)(2,1)S(1)} %collective-permute-done.4.f, ...), custom_call_target="tpu_custom_call" | custom-call | flops 2048000000 | bytes 1 | tf_op jit(solution)/shard_map/assemble_weights/pallas_call | solution.py:560
  80.4 55.4 %conv_and_third_norm.1 = (bf16[4,800,512]{2,1,0:T(8,128)(2,1)}, bf16[4,800,512]{2,1,0:T(8,128)(2,1)}, bf16[4,8,800]{2,1,0:T(8,128)(2,1)}, f32[8,800]{1,0:T(8,128...) custom-call(bf16[4,800,512]{2,1,0:T(8,128)(2,1)} %get-tuple-element., ...), custom_call_target="tpu_custom_call" | custom-call | flops 526909440000 | bytes 1 | tf_op jit(solution)/shard_map/conv_and_third_norm/pallas_call | solution.py:761
  137.3 4.2 %transpose_out.1.wt_ref = bf16[1600,800]{1,0:T(8,128)(2,1)} custom-call(bf16[2,800,800]{2,1,0:T(8,128)(2,1)} %copy-done), custom_call_target="tpu_custom_call" | custom-call | tf_op jit(solution)/shard_map/transpose_out/pallas_call | solution.py:597
  141.5 7.1 %block_output.3 = (bf16[4,1600,512]{2,1,0:T(8,128)(2,1)}, f32[8,512]{1,0:T(8,128)}) custom-call(bf16[4,1600,512]{2,1,0:T(8,128)(2,1)} %bitcast.37, bf16[4,800,512]{2,1,0:T(8,128)(2,1)} %get-tuple-element.120.a2_ref, bf16[1600,800]{1,0:T(8,128)(2,1)} %transpose_out.1.wt_ref, bf16[224,800]{1,0:T(8,128)(2,1)} %prepare_in.1.v0, bf16[224,800]{1,0:T(8,128)(2,1)} %copy-done.20, ...), custom_call_target="tpu_custom_call" | custom-call | flops 26378240000 | bytes 1 | tf_op jit(solution)/shard_map/block_output/pallas_call | solution.py:1099
  148.6 3.2 %add_convert_fusion = bf16[2,5,104,800]{3,2,1,0:T(8,128)(2,1)} fusion(bf16[4,5,104,800]{3,2,1,0:T(8,128)(2,1)} %collective-permute-done.9, bf16[4,5,104,800]{3,2,1,0:T(8,128)(2,1)S(1)} %copy-done.18), kind=kLoop, calls=%fused_computation | loop fusion | flops 3328000 | bytes 4992000 | tf_op jit(solution)/shard_map/convert_element_type | solution.py:86
  154.4 24.8 %conv_backward.1 = (bf16[4,800,512]{2,1,0:T(8,128)(2,1)}, f32[8,800]{1,0:T(8,128)}) custom-call(bf16[4,800,512]{2,1,0:T(8,128)(2,1)} %get-tuple-element.129.dh2_ref, bf16[4,8,800]{2,1,0:T(8,128)(2,1)} %copy-done.25, f32[4,800,512]{2,1,0:T(8,128)} %get-tuple-element.130.h1_ref, f32[4,8,512]{2,1,0:T(8,128)} %get-tuple-element.131.st_ref, ...), custom_call_target="tpu_custom_call" | custom-call | flops 159907840000 | bytes 1 | tf_op jit(solution)/shard_map/conv_backward/pallas_call | solution.py:961
  179.2 2.1 fusion
  182.9 11.3 %grad_weight_in.1 = (bf16[4,208,800]{2,1,0:T(8,128)(2,1)}, bf16[4,208,800]{2,1,0:T(8,128)(2,1)}) custom-call(bf16[4,1600,512]{2,1,0:T(8,128)(2,1)} %first_act.1.a0_ref.a_ref, bf16[4,800,512]{2,1,0:T(8,128)(2,1)} %get-tuple-element.137.b_ref.dh1_ref), custom_call_target="tpu_custom_call" | custom-call | flops 104857600000 | bytes 1 | tf_op jit(solution)/shard_map/grad_weight_in/pallas_call | solution.py:836
  194.9 2.2 bitcast_add_fusion
  197.9 2.6 collective-permute-start.15
  200.5 6.8 %block_output.4 = (bf16[4,1600,512]{2,1,0:T(8,128)(2,1)}, f32[8,512]{1,0:T(8,128)}) custom-call(bf16[4,1600,512]{2,1,0:T(8,128)(2,1)} %bitcast.38, bf16[4,800,512]{2,1,0:T(8,128)(2,1)} %get-tuple-element.120.a2_ref, bf16[1600,800]{1,0:T(8,128)(2,1)} %transpose_out.1.wt_ref, bf16[224,800]{1,0:T(8,128)(2,1)} %prepare_in.1.v0, ...), custom_call_target="tpu_custom_call", output_to_operand_aliasing={{0}: (6, {})} | custom-call | flops 26378240000 | bytes 1 | tf_op jit(solution)/shard_map/block_output/pallas_call | solution.py:1099
  207.3 2.2 add_convert_fusion.2
  209.7 9.3 %grad_stream.3 = (bf16[4,1600,512]{2,1,0:T(8,128)(2,1)}, f32[8,1600]{1,0:T(8,128)}) custom-call(bf16[4,1600,512]{2,1,0:T(8,128)(2,1)} %bitcast.39, f32[4,8,512]{2,1,0:T(8,128)} %get-tuple-element.111.st_ref.before_ref, bf16[4,1600,512]{2,1,0:T(8,128)(2,1)} %bitcast.48, bf16[4,800,512]{2,1,0:T(8,128)(2,1)} %get-tuple-element.137.b_ref.dh1_ref, ...), custom_call_target="tpu_custom_call" | custom-call | flops 26869760000 | bytes 1 | tf_op jit(solution)/shard_map/grad_stream/pallas_call | solution.py:1044
  219.1 3.1 %collective-permute-start.17 = (bf16[5,32,800]{2,1,0:T(8,128)(2,1)S(1)}, bf16[5,32,800]{2,1,0:T(8,128)(2,1)S(1)}, u32[]{:S(2)}, u32[]{:S(2)}) collective-permute-start(bf16[5,32,800]{2,1,0:T(8,128)(2,1)S(1)} %dynamic-slice_convert_fusion.1), channel_id=1, source_target_pairs={{0,4},{1,5},{2,6},{3,7},{4,0},{5,1},{6,2},{7,3},{8,12},{9,13},{10,... | collective-permute-start | bytes 768008 | tf_op jit(solution)/shard_map/ppermute | solution.py:29
  225.0 9.7 %block_output.5 = (bf16[4,1600,512]{2,1,0:T(8,128)(2,1)}, f32[8,512]{1,0:T(8,128)}) custom-call(bf16[4,1600,512]{2,1,0:T(8,128)(2,1)} %bitcast.40, bf16[4,800,512]{2,1,0:T(8,128)(2,1)} %get-tuple-element.120.a2_ref, bf16[1600,800]{1,0:T(8,128)(2,1)} %transpose_out.1.wt_ref, bf16[224,800]{1,0:T(8,128)(2,1)} %prepare_in.1.v0, ...), custom_call_target="tpu_custom_call", output_to_operand_aliasing={{0}: (6, {})} | custom-call | flops 52756480000 | bytes 1 | tf_op jit(solution)/shard_map/block_output/pallas_call | solution.py:1099
  239.1 9.3 %grad_stream.4 = (bf16[4,1600,512]{2,1,0:T(8,128)(2,1)}, f32[8,1600]{1,0:T(8,128)}) custom-call(bf16[4,1600,512]{2,1,0:T(8,128)(2,1)} %bitcast.41, f32[4,8,512]{2,1,0:T(8,128)} %get-tuple-element.111.st_ref.before_ref, bf16[4,1600,512]{2,1,0:T(8,128)(2,1)} %bitcast.49, ...), custom_call_target="tpu_custom_call", output_to_operand_aliasing={{0}: (8, {})} | custom-call | flops 26869760000 | bytes 1 | tf_op jit(solution)/shard_map/grad_stream/pallas_call | solution.py:1044
  249.5 3.6 %collective-permute-done.18 = bf16[208,800]{1,0:T(8,128)(2,1)S(1)} collective-permute-done((bf16[208,800]{1,0:T(8,128)(2,1)S(1)}, bf16[208,800]{1,0:T(8,128)(2,1)S(1)}, u32[]{:S(2)}, u32[]{:S(2)}) %collective-permute-start.18) | collective-permute-done | bytes 332832 | tf_op jit(solution)/shard_map/ppermute | solution.py:29
  253.6 15.4 %grad_stream.5 = (bf16[4,1600,512]{2,1,0:T(8,128)(2,1)}, f32[8,1600]{1,0:T(8,128)}) custom-call(bf16[4,1600,512]{2,1,0:T(8,128)(2,1)} %bitcast.42, f32[4,8,512]{2,1,0:T(8,128)} %get-tuple-element.111.st_ref.before_ref, bf16[4,1600,512]{2,1,0:T(8,128)(2,1)} %bitcast.50, ...), custom_call_target="tpu_custom_call", output_to_operand_aliasing={{0}: (8, {})} | custom-call | flops 53739520000 | bytes 1 | tf_op jit(solution)/shard_map/grad_stream/pallas_call | solution.py:1044
  269.0 2.4 collective-permute-done.23
  272.9 2.7 collective-permute-done.21
  279.8 2.5 join_grads.1
  283.1 2.7 collective-permute-start.29
  288.1 3.6 %collective-permute-done.30 = f32[8,1600]{1,0:T(8,128)S(1)} collective-permute-done((f32[8,1600]{1,0:T(8,128)S(1)}, f32[8,1600]{1,0:T(8,128)S(1)}, u32[]{:S(2)}, u32[]{:S(2)}) %collective-permute-start.30) | collective-permute-done | bytes 51232 | tf_op jit(solution)/shard_map/ppermute | solution.py:29
  (132 shorter events, 48.4 us)
Async XLA Ops:
  2.6 9.1 %collective-permute-start = (bf16[224,800]{1,0:T(8,128)(2,1)}, bf16[224,800]{1,0:T(8,128)(2,1)S(1)}, u32[]{:S(2)}, u32[]{:S(2)}) collective-permute-start(bf16[224,800]{1,0:T(8,128)(2,1)} %prepare_in.1.v0), channel_id=1, source_target_pairs={{0,8},{1,17},{2,10},{3,19},{4,12},{5,21},{6,14},{7,23},{8,0},{9,25... | collective-permute-start | bytes 1075208 | tf_op jit(solution)/shard_map/ppermute | solution.py:25
  11.8 12.3 %collective-permute-start.1 = (bf16[2,224,800]{2,1,0:T(8,128)(2,1)S(1)}, bf16[2,224,800]{2,1,0:T(8,128)(2,1)}, u32[]{:S(2)}, u32[]{:S(2)}) collective-permute-start(bf16[2,224,800]{2,1,0:T(8,128)(2,1)S(1)} %pad_maximum_fusion.2), channel_id=1, source_target_pairs={{0,16},{1,9},{2,18},{3,11},{4,20},{5,13},{6,22},{7,15},{8,24},{9,1... | collective-permute-start | bytes 2150408 | tf_op jit(solution)/shard_map/ppermute | solution.py:25
  24.2 13.5 %collective-permute-start.4 = (bf16[5,104,800]{2,1,0:T(8,128)(2,1)S(1)}, bf16[5,104,800]{2,1,0:T(8,128)(2,1)S(1)}, u32[]{:S(2)}, u32[]{:S(2)}) collective-permute-start(bf16[5,104,800]{2,1,0:T(8,128)(2,1)S(1)} %copy-done.17), channel_id=1, source_target_pairs={{0,8},{1,17},{2,10},{3,19},{4,12},{5,21},{6,14},{7,23},{8,0},{9,25... | collective-permute-start | bytes 2496008 | tf_op jit(solution)/shard_map/ppermute | solution.py:25
  26.1 15.1 %collective-permute-start.3 = (bf16[2,224,800]{2,1,0:T(8,128)(2,1)}, bf16[2,224,800]{2,1,0:T(8,128)(2,1)}, u32[]{:S(2)}, u32[]{:S(2)}) collective-permute-start(bf16[2,224,800]{2,1,0:T(8,128)(2,1)} %collective-permute-done.1.v2.p2), channel_id=1, source_target_pairs={{0,1},{1,0},{2,3},{3,2},{4,5},{5,4},{6,7},{7,6},{8,9},{9,8},{10,11... | collective-permute-start | bytes 2150408 | tf_op jit(solution)/shard_map/ppermute | solution.py:29
  26.1 15.1 %collective-permute-start.2 = (bf16[224,800]{1,0:T(8,128)(2,1)S(1)}, bf16[224,800]{1,0:T(8,128)(2,1)S(1)}, u32[]{:S(2)}, u32[]{:S(2)}) collective-permute-start(bf16[224,800]{1,0:T(8,128)(2,1)S(1)} %collective-permute-done.v1.p1), channel_id=1, source_target_pairs={{0,1},{1,0},{2,3},{3,2},{4,5},{5,4},{6,7},{7,6},{8,9},{9,8},{10,11... | collective-permute-start | bytes 1075208 | tf_op jit(solution)/shard_map/ppermute | solution.py:29
  39.2 29.2 %copy-start.2 = (bf16[200,1600]{1,0:T(8,128)(2,1)S(1)}, bf16[200,1600]{1,0:T(8,128)(2,1)}, u32[]{:S(2)}) copy-start(bf16[200,1600]{1,0:T(8,128)(2,1)} %wo_own.1) | copy-start | bytes 1920004
  39.2 23.8 %collective-permute-start.6 = (bf16[2,5,104,800]{3,2,1,0:T(8,128)(2,1)}, bf16[2,5,104,800]{3,2,1,0:T(8,128)(2,1)}, u32[]{:S(2)}, u32[]{:S(2)}) collective-permute-start(bf16[2,5,104,800]{3,2,1,0:T(8,128)(2,1)} %pad_maximum_fusion), channel_id=1, source_target_pairs={{0,16},{1,9},{2,18},{3,11},{4,20},{5,13},{6,22},{7,15},{8,24},{9,1... | collective-permute-start | bytes 4992008 | tf_op jit(solution)/shard_map/ppermute | solution.py:25
  63.1 5.4 %collective-permute-start.8 = (bf16[2,5,104,800]{3,2,1,0:T(8,128)(2,1)}, bf16[2,5,104,800]{3,2,1,0:T(8,128)(2,1)S(1)}, u32[]{:S(2)}, u32[]{:S(2)}) collective-permute-start(bf16[2,5,104,800]{3,2,1,0:T(8,128)(2,1)} %collective-permute-done.6.g), channel_id=1, source_target_pairs={{0,1},{1,0},{2,3},{3,2},{4,5},{5,4},{6,7},{7,6},{8,9},{9,8},{10,11... | collective-permute-start | bytes 4992008 | tf_op jit(solution)/shard_map/ppermute | solution.py:29
  63.1 4.9 %collective-permute-start.7 = (bf16[5,104,800]{2,1,0:T(8,128)(2,1)S(1)}, bf16[5,104,800]{2,1,0:T(8,128)(2,1)S(1)}, u32[]{:S(2)}, u32[]{:S(2)}) collective-permute-start(bf16[5,104,800]{2,1,0:T(8,128)(2,1)S(1)} %collective-permute-done.4.f), channel_id=1, source_target_pairs={{0,1},{1,0},{2,3},{3,2},{4,5},{5,4},{6,7},{7,6},{8,9},{9,8},{10,11... | collective-permute-start | bytes 2496008 | tf_op jit(solution)/shard_map/ppermute | solution.py:29
  63.6 16.3 %collective-permute-start.5 = (bf16[4,8,800]{2,1,0:T(8,128)(2,1)}, bf16[4,8,800]{2,1,0:T(8,128)(2,1)S(1)}, u32[]{:S(2)}, u32[]{:S(2)}) collective-permute-start(bf16[4,8,800]{2,1,0:T(8,128)(2,1)} %get-tuple-element.115), channel_id=1, source_target_pairs={{0,1},{1,2},{2,3},{3,4},{4,5},{5,6},{6,7},{8,9},{9,10},{10,11},{11... | collective-permute-start | bytes 153608 | tf_op jit(solution)/shard_map/ppermute | solution.py:34
  135.8 12.8 %collective-permute-start.9 = (bf16[4,5,104,800]{3,2,1,0:T(8,128)(2,1)}, bf16[4,5,104,800]{3,2,1,0:T(8,128)(2,1)}, u32[]{:S(2)}, u32[]{:S(2)}) collective-permute-start(bf16[4,5,104,800]{3,2,1,0:T(8,128)(2,1)} %get-tuple-element.123), channel_id=1, source_target_pairs={{0,1},{1,0},{2,3},{3,2},{4,5},{5,4},{6,7},{7,6},{8,9},{9,8},{10,11... | collective-permute-start | bytes 9984008 | tf_op jit(solution)/shard_map/ppermute | solution.py:29
  136.0 17.7 %collective-permute-start.11 = (bf16[4,8,800]{2,1,0:T(8,128)(2,1)}, bf16[4,8,800]{2,1,0:T(8,128)(2,1)S(1)}, u32[]{:S(2)}, u32[]{:S(2)}) collective-permute-start(bf16[4,8,800]{2,1,0:T(8,128)(2,1)} %get-tuple-element.121), channel_id=1, source_target_pairs={{1,0},{2,1},{3,2},{4,3},{5,4},{6,5},{7,6},{9,8},{10,9},{11,10},{12... | collective-permute-start | bytes 153608 | tf_op jit(solution)/shard_map/ppermute | solution.py:34
  151.8 27.4 %collective-permute-start.10 = (bf16[2,5,104,800]{3,2,1,0:T(8,128)(2,1)}, bf16[2,5,104,800]{3,2,1,0:T(8,128)(2,1)}, u32[]{:S(2)}, u32[]{:S(2)}) collective-permute-start(bf16[2,5,104,800]{3,2,1,0:T(8,128)(2,1)} %add_convert_fusion), channel_id=1, source_target_pairs={{0,8},{1,17},{2,10},{3,19},{4,12},{5,21},{6,14},{7,23},{8,0},{9,25... | collective-permute-start | bytes 4992008 | tf_op jit(solution)/shard_map/ppermute | solution.py:25
  181.3 13.6 %collective-permute-start.12 = (bf16[5,104,800]{2,1,0:T(8,128)(2,1)S(1)}, bf16[5,104,800]{2,1,0:T(8,128)(2,1)S(1)}, u32[]{:S(2)}, u32[]{:S(2)}) collective-permute-start(bf16[5,104,800]{2,1,0:T(8,128)(2,1)S(1)} %fusion), channel_id=1, source_target_pairs={{0,16},{1,9},{2,18},{3,11},{4,20},{5,13},{6,22},{7,15},{8,24},{9,1... | collective-permute-start | bytes 2496008 | tf_op jit(solution)/shard_map/ppermute | solution.py:25
  194.2 13.2 %collective-permute-start.13 = (bf16[4,208,800]{2,1,0:T(8,128)(2,1)}, bf16[4,208,800]{2,1,0:T(8,128)(2,1)}, u32[]{:S(2)}, u32[]{:S(2)}) collective-permute-start(bf16[4,208,800]{2,1,0:T(8,128)(2,1)} %get-tuple-element.138), channel_id=1, source_target_pairs={{0,1},{1,0},{2,3},{3,2},{4,5},{5,4},{6,7},{7,6},{8,9},{9,8},{10,11... | collective-permute-start | bytes 3993608 | tf_op jit(solution)/shard_map/ppermute | solution.py:29
  197.9 21.0 %collective-permute-start.15 = (bf16[5,56,800]{2,1,0:T(8,128)(2,1)}, bf16[5,56,800]{2,1,0:T(8,128)(2,1)S(1)}, u32[]{:S(2)}, u32[]{:S(2)}) collective-permute-start(bf16[5,56,800]{2,1,0:T(8,128)(2,1)} %dynamic-slice_convert_fusion), channel_id=1, source_target_pairs={{0,2},{1,3},{2,0},{3,1},{4,6},{5,7},{6,4},{7,5},{8,10},{9,11},{10,... | collective-permute-start | bytes 1344008 | tf_op jit(solution)/shard_map/ppermute | solution.py:29
  209.5 12.7 %collective-permute-start.14 = (bf16[2,208,800]{2,1,0:T(8,128)(2,1)}, bf16[2,208,800]{2,1,0:T(8,128)(2,1)S(1)}, u32[]{:S(2)}, u32[]{:S(2)}) collective-permute-start(bf16[2,208,800]{2,1,0:T(8,128)(2,1)} %add_convert_fusion.2), channel_id=1, source_target_pairs={{0,8},{1,17},{2,10},{3,19},{4,12},{5,21},{6,14},{7,23},{8,0},{9,25... | collective-permute-start | bytes 1996808 | tf_op jit(solution)/shard_map/ppermute | solution.py:25
  219.1 15.6 %collective-permute-start.17 = (bf16[5,32,800]{2,1,0:T(8,128)(2,1)S(1)}, bf16[5,32,800]{2,1,0:T(8,128)(2,1)S(1)}, u32[]{:S(2)}, u32[]{:S(2)}) collective-permute-start(bf16[5,32,800]{2,1,0:T(8,128)(2,1)S(1)} %dynamic-slice_convert_fusion.1), channel_id=1, source_target_pairs={{0,4},{1,5},{2,6},{3,7},{4,0},{5,1},{6,2},{7,3},{8,12},{9,13},{10,... | collective-permute-start | bytes 768008 | tf_op jit(solution)/shard_map/ppermute | solution.py:29
  223.5 13.1 %collective-permute-start.16 = (bf16[208,800]{1,0:T(8,128)(2,1)S(1)}, bf16[208,800]{1,0:T(8,128)(2,1)S(1)}, u32[]{:S(2)}, u32[]{:S(2)}) collective-permute-start(bf16[208,800]{1,0:T(8,128)(2,1)S(1)} %fusion.4), channel_id=1, source_target_pairs={{0,16},{1,9},{2,18},{3,11},{4,20},{5,13},{6,22},{7,15},{8,24},{9,1... | collective-permute-start | bytes 998408 | tf_op jit(solution)/shard_map/ppermute | solution.py:25
  234.8 14.5 %collective-permute-start.19 = (bf16[5,32,800]{2,1,0:T(8,128)(2,1)S(1)}, bf16[5,32,800]{2,1,0:T(8,128)(2,1)S(1)}, u32[]{:S(2)}, u32[]{:S(2)}) collective-permute-start(bf16[5,32,800]{2,1,0:T(8,128)(2,1)S(1)} %add_convert_fusion.5), channel_id=1, source_target_pairs={{0,4},{1,5},{2,6},{3,7},{4,0},{5,1},{6,2},{7,3},{8,12},{9,13},{10,... | collective-permute-start | bytes 768008 | tf_op jit(solution)/shard_map/ppermute | solution.py:29
  237.9 15.3 %collective-permute-start.18 = (bf16[208,800]{1,0:T(8,128)(2,1)S(1)}, bf16[208,800]{1,0:T(8,128)(2,1)S(1)}, u32[]{:S(2)}, u32[]{:S(2)}) collective-permute-start(bf16[208,800]{1,0:T(8,128)(2,1)S(1)} %fusion.1), channel_id=1, source_target_pairs={{0,2},{1,3},{2,0},{3,1},{4,6},{5,7},{6,4},{7,5},{8,10},{9,11},{10,... | collective-permute-start | bytes 998408 | tf_op jit(solution)/shard_map/ppermute | solution.py:29
  249.4 21.9 %collective-permute-start.23 = (bf16[5,56,800]{2,1,0:T(8,128)(2,1)S(1)}, bf16[5,56,800]{2,1,0:T(8,128)(2,1)S(1)}, u32[]{:S(2)}, u32[]{:S(2)}) collective-permute-start(bf16[5,56,800]{2,1,0:T(8,128)(2,1)S(1)} %pad_maximum_fusion.3), channel_id=1, source_target_pairs={{0,2},{1,3},{2,0},{3,1},{4,6},{5,7},{6,4},{7,5},{8,10},{9,11},{10,... | collective-permute-start | bytes 1344008 | tf_op jit(solution)/shard_map/ppermute | solution.py:29
  253.3 18.7 %collective-permute-start.20 = (bf16[208,800]{1,0:T(8,128)(2,1)S(1)}, bf16[208,800]{1,0:T(8,128)(2,1)S(1)}, u32[]{:S(2)}, u32[]{:S(2)}) collective-permute-start(bf16[208,800]{1,0:T(8,128)(2,1)S(1)} %add_convert_fusion.3), channel_id=1, source_target_pairs={{0,4},{1,5},{2,6},{3,7},{4,0},{5,1},{6,2},{7,3},{8,12},{9,13},{10,... | collective-permute-start | bytes 998408 | tf_op jit(solution)/shard_map/ppermute | solution.py:29
  271.9 7.9 %collective-permute-start.24 = (bf16[5,104,800]{2,1,0:T(8,128)(2,1)S(1)}, bf16[5,104,800]{2,1,0:T(8,128)(2,1)S(1)}, u32[]{:S(2)}, u32[]{:S(2)}) collective-permute-start(bf16[5,104,800]{2,1,0:T(8,128)(2,1)S(1)} %pad_maximum_fusion.1.mine_ref), channel_id=1, source_target_pairs={{0,1},{1,0},{2,3},{3,2},{4,5},{5,4},{6,7},{7,6},{8,9},{9,8},{10,11... | collective-permute-start | bytes 2496008 | tf_op jit(solution)/shard_map/ppermute | solution.py:29
  272.0 7.8 %collective-permute-start.25 = (f32[208,800]{1,0:T(8,128)S(1)}, f32[208,800]{1,0:T(8,128)S(1)}, u32[]{:S(2)}, u32[]{:S(2)}) collective-permute-start(f32[208,800]{1,0:T(8,128)S(1)} %convert_add_fusion.1.mine_in), channel_id=1, source_target_pairs={{0,1},{1,0},{2,3},{3,2},{4,5},{5,4},{6,7},{7,6},{8,9},{9,8},{10,11... | collective-permute-start | bytes 1996808 | tf_op jit(solution)/shard_map/ppermute | solution.py:29
  272.8 2.8 collective-permute-start.21
  275.6 4.2 %collective-permute-start.22 = (f32[8,1600]{1,0:T(8,128)S(1)}, f32[8,1600]{1,0:T(8,128)S(1)}, u32[]{:S(2)}, u32[]{:S(2)}) collective-permute-start(f32[8,1600]{1,0:T(8,128)S(1)} %add.132), channel_id=1, source_target_pairs={{0,8},{8,0},{16,24},{24,16},{1,9},{9,1},{17,25},{25,17},{2,10},{10... | collective-permute-start | bytes 153608 | tf_op jit(solution)/shard_map/ppermute | solution.py:29
  276.4 5.9 %collective-permute-start.26 = (f32[8,1600]{1,0:T(8,128)S(1)}, f32[8,1600]{1,0:T(8,128)S(1)}, u32[]{:S(2)}, u32[]{:S(2)}) collective-permute-start(f32[8,1600]{1,0:T(8,128)S(1)} %add.132), channel_id=1, source_target_pairs={{0,16},{8,24},{16,0},{24,8},{1,17},{9,25},{17,1},{25,9},{2,18},{10... | collective-permute-start | bytes 153608 | tf_op jit(solution)/shard_map/ppermute | solution.py:29
  277.9 5.0 %collective-permute-start.27 = (f32[8,1600]{1,0:T(8,128)S(1)}, f32[8,1600]{1,0:T(8,128)S(1)}, u32[]{:S(2)}, u32[]{:S(2)}) collective-permute-start(f32[8,1600]{1,0:T(8,128)S(1)} %add.132), channel_id=1, source_target_pairs={{0,24},{8,16},{16,8},{24,0},{1,25},{9,17},{17,9},{25,1},{2,26},{10... | collective-permute-start | bytes 153608 | tf_op jit(solution)/shard_map/ppermute | solution.py:29
  283.0 4.5 %collective-permute-start.28 = (f32[8,1600]{1,0:T(8,128)S(1)}, f32[8,1600]{1,0:T(8,128)S(1)}, u32[]{:S(2)}, u32[]{:S(2)}) collective-permute-start(f32[8,1600]{1,0:T(8,128)S(1)} %add_add_fusion.1), channel_id=1, source_target_pairs={{0,2},{1,3},{2,0},{3,1},{4,6},{5,7},{6,4},{7,5},{8,10},{9,11},{10,... | collective-permute-start | bytes 153608 | tf_op jit(solution)/shard_map/ppermute | solution.py:29
  283.1 5.0 %collective-permute-start.29 = (f32[8,1600]{1,0:T(8,128)S(1)}, f32[8,1600]{1,0:T(8,128)S(1)}, u32[]{:S(2)}, u32[]{:S(2)}) collective-permute-start(f32[8,1600]{1,0:T(8,128)S(1)} %add_add_fusion.1), channel_id=1, source_target_pairs={{0,4},{1,5},{2,6},{3,7},{4,0},{5,1},{6,2},{7,3},{8,12},{9,13},{10,... | collective-permute-start | bytes 153608 | tf_op jit(solution)/shard_map/ppermute | solution.py:29
  285.8 5.9 %collective-permute-start.30 = (f32[8,1600]{1,0:T(8,128)S(1)}, f32[8,1600]{1,0:T(8,128)S(1)}, u32[]{:S(2)}, u32[]{:S(2)}) collective-permute-start(f32[8,1600]{1,0:T(8,128)S(1)} %add_add_fusion.1), channel_id=1, source_target_pairs={{0,6},{1,7},{2,4},{3,5},{4,2},{5,3},{6,0},{7,1},{8,14},{9,15},{10,... | collective-permute-start | bytes 153608 | tf_op jit(solution)/shard_map/ppermute | solution.py:29
  (25 other events, 108.2 us)
